TPU v7x, 128 devices: a whole 4x4x4 slice. The times are simulated.
128 devices in a mesh: req: 8 (over z, core), mlp: 16 (over x, y).
Axes of the slice: x: 4, y: 4, z: 4, core: 2. Of those that a mesh axis runs over, the one named last changes fastest.
Arguments:
- inputs: bfloat16 [2, 768, 4096], P(None, 'mlp', 'req'), may hold values from -6 to 6
- norm_gains: float32 [3, 4096], P(None, 'req'), may hold values from 0.25 to 1.75
- attn_weight: bfloat16 [4096, 12288], P('req', 'mlp'), may hold values from -0.09375 to 0.09375
- up_weight: bfloat16 [4096, 16384], P('req', 'mlp'), may hold values from -0.09375 to 0.09375
- dense_weight: bfloat16 [4096, 4096], P('mlp', 'req'), may hold values from -0.09375 to 0.09375
- down_weight: bfloat16 [16384, 4096], P('mlp', 'req'), may hold values from -0.046875 to 0.046875
- next_weight: bfloat16 [4096, 12288], P('req', 'mlp'), may hold values from -0.09375 to 0.09375
- cache_keys: bfloat16 [512, 128, 4096], P('req', None, 'mlp'), may hold values from -360 to 360
- cache_values: bfloat16 [512, 128, 4096], P('req', None, 'mlp'), may hold values from -6 to 6
- lengths: int32 [96], replicated, may hold values from 1 to 4096, as said below
- slot_table: int32 [2, 512], P(None, 'req'), may hold values from -1 to 95, as said below
- parents: int32 [1, 768], P(None, 'req'), may hold values from 0 to 7
Outputs:
- layer_out: bfloat16 [2, 768, 4096], P(None, 'mlp', 'req')
- next_qkv: bfloat16 [2, 768, 12288], P(None, 'req', 'mlp')
Inputs may be any that keep to these rules, and one draw needn't show every extreme that they name: `lengths`: each request has between 1 and 32 pages of 128 tokens; the longest request has exactly 32 full pages. `slot_table`: every page of every request is held by exactly one slot; an empty slot has request -1 and page 0. All requests together hold 440 pages, and in every draw the slots of some index of req are all in use.
All inputs are finite; a program needn't handle non-finite values.
Results may differ from a plain program's by a relative error of at most 0.04.
Values may be sent and summed in bfloat16 or wider, within the bound.
A program may use at most 128 MiB of HBM per device.

v0:
```python
import math

import jax
import jax.numpy as jnp
from jax import lax
from jax.sharding import PartitionSpec as P

HD = 128
ROT = 32
PAGE = 128
BEAM = 8
STEPS = 2


NEG_FILL = -1e30
EPSILON = 1e-05


def combined_all(value, axis, combine):
    everything = jax.tree.map(
        lambda part, kind: lax.all_gather(part.astype(kind), axis),
        value,
        (jnp.bfloat16, jnp.bfloat16, jnp.bfloat16),
    )

    def take(k):
        return jax.tree.map(lambda part, own: part[k].astype(own.dtype), everything, value)

    return lax.fori_loop(
        1, lax.axis_size(axis), lambda k, so_far: combine(so_far, take(k)), take(0)
    )


def rotate(vectors, positions):
    half = ROT // 2
    freq = jnp.exp(jnp.arange(half, dtype=jnp.float32) * (-2.0 * math.log(10000.0) / ROT))
    angles = positions.astype(jnp.float32)[:, None] * freq[None, :]
    cosine = jnp.concatenate([jnp.cos(angles), jnp.cos(angles)], axis=1)[:, None, :]
    sine = jnp.concatenate([jnp.sin(angles), jnp.sin(angles)], axis=1)[:, None, :]
    turned = vectors[..., :ROT]
    swapped = jnp.concatenate([-turned[..., half:], turned[..., :half]], axis=-1)
    return jnp.concatenate([turned * cosine + swapped * sine, vectors[..., ROT:]], axis=-1)


def row_normalize(block):
    values = block.astype(jnp.float32)
    whole = lax.all_gather(block, "req", axis=1, tiled=True).astype(jnp.float32)
    row_mean = jnp.mean(whole, axis=1, keepdims=True)
    centred_whole = whole - row_mean
    row_var = jnp.mean(centred_whole * centred_whole, axis=1, keepdims=True)
    return (values - row_mean) * lax.rsqrt(row_var + EPSILON)


def merge_partials(first, second):
    top = jnp.maximum(first[0], second[0])
    left = jnp.exp(first[0] - top)
    right = jnp.exp(second[0] - top)
    return (
        top,
        first[1] * left + second[1] * right,
        first[2] * left[..., None] + second[2] * right[..., None],
    )


def shards(
    inputs,
    norm_gains,
    attn_weight,
    up_weight,
    dense_weight,
    down_weight,
    next_weight,
    cache_keys,
    cache_values,
    lengths,
    slot_table,
    parents,
):
    scale = 1.0 / math.sqrt(HD)
    highest = lax.Precision.HIGHEST
    own_count = parents.shape[1]
    request_count = lengths.shape[0]
    beam_total = request_count * BEAM
    head_count = dense_weight.shape[0] // HD
    triple_width = attn_weight.shape[1]
    slot_count = slot_table.shape[1]
    offset = lax.axis_index("req") * own_count
    beam_group = jnp.arange(beam_total, dtype=jnp.int32) // BEAM
    all_positions = lengths[beam_group]
    own_positions = lax.dynamic_slice_in_dim(all_positions, offset, own_count, 0)
    own_group = jnp.arange(own_count, dtype=jnp.int32) // BEAM
    slot_owner = slot_table[0]
    slot_pageno = slot_table[1]
    valid_owner = jnp.maximum(slot_owner, 0)
    token_pos = slot_pageno[:, None] * PAGE + jnp.arange(PAGE, dtype=jnp.int32)[None, :]
    live = (slot_owner[:, None] >= 0) & (token_pos < lengths[valid_owner][:, None])
    live_wide = live[:, None, None, :]
    owner_mask = slot_owner[:, None] == jnp.arange(request_count, dtype=jnp.int32)[None, :]
    owner_float = owner_mask.astype(jnp.float32)
    gather_rows = valid_owner[:, None] * BEAM + jnp.arange(BEAM, dtype=jnp.int32)[None, :]
    page_keys = cache_keys.reshape(slot_count, PAGE, head_count, HD)
    page_values = cache_values.reshape(slot_count, PAGE, head_count, HD)
    tail_keys = []
    tail_values = []
    layer_list = []
    next_list = []
    for step_index in range(STEPS):
        if step_index > 0:
            source = own_group * BEAM + parents[step_index - 1]
            tail_keys = [entry[source] for entry in tail_keys]
            tail_values = [entry[source] for entry in tail_values]
        block = inputs[step_index]
        normed = row_normalize(block)
        attn_in = (normed * norm_gains[0]).astype(jnp.bfloat16)
        mlp_in = (normed * norm_gains[1]).astype(jnp.bfloat16)
        joined = jnp.concatenate([attn_in, mlp_in], axis=1)
        split_at = attn_in.shape[1]
        piece = lax.all_gather(joined, "mlp", axis=0, tiled=True)
        first = jnp.dot(piece[:, :split_at], attn_weight, preferred_element_type=jnp.float32)
        second = jnp.dot(piece[:, split_at:], up_weight, preferred_element_type=jnp.float32)
        partial_sums = jnp.concatenate([first, second], axis=1)
        step_positions = own_positions + step_index
        summed_all = lax.psum(partial_sums.astype(jnp.bfloat16), "req").astype(jnp.float32)
        mixed_all = summed_all[:, :triple_width].reshape(beam_total, head_count, 3, HD)
        queries_all = rotate(mixed_all[:, :, 0], all_positions + step_index).astype(jnp.bfloat16)
        mixed_own = lax.dynamic_slice_in_dim(mixed_all, offset, own_count, 0)
        queries_own = lax.dynamic_slice_in_dim(queries_all, offset, own_count, 0)
        activated_all = jax.nn.gelu(summed_all[:, triple_width:], approximate=False).astype(
            jnp.bfloat16
        )
        keys_new = rotate(mixed_own[:, :, 1], step_positions).astype(jnp.bfloat16)
        values_new = mixed_own[:, :, 2].astype(jnp.bfloat16)
        chosen = queries_all[gather_rows]
        scores = (
            jnp.einsum("sbhd,sthd->sbht", chosen, page_keys, preferred_element_type=jnp.float32)
            * scale
        )
        masked = jnp.where(live_wide, scores, NEG_FILL)
        slot_top = jnp.max(masked, axis=3)
        weights = jnp.where(live_wide, jnp.exp(masked - slot_top[..., None]), 0.0)
        slot_total = jnp.sum(weights, axis=3)
        slot_out = jnp.einsum(
            "sbht,sthd->sbhd",
            weights.astype(jnp.bfloat16),
            page_values,
            preferred_element_type=jnp.float32,
        )
        request_top = jnp.max(
            jnp.where(owner_mask[:, :, None, None], slot_top[:, None], NEG_FILL), axis=0
        )
        factor = jnp.exp(slot_top - request_top[valid_owner])
        page_total = jnp.einsum(
            "sr,sbh->rbh", owner_float, slot_total * factor, precision=highest
        ).reshape(beam_total, head_count)
        page_out = jnp.einsum(
            "sr,sbhd->rbhd", owner_float, slot_out * factor[..., None], precision=highest
        ).reshape(beam_total, head_count, HD)
        page_top = request_top.reshape(beam_total, head_count)
        merged = combined_all((page_top, page_total, page_out), "req", merge_partials)
        own_top = lax.dynamic_slice_in_dim(merged[0], offset, own_count, 0)
        own_total = lax.dynamic_slice_in_dim(merged[1], offset, own_count, 0)
        own_out = lax.dynamic_slice_in_dim(merged[2], offset, own_count, 0)
        history_keys = jnp.stack(tail_keys + [keys_new], axis=0)
        history_values = jnp.stack(tail_values + [values_new], axis=0)
        own_scores = (
            jnp.einsum(
                "bhd,nbhd->bhn", queries_own, history_keys, preferred_element_type=jnp.float32
            )
            * scale
        )
        top = jnp.maximum(own_top, jnp.max(own_scores, axis=2))
        page_factor = jnp.exp(own_top - top)
        own_weights = jnp.exp(own_scores - top[..., None])
        total = own_total * page_factor + jnp.sum(own_weights, axis=2)
        summed = own_out * page_factor[..., None] + jnp.einsum(
            "bhn,nbhd->bhd",
            own_weights.astype(jnp.bfloat16),
            history_values,
            preferred_element_type=jnp.float32,
        )
        attended = (
            (summed / total[..., None]).astype(jnp.bfloat16).reshape(own_count, head_count * HD)
        )
        attended_all = lax.all_gather(attended, "req", axis=0, tiled=True)
        update = lax.psum_scatter(
            (
                jnp.dot(attended_all, dense_weight, preferred_element_type=jnp.float32)
                + jnp.dot(activated_all, down_weight, preferred_element_type=jnp.float32)
            ).astype(jnp.bfloat16),
            "mlp",
            scatter_dimension=0,
            tiled=True,
        ).astype(jnp.float32)
        layer = (block.astype(jnp.float32) + update).astype(jnp.bfloat16)
        next_in = (row_normalize(layer) * norm_gains[2]).astype(jnp.bfloat16)
        next_partial = jnp.dot(
            lax.all_gather(next_in, "mlp", axis=0, tiled=True),
            next_weight,
            preferred_element_type=jnp.float32,
        )
        next_out = lax.psum_scatter(
            next_partial.astype(jnp.bfloat16), "req", scatter_dimension=0, tiled=True
        )
        tail_keys = tail_keys + [keys_new]
        tail_values = tail_values + [values_new]
        layer_list.append(layer)
        next_list.append(next_out)
    return (jnp.stack(layer_list), jnp.stack(next_list))


def solution(mesh):
    in_specs = (
        P(None, "mlp", "req"),
        P(None, "req"),
        P("req", "mlp"),
        P("req", "mlp"),
        P("mlp", "req"),
        P("mlp", "req"),
        P("req", "mlp"),
        P("req", None, "mlp"),
        P("req", None, "mlp"),
        P(),
        P(None, "req"),
        P(None, "req"),
    )
    out_specs = (P(None, "mlp", "req"), P(None, "req", "mlp"))
    return jax.shard_map(shards, mesh=mesh, in_specs=in_specs, out_specs=out_specs, check_vma=False)
```

profile of v0, /device:TPU:0, one launch (start us, length us, event | category | flops | bytes accessed | tf_op | source)
XLA Modules:
  0.0 711.8 jit_solution(18122759081205407512)
XLA Ops:
  9.5 14.2 %all-gather = bf16[1,48,4096]{2,1,0:T(8,128)(2,1)S(1)} all-gather(bf16[1,48,512]{2,1,0:T(8,128)(2,1)S(1)} %get-tuple-element.516), channel_id=2, replica_groups=mesh['req'=8,'mlp'=16] {'req'}, dimensions={2}, use_global_device_ids=true | all-gather | bytes 442368 | tf_op jit(solution)/shard_map/all_gather | solution.py:47
  24.2 13.0 %all-gather.1 = bf16[1,48,4096]{2,1,0:T(8,128)(2,1)S(1)} all-gather(bf16[1,48,512]{2,1,0:T(8,128)(2,1)S(1)} %get-tuple-element.517), channel_id=3, replica_groups=mesh['req'=8,'mlp'=16] {'req'}, dimensions={2}, use_global_device_ids=true | all-gather | bytes 442368 | tf_op jit(solution)/shard_map/all_gather | solution.py:47
  40.1 44.4 %all-gather.7.cloned.1.call-done = bf16[768,1024]{1,0:T(8,128)(2,1)} async-done(((bf16[48,1024]{1,0:T(8,128)(2,1)}), bf16[768,1024]{1,0:T(8,128)(2,1)}) %all-gather.7.cloned.1.call-update) | async-done | bytes 1572880 | tf_op jit(solution)/shard_map/all_gather | solution.py:118
  87.1 43.4 %all-gather.11.cloned.1.call-done = bf16[768,1024]{1,0:T(8,128)(2,1)} async-done(((bf16[48,1024]{1,0:T(8,128)(2,1)}), bf16[768,1024]{1,0:T(8,128)(2,1)}) %all-gather.11.cloned.1.call-update) | async-done | bytes 1572880 | tf_op jit(solution)/shard_map/all_gather | solution.py:118
  146.4 70.9 %all-reduce.3.cloned.1.call-done = (bf16[768,1792]{1,0:T(8,128)(2,1)}, bf16[768,1792]{1,0:T(8,128)(2,1)}) async-done(((bf16[768,1792]{1,0:T(8,128)(2,1)}, bf16[768,1792]{1,0:T(8,128)(2,1)}), (bf16[768,1792]{1,0:T(8,128)(2,1)}, bf16[768,1792]{1,0:T(8,128)(2,1)})) %all-reduce.3.cloned.1.call-update) | async-done | bytes 5505040 | tf_op jit(solution)/shard_map/psum | solution.py:123
  248.9 11.7 %all-gather.9.cloned.1.call-start = ((), (), s32[]{:S(2)}) async-start(), calls=%async_computation.5 | async-start | bytes 3538944 | tf_op jit(solution)/shard_map/all_gather | solution.py:21
  271.8 12.7 %all_gather.62 = bf16[8,768,2]{1,2,0:T(2,128)(2,1)S(1)} all-gather(bf16[1,768,2]{1,2,0:T(2,128)(2,1)S(1)} %convert_element_type.378), channel_id=1, replica_groups=mesh['req'=8,'mlp'=16] {'req'}, dimensions={0}, use_global_device_ids=true | all-gather | bytes 27648 | tf_op jit(solution)/shard_map/all_gather | solution.py:21
  284.5 12.7 %all_gather.56 = bf16[8,768,2]{1,2,0:T(2,128)(2,1)S(1)} all-gather(bf16[1,768,2]{1,2,0:T(2,128)(2,1)S(1)} %convert_element_type.351), channel_id=1, replica_groups=mesh['req'=8,'mlp'=16] {'req'}, dimensions={0}, use_global_device_ids=true | all-gather | bytes 27648 | tf_op jit(solution)/shard_map/all_gather | solution.py:21
  297.2 12.7 %all_gather.57 = bf16[8,768,2]{1,2,0:T(2,128)(2,1)S(1)} all-gather(bf16[1,768,2]{1,2,0:T(2,128)(2,1)S(1)} %convert_element_type.355), channel_id=1, replica_groups=mesh['req'=8,'mlp'=16] {'req'}, dimensions={0}, use_global_device_ids=true | all-gather | bytes 27648 | tf_op jit(solution)/shard_map/all_gather | solution.py:21
  309.9 12.7 %all_gather.63 = bf16[8,768,2]{1,2,0:T(2,128)(2,1)S(1)} all-gather(bf16[1,768,2]{1,2,0:T(2,128)(2,1)S(1)} %convert_element_type.382), channel_id=1, replica_groups=mesh['req'=8,'mlp'=16] {'req'}, dimensions={0}, use_global_device_ids=true | all-gather | bytes 27648 | tf_op jit(solution)/shard_map/all_gather | solution.py:21
  327.4 8.0 %fusion.40 = f32[768,512]{1,0:T(8,128)} fusion(bf16[1024,512]{1,0:T(8,128)(2,1)S(1)} %copy-done.21, f32[768,1792]{1,0:T(8,128)S(1)} %convert_element_type.348), kind=kOutput, calls=%fused_computation.85 | convolution fusion | flops 856424448 | bytes 5767168 | tf_op jit(solution)/shard_map/dot_general | solution.py:188
  335.4 8.0 %fusion.38 = f32[768,512]{1,0:T(8,128)} fusion(bf16[1024,512]{1,0:T(8,128)(2,1)S(1)} %copy-done.21, f32[768,1792]{1,0:T(8,128)S(1)} %convert_element_type.375), kind=kOutput, calls=%fused_computation.84 | convolution fusion | flops 856424448 | bytes 5767168 | tf_op jit(solution)/shard_map/dot_general | solution.py:188
  352.1 60.4 %while.38 = (s32[]{:T(128)}, f32[768,2]{0,1:T(2,128)S(1)}, f32[768,2]{0,1:T(2,128)S(1)}, f32[768,2,128]{2,1,0:T(2,128)S(1)}, bf16[8,768,2]{1,2,0:T(2,128)(2,1)S(...) while((s32[]{:T(128)}, f32[768,2]{0,1:T(2,128)S(1)}, ...), condition=%wide.region_7.8_spmd, body=%wide.region_6.7_spmd.sunk | while | flops 798725 | bytes 2832527 | solution.py:29
  353.6 7.1 %fusion.262 = f32[768,2,128]{2,1,0:T(2,128)S(1)} fusion(f32[768,2,128]{2,1,0:T(2,128)S(1)} %get-tuple-element.678, bf16[1,768,2,128]{3,1,2,0:T(8,128)(2,1)S(1)} %constant_dynamic-slice_fusion.10, f32[768,2]{1,0:T(8,128)S(1)} %copy.475, f32[768,2]{1,0:T(8,128)S(1)} %copy.476), kind=kLoop, calls=%fused_computation.9.clone.1 | loop fusion | flops 786432 | bytes 1978368 | tf_op jit(solution)/shard_map/while/body/eval_jaxpr/add | solution.py:61
  362.2 7.1 %fusion.262 = f32[768,2,128]{2,1,0:T(2,128)S(1)} fusion(f32[768,2,128]{2,1,0:T(2,128)S(1)} %get-tuple-element.678, bf16[1,768,2,128]{3,1,2,0:T(8,128)(2,1)S(1)} %constant_dynamic-slice_fusion.10, f32[768,2]{1,0:T(8,128)S(1)} %copy.475, f32[768,2]{1,0:T(8,128)S(1)} %copy.476), kind=kLoop, calls=%fused_computation.9.clone.1 | loop fusion | flops 786432 | bytes 1978368 | tf_op jit(solution)/shard_map/while/body/eval_jaxpr/add | solution.py:61
  370.8 7.1 %fusion.262 = f32[768,2,128]{2,1,0:T(2,128)S(1)} fusion(f32[768,2,128]{2,1,0:T(2,128)S(1)} %get-tuple-element.678, bf16[1,768,2,128]{3,1,2,0:T(8,128)(2,1)S(1)} %constant_dynamic-slice_fusion.10, f32[768,2]{1,0:T(8,128)S(1)} %copy.475, f32[768,2]{1,0:T(8,128)S(1)} %copy.476), kind=kLoop, calls=%fused_computation.9.clone.1 | loop fusion | flops 786432 | bytes 1978368 | tf_op jit(solution)/shard_map/while/body/eval_jaxpr/add | solution.py:61
  379.4 7.1 %fusion.262 = f32[768,2,128]{2,1,0:T(2,128)S(1)} fusion(f32[768,2,128]{2,1,0:T(2,128)S(1)} %get-tuple-element.678, bf16[1,768,2,128]{3,1,2,0:T(8,128)(2,1)S(1)} %constant_dynamic-slice_fusion.10, f32[768,2]{1,0:T(8,128)S(1)} %copy.475, f32[768,2]{1,0:T(8,128)S(1)} %copy.476), kind=kLoop, calls=%fused_computation.9.clone.1 | loop fusion | flops 786432 | bytes 1978368 | tf_op jit(solution)/shard_map/while/body/eval_jaxpr/add | solution.py:61
  388.0 7.1 %fusion.262 = f32[768,2,128]{2,1,0:T(2,128)S(1)} fusion(f32[768,2,128]{2,1,0:T(2,128)S(1)} %get-tuple-element.678, bf16[1,768,2,128]{3,1,2,0:T(8,128)(2,1)S(1)} %constant_dynamic-slice_fusion.10, f32[768,2]{1,0:T(8,128)S(1)} %copy.475, f32[768,2]{1,0:T(8,128)S(1)} %copy.476), kind=kLoop, calls=%fused_computation.9.clone.1 | loop fusion | flops 786432 | bytes 1978368 | tf_op jit(solution)/shard_map/while/body/eval_jaxpr/add | solution.py:61
  405.3 7.1 %fusion.262 = f32[768,2,128]{2,1,0:T(2,128)S(1)} fusion(f32[768,2,128]{2,1,0:T(2,128)S(1)} %get-tuple-element.678, bf16[1,768,2,128]{3,1,2,0:T(8,128)(2,1)S(1)} %constant_dynamic-slice_fusion.10, f32[768,2]{1,0:T(8,128)S(1)} %copy.475, f32[768,2]{1,0:T(8,128)S(1)} %copy.476), kind=kLoop, calls=%fused_computation.9.clone.1 | loop fusion | flops 786432 | bytes 1978368 | tf_op jit(solution)/shard_map/while/body/eval_jaxpr/add | solution.py:61
  415.6 13.0 %all_gather.59 = bf16[768,256]{1,0:T(8,128)(2,1)S(1)} all-gather(bf16[96,256]{1,0:T(8,128)(2,1)S(1)} %copy.319), channel_id=1, replica_groups=mesh['req'=8,'mlp'=16] {'req'}, dimensions={0}, use_global_device_ids=true | all-gather | bytes 442368 | tf_op jit(solution)/shard_map/all_gather | solution.py:184
  429.9 65.2 %while.39 = (s32[]{:T(128)}, f32[768,2]{0,1:T(2,128)S(1)}, f32[768,2]{0,1:T(2,128)S(1)}, f32[768,2,128]{2,1,0:T(2,128)S(1)}, bf16[8,768,2]{1,2,0:T(2,128)(2,1)},...) while((s32[]{:T(128)}, f32[768,2]{0,1:T(2,128)S(1)}, ...), condition=%wide.region_16.17_spmd, body=%wide.region_15.16_spmd.sunk | while | flops 798725 | bytes 2832527 | solution.py:29
  432.1 7.1 %fusion.264 = f32[768,2,128]{2,1,0:T(2,128)S(1)} fusion(f32[768,2,128]{2,1,0:T(2,128)S(1)} %get-tuple-element.708, bf16[1,768,2,128]{3,1,2,0:T(8,128)(2,1)S(1)} %constant_dynamic-slice_fusion.11, f32[768,2]{1,0:T(8,128)S(1)} %copy.478, f32[768,2]{1,0:T(8,128)S(1)} %copy.479), kind=kLoop, calls=%fused_computation.19.clone.1 | loop fusion | flops 786432 | bytes 1978368 | tf_op jit(solution)/shard_map/while/body/eval_jaxpr/add | solution.py:61
  441.4 7.1 %fusion.264 = f32[768,2,128]{2,1,0:T(2,128)S(1)} fusion(f32[768,2,128]{2,1,0:T(2,128)S(1)} %get-tuple-element.708, bf16[1,768,2,128]{3,1,2,0:T(8,128)(2,1)S(1)} %constant_dynamic-slice_fusion.11, f32[768,2]{1,0:T(8,128)S(1)} %copy.478, f32[768,2]{1,0:T(8,128)S(1)} %copy.479), kind=kLoop, calls=%fused_computation.19.clone.1 | loop fusion | flops 786432 | bytes 1978368 | tf_op jit(solution)/shard_map/while/body/eval_jaxpr/add | solution.py:61
  450.7 7.1 %fusion.264 = f32[768,2,128]{2,1,0:T(2,128)S(1)} fusion(f32[768,2,128]{2,1,0:T(2,128)S(1)} %get-tuple-element.708, bf16[1,768,2,128]{3,1,2,0:T(8,128)(2,1)S(1)} %constant_dynamic-slice_fusion.11, f32[768,2]{1,0:T(8,128)S(1)} %copy.478, f32[768,2]{1,0:T(8,128)S(1)} %copy.479), kind=kLoop, calls=%fused_computation.19.clone.1 | loop fusion | flops 786432 | bytes 1978368 | tf_op jit(solution)/shard_map/while/body/eval_jaxpr/add | solution.py:61
  469.3 7.1 %fusion.264 = f32[768,2,128]{2,1,0:T(2,128)S(1)} fusion(f32[768,2,128]{2,1,0:T(2,128)S(1)} %get-tuple-element.708, bf16[1,768,2,128]{3,1,2,0:T(8,128)(2,1)S(1)} %constant_dynamic-slice_fusion.11, f32[768,2]{1,0:T(8,128)S(1)} %copy.478, f32[768,2]{1,0:T(8,128)S(1)} %copy.479), kind=kLoop, calls=%fused_computation.19.clone.1 | loop fusion | flops 786432 | bytes 1978368 | tf_op jit(solution)/shard_map/while/body/eval_jaxpr/add | solution.py:61
  497.1 13.2 %all_gather.65 = bf16[768,256]{1,0:T(8,128)(2,1)S(1)} all-gather(bf16[96,256]{1,0:T(8,128)(2,1)S(1)} %bitcast.284), channel_id=1, replica_groups=mesh['req'=8,'mlp'=16] {'req'}, dimensions={0}, use_global_device_ids=true | all-gather | bytes 442368 | tf_op jit(solution)/shard_map/all_gather | solution.py:184
  513.1 72.3 %reduce-scatter.7.cloned.1.call-done = bf16[48,512]{1,0:T(8,128)(2,1)} async-done(((bf16[768,512]{1,0:T(8,128)(2,1)}), bf16[48,512]{1,0:T(8,128)(2,1)}) %reduce-scatter.7.cloned.1.call-update) | async-done | bytes 49168 | tf_op jit(solution)/shard_map/reduce_scatter | solution.py:185
  586.2 13.5 %all_gather.66 = bf16[48,4096]{1,0:T(8,128)(2,1)S(1)} all-gather(bf16[48,512]{1,0:T(8,128)(2,1)S(1)} %get-tuple-element.514), channel_id=1, replica_groups=mesh['req'=8,'mlp'=16] {'req'}, dimensions={1}, use_global_device_ids=true | all-gather | bytes 442368 | tf_op jit(solution)/shard_map/all_gather | solution.py:47
  600.2 13.0 %all_gather.68 = bf16[48,4096]{1,0:T(8,128)(2,1)S(1)} all-gather(bf16[48,512]{1,0:T(8,128)(2,1)S(1)} %get-tuple-element.515), channel_id=1, replica_groups=mesh['req'=8,'mlp'=16] {'req'}, dimensions={1}, use_global_device_ids=true | all-gather | bytes 442368 | tf_op jit(solution)/shard_map/all_gather | solution.py:47
  613.7 23.6 %all_gather.67 = bf16[768,512]{1,0:T(8,128)(2,1)S(1)} all-gather(bf16[48,512]{1,0:T(8,128)(2,1)S(1)} %get-tuple-element.532), channel_id=1, replica_groups=mesh['req'=8,'mlp'=16] {'mlp'}, dimensions={0}, use_global_device_ids=true | all-gather | bytes 835584 | tf_op jit(solution)/shard_map/all_gather | solution.py:197
  639.3 22.6 %all_gather.69 = bf16[768,512]{1,0:T(8,128)(2,1)S(1)} all-gather(bf16[48,512]{1,0:T(8,128)(2,1)S(1)} %get-tuple-element.533), channel_id=1, replica_groups=mesh['req'=8,'mlp'=16] {'mlp'}, dimensions={0}, use_global_device_ids=true | all-gather | bytes 835584 | tf_op jit(solution)/shard_map/all_gather | solution.py:197
  670.0 33.3 %reduce-scatter.11.cloned.1.call-done = bf16[96,768]{1,0:T(8,128)(2,1)} async-done(((bf16[768,768]{1,0:T(8,128)(2,1)}), bf16[96,768]{1,0:T(8,128)(2,1)}) %reduce-scatter.11.cloned.1.call-update) | async-done | bytes 147472 | tf_op jit(solution)/shard_map/reduce_scatter | solution.py:201
  (282 shorter events, 156.2 us)
Async XLA Ops:
  7.2 125.5 %copy-start = (bf16[512,1024]{1,0:T(8,128)(2,1)S(1)}, bf16[512,1024]{1,0:T(8,128)(2,1)}, u32[]{:S(2)}) copy-start(bf16[512,1024]{1,0:T(8,128)(2,1)} %param.19) | copy-start | bytes 3145732
  7.2 77.3 %copy-start.22 = (bf16[512,768]{1,0:T(8,128)(2,1)S(1)}, bf16[512,768]{1,0:T(8,128)(2,1)}, u32[]{:S(2)}) copy-start(bf16[512,768]{1,0:T(8,128)(2,1)} %param.18) | copy-start | bytes 2359300
  7.2 77.2 %all-gather.7.cloned.1.call-start = ((), (), s32[]{:S(2)}) async-start(), calls=%async_computation.4 | async-start | bytes 1671168 | tf_op jit(solution)/shard_map/all_gather | solution.py:118
  39.3 91.1 %all-gather.11.cloned.1.call-start = ((), (), s32[]{:S(2)}) async-start(), calls=%async_computation.7 | async-start | bytes 1671168 | tf_op jit(solution)/shard_map/all_gather | solution.py:118
  40.0 177.2 %all-reduce.3.cloned.1.call-start = ((), (), s32[]{:S(2)}) async-start(), calls=%async_computation.12 | async-start | bytes 11010048 | tf_op jit(solution)/shard_map/psum | solution.py:123
  130.4 2.3 copy-start.20
  133.7 2.0 copy-start.19
  138.5 204.9 %all-gather.13.cloned.1.call-start = ((), (), s32[]{:S(2)}) async-start(), calls=%async_computation.8 | async-start | bytes 3538944 | tf_op jit(solution)/shard_map/all_gather | solution.py:21
  221.9 5.0 copy-start.5
  226.9 2.4 copy-start.6
  234.5 4.8 copy-start.3
  243.7 17.0 %copy-start.24 = (s32[1,96]{1,0:T(1,128)S(1)}, s32[1,96]{1,0:T(1,128)}, u32[]{:S(2)}) copy-start(s32[1,96]{1,0:T(1,128)} %param.27) | copy-start | bytes 1156
  248.9 101.5 %all-gather.9.cloned.1.call-start = ((), (), s32[]{:S(2)}) async-start(), calls=%async_computation.5 | async-start | bytes 3538944 | tf_op jit(solution)/shard_map/all_gather | solution.py:21
  260.7 4.9 copy-start.16
  262.7 0.7 copy-start.10
  284.5 38.2 %copy-start.11 = (bf16[8,768,2]{1,2,0:T(2,128)(2,1)}, bf16[8,768,2]{1,2,0:T(2,128)(2,1)S(1)}, u32[]{:S(2)}) copy-start(bf16[8,768,2]{1,2,0:T(2,128)(2,1)S(1)} %all_gather.62) | copy-start | bytes 73732
  322.6 4.6 copy-start.12
  322.8 190.3 %reduce-scatter.5.cloned.1.call-start = ((), (), s32[]{:S(2)}) async-start(), calls=%async_computation.6 | async-start | bytes 835584 | tf_op jit(solution)/shard_map/reduce_scatter | solution.py:185
  322.9 3.7 copy-start.13
  323.6 2.6 copy-start.4
  326.2 1.2 copy-start.21
  352.1 76.5 %copy-start.8 = (bf16[256,512]{1,0:T(8,128)(2,1)S(1)}, bf16[256,512]{1,0:T(8,128)(2,1)}, u32[]{:S(2)}) copy-start(bf16[256,512]{1,0:T(8,128)(2,1)} %param.20) | copy-start | bytes 786436
  412.4 16.1 %copy-start.7 = (f32[768,512]{1,0:T(8,128)S(1)}, f32[768,512]{1,0:T(8,128)}, u32[]{:S(2)}) copy-start(f32[768,512]{1,0:T(8,128)} %fusion.40) | copy-start | bytes 4718596
  429.9 155.5 %reduce-scatter.7.cloned.1.call-start = ((), (), s32[]{:S(2)}) async-start(), calls=%async_computation.9 | async-start | bytes 835584 | tf_op jit(solution)/shard_map/reduce_scatter | solution.py:185
  429.9 65.2 %copy-start.17 = (f32[96,2]{0,1:T(2,128)S(1)}, f32[96,2]{0,1:T(2,128)}, u32[]{:S(2)}) copy-start(f32[96,2]{0,1:T(2,128)} %fusion.162) | copy-start | bytes 2308
  429.9 65.3 %copy-start.14 = (f32[96,2,2]{0,1,2:T(2,128)S(1)}, f32[96,2,2]{0,1,2:T(2,128)}, u32[]{:S(2)}) copy-start(f32[96,2,2]{0,1,2:T(2,128)} %copy-done.13) | copy-start | bytes 4612
  495.1 90.3 %copy-start.9 = (bf16[2,48,512]{2,1,0:T(8,128)(2,1)S(1)}, bf16[2,48,512]{2,1,0:T(8,128)(2,1)}, u32[]{:S(2)}) copy-start(bf16[2,48,512]{2,1,0:T(8,128)(2,1)} %param.16) | copy-start | bytes 294916
  510.2 103.4 %copy-start.15 = (f32[1,512]{1,0:T(1,128)S(1)}, f32[1,512]{1,0:T(1,128)}, u32[]{:S(2)}) copy-start(f32[1,512]{1,0:T(1,128)} %get-tuple-element.518) | copy-start | bytes 6148
  510.2 127.1 %copy-start.23 = (bf16[512,768]{1,0:T(8,128)(2,1)S(1)}, bf16[512,768]{1,0:T(8,128)(2,1)}, u32[]{:S(2)}) copy-start(bf16[512,768]{1,0:T(8,128)(2,1)} %param.22) | copy-start | bytes 2359300
  513.0 157.0 %reduce-scatter.9.cloned.1.call-start = ((), (), s32[]{:S(2)}) async-start(), calls=%async_computation.10 | async-start | bytes 1327104 | tf_op jit(solution)/shard_map/reduce_scatter | solution.py:201
  639.2 65.8 %copy-start.1 = (bf16[512,1024]{1,0:T(8,128)(2,1)S(1)}, bf16[512,1024]{1,0:T(8,128)(2,1)}, u32[]{:S(2)}) copy-start(bf16[512,1024]{1,0:T(8,128)(2,1)} %param.19) | copy-start | bytes 3145732
  639.2 64.1 %reduce-scatter.11.cloned.1.call-start = ((), (), s32[]{:S(2)}) async-start(), calls=%async_computation.11 | async-start | bytes 1327104 | tf_op jit(solution)/shard_map/reduce_scatter | solution.py:201
  (2 other events, 1.4 us)
Sparse Core Ops, SparseCore 0:
  39.4 44.9 all-gather.6
  87.2 43.1 all-gather.10
  138.7 78.5 all-reduce.2
  249.0 27.8 all-gather.12
  322.9 27.4 all-gather.8
  430.0 72.2 reduce-scatter.4
  513.1 72.2 reduce-scatter.6
  639.3 30.6 reduce-scatter.8
  672.4 30.8 reduce-scatter.10
where the time goes:
time: 718 us; the launch traced here: 712 us
  waiting for transfers between devices  275 us (38%)
  blocking collectives  177 us (25%)
  other arithmetic  130 us (18%)
  local copies, waits for them, and re-layouts  56.3 us (8%)
  matrix products  45.8 us (6%)
  between operations  14.9 us (2%)
  starting transfers between devices  12.4 us (2%)
    add x14, other arithmetic, merge_partials(): first[2] * left[..., None] + second[2] * right[..., None]  99.9 us
    all_gather x2, waiting for transfers between devices, shards(): piece = lax.all_gather(joined, 'mlp', axis=0, tiled=True)  87.7 us
    reduce_scatter x2, waiting for transfers between devices, shards(): lax.psum_scatter((jnp.dot(attended_all, dense_weight, preferred_element_t...  72.3 us
    psum x1, waiting for transfers between devices, shards(): lax.psum(partial_sums.astype(jnp.bfloat16), 'req').astype(jnp.float32)  70.9 us
    all_gather x4, blocking collectives, row_normalize(): whole = lax.all_gather(block, 'req', axis=1, tiled=True).astype(jnp.float32)  53.7 us
    all_gather x4, blocking collectives, combined_all(): lax.all_gather(part.astype(kind), axis)  50.7 us
    all_gather x2, blocking collectives, shards(): lax.all_gather(next_in, 'mlp', axis=0, tiled=True)  46.3 us
    reduce_scatter x2, waiting for transfers between devices, shards(): lax.psum_scatter(next_partial.astype(jnp.bfloat16), 'req', scatter_dimens...  38.9 us
  transfers between devices with their start and end apart: 9, of which 7 were waited for; matrix products, arithmetic and copies ran while one was open for 16% of the time, Pallas kernels for 0%

commit v1 on v0

v1 whole, which is shorter than its diff:
```python
import math

import jax
import jax.numpy as jnp
from jax import lax
from jax.sharding import PartitionSpec as P

HD = 128
ROT = 32
PAGE = 128
BEAM = 8
STEPS = 2


NEG_FILL = -1e30
EPSILON = 1e-05


def rotate(vectors, positions):
    half = ROT // 2
    freq = jnp.exp(jnp.arange(half, dtype=jnp.float32) * (-2.0 * math.log(10000.0) / ROT))
    angles = positions.astype(jnp.float32)[..., None] * freq
    cosine = jnp.concatenate([jnp.cos(angles), jnp.cos(angles)], axis=-1)[..., None, :]
    sine = jnp.concatenate([jnp.sin(angles), jnp.sin(angles)], axis=-1)[..., None, :]
    turned = vectors[..., :ROT]
    swapped = jnp.concatenate([-turned[..., half:], turned[..., :half]], axis=-1)
    return jnp.concatenate([turned * cosine + swapped * sine, vectors[..., ROT:]], axis=-1)


def row_normalize(values):
    width = values.shape[-1]
    local_mean = jnp.mean(values, axis=-1)
    centred = values - local_mean[..., None]
    local_m2 = jnp.sum(centred * centred, axis=-1)
    stats = lax.all_gather(jnp.stack([local_mean, local_m2], axis=-1), "req")
    means = stats[..., 0]
    row_mean = jnp.mean(means, axis=0)
    spread = means - row_mean
    row_m2 = jnp.sum(stats[..., 1], axis=0) + width * jnp.sum(spread * spread, axis=0)
    row_var = row_m2 / (width * stats.shape[0])
    return (values - row_mean[..., None]) * lax.rsqrt(row_var + EPSILON)[..., None]


def shards(
    inputs,
    norm_gains,
    attn_weight,
    up_weight,
    dense_weight,
    down_weight,
    next_weight,
    cache_keys,
    cache_values,
    lengths,
    slot_table,
    parents,
):
    scale = 1.0 / math.sqrt(HD)
    highest = lax.Precision.HIGHEST
    steps, local_rows, local_width = inputs.shape
    own_count = parents.shape[1]
    request_count = lengths.shape[0]
    beam_total = request_count * BEAM
    head_count = dense_weight.shape[0] // HD
    triple_width = attn_weight.shape[1]
    slot_count = slot_table.shape[1]
    req_size = beam_total // own_count
    mlp_size = beam_total // local_rows
    offset = lax.axis_index("req") * own_count
    beam_group = jnp.arange(beam_total, dtype=jnp.int32) // BEAM
    all_positions = lengths[beam_group][None, :] + jnp.arange(steps, dtype=jnp.int32)[:, None]
    own_group = jnp.arange(own_count, dtype=jnp.int32) // BEAM
    slot_owner = slot_table[0]
    slot_pageno = slot_table[1]
    valid_owner = jnp.maximum(slot_owner, 0)
    token_pos = slot_pageno[:, None] * PAGE + jnp.arange(PAGE, dtype=jnp.int32)[None, :]
    live = (slot_owner[:, None] >= 0) & (token_pos < lengths[valid_owner][:, None])
    live_wide = live[None, :, None, None, :]
    owner_mask = slot_owner[:, None] == jnp.arange(request_count, dtype=jnp.int32)[None, :]
    owner_float = owner_mask.astype(jnp.float32)
    gather_rows = valid_owner[:, None] * BEAM + jnp.arange(BEAM, dtype=jnp.int32)[None, :]
    page_keys = cache_keys.reshape(slot_count, PAGE, head_count, HD)
    page_values = cache_values.reshape(slot_count, PAGE, head_count, HD)

    block = inputs.astype(jnp.float32)
    normed = row_normalize(block)
    attn_in = (normed * norm_gains[0]).astype(jnp.bfloat16)
    mlp_in = (normed * norm_gains[1]).astype(jnp.bfloat16)
    joined = jnp.concatenate([attn_in, mlp_in], axis=-1)
    piece = lax.all_gather(joined, "mlp", axis=1, tiled=True).reshape(steps * beam_total, -1)
    first = jnp.dot(piece[:, :local_width], attn_weight, preferred_element_type=jnp.float32)
    second = jnp.dot(piece[:, local_width:], up_weight, preferred_element_type=jnp.float32)
    partial_sums = jnp.concatenate([first, second], axis=1)
    summed_all = lax.psum(partial_sums.astype(jnp.bfloat16), "req").astype(jnp.float32)
    mixed_all = summed_all[:, :triple_width].reshape(steps, beam_total, head_count, 3, HD)
    activated_all = jax.nn.gelu(summed_all[:, triple_width:], approximate=False).astype(
        jnp.bfloat16
    )
    queries_all = rotate(mixed_all[:, :, :, 0], all_positions).astype(jnp.bfloat16)
    mixed_own = lax.dynamic_slice_in_dim(mixed_all, offset, own_count, 1)
    own_positions = lax.dynamic_slice_in_dim(all_positions, offset, own_count, 1)
    queries_own = lax.dynamic_slice_in_dim(queries_all, offset, own_count, 1)
    keys_new = rotate(mixed_own[:, :, :, 1], own_positions).astype(jnp.bfloat16)
    values_new = mixed_own[:, :, :, 2].astype(jnp.bfloat16)

    chosen = queries_all[:, gather_rows]
    scores = (
        jnp.einsum("zsbhd,sthd->zsbht", chosen, page_keys, preferred_element_type=jnp.float32)
        * scale
    )
    masked = jnp.where(live_wide, scores, NEG_FILL)
    slot_top = jnp.max(masked, axis=4)
    weights = jnp.where(live_wide, jnp.exp(masked - slot_top[..., None]), 0.0)
    slot_total = jnp.sum(weights, axis=4)
    slot_out = jnp.einsum(
        "zsbht,sthd->zsbhd",
        weights.astype(jnp.bfloat16),
        page_values,
        preferred_element_type=jnp.float32,
    )
    request_top = jnp.max(
        jnp.where(owner_mask[None, :, :, None, None], slot_top[:, :, None], NEG_FILL), axis=1
    )
    factor = jnp.exp(slot_top - request_top[:, valid_owner])
    page_total = jnp.einsum(
        "sr,zsbh->zrbh", owner_float, slot_total * factor, precision=highest
    ).reshape(steps, beam_total, head_count)
    page_out = jnp.einsum(
        "sr,zsbhd->zrbhd", owner_float, slot_out * factor[..., None], precision=highest
    ).reshape(steps, beam_total, head_count, HD)
    page_top = request_top.reshape(steps, beam_total, head_count)
    global_top = lax.pmax(page_top, "req")
    rescale = jnp.exp(page_top - global_top)
    partial = jnp.concatenate(
        [page_out * rescale[..., None], (page_total * rescale)[..., None]], axis=-1
    )
    own_partial = lax.psum_scatter(
        partial.astype(jnp.bfloat16), "req", scatter_dimension=1, tiled=True
    ).astype(jnp.float32)
    own_top = lax.dynamic_slice_in_dim(global_top, offset, own_count, 1)
    own_out = own_partial[..., :HD]
    own_total = own_partial[..., HD]

    source = own_group * BEAM + parents[0]
    attended_steps = []
    for step_index in range(steps):
        tail_keys = [keys_new[prior][source] for prior in range(step_index)]
        tail_values = [values_new[prior][source] for prior in range(step_index)]
        history_keys = jnp.stack(tail_keys + [keys_new[step_index]], axis=0)
        history_values = jnp.stack(tail_values + [values_new[step_index]], axis=0)
        own_scores = (
            jnp.einsum(
                "bhd,nbhd->bhn",
                queries_own[step_index],
                history_keys,
                preferred_element_type=jnp.float32,
            )
            * scale
        )
        top = jnp.maximum(own_top[step_index], jnp.max(own_scores, axis=2))
        page_factor = jnp.exp(own_top[step_index] - top)
        own_weights = jnp.exp(own_scores - top[..., None])
        total = own_total[step_index] * page_factor + jnp.sum(own_weights, axis=2)
        summed = own_out[step_index] * page_factor[..., None] + jnp.einsum(
            "bhn,nbhd->bhd",
            own_weights.astype(jnp.bfloat16),
            history_values,
            preferred_element_type=jnp.float32,
        )
        attended_steps.append(
            (summed / total[..., None]).astype(jnp.bfloat16).reshape(own_count, head_count * HD)
        )
    attended = jnp.stack(attended_steps)
    attended_all = lax.all_gather(attended, "req", axis=1, tiled=True)

    def by_mlp(rows):
        return (
            rows.reshape(steps, mlp_size, local_rows, -1)
            .transpose(1, 0, 2, 3)
            .reshape(steps * beam_total, -1)
        )

    update = lax.psum_scatter(
        (
            jnp.dot(by_mlp(attended_all), dense_weight, preferred_element_type=jnp.float32)
            + jnp.dot(
                by_mlp(activated_all.reshape(steps, beam_total, -1)),
                down_weight,
                preferred_element_type=jnp.float32,
            )
        ).astype(jnp.bfloat16),
        "mlp",
        scatter_dimension=0,
        tiled=True,
    ).astype(jnp.float32)
    layer = (block + update.reshape(steps, local_rows, local_width)).astype(jnp.bfloat16)
    next_in = (row_normalize(layer.astype(jnp.float32)) * norm_gains[2]).astype(jnp.bfloat16)
    gathered = lax.all_gather(next_in, "mlp", axis=1, tiled=True)
    by_req = (
        gathered.reshape(steps, req_size, own_count, local_width)
        .transpose(1, 0, 2, 3)
        .reshape(steps * beam_total, local_width)
    )
    next_partial = jnp.dot(by_req, next_weight, preferred_element_type=jnp.float32)
    next_out = lax.psum_scatter(
        next_partial.astype(jnp.bfloat16), "req", scatter_dimension=0, tiled=True
    ).reshape(steps, own_count, -1)
    return (layer, next_out)


def solution(mesh):
    in_specs = (
        P(None, "mlp", "req"),
        P(None, "req"),
        P("req", "mlp"),
        P("req", "mlp"),
        P("mlp", "req"),
        P("mlp", "req"),
        P("req", "mlp"),
        P("req", None, "mlp"),
        P("req", None, "mlp"),
        P(),
        P(None, "req"),
        P(None, "req"),
    )
    out_specs = (P(None, "mlp", "req"), P(None, "req", "mlp"))
    return jax.shard_map(shards, mesh=mesh, in_specs=in_specs, out_specs=out_specs, check_vma=False)
```

time: 718 us -> 449 us (0.63)
  blocking collectives: 177 us -> 63.5 us
  other arithmetic: 130 us -> 34.5 us
  matrix products: 45.8 us -> 25.1 us
  waiting for transfers between devices: 275 us -> 255 us
  starting transfers between devices: 12.4 us -> 0.69 us
    all_gather x12 -> x3, blocking collectives: 177 us -> 38.4 us  [the longest x2 25 us: row_normalize(): stats = lax.all_gather(jnp.stack([local_mean, local_m2], axis=-1), 'req')]
    add x30 -> x2, other arithmetic: 106 us -> 0.1 us  [the longest x1 0.09 us: shards(): total = own_total[step_index] * page_factor + jnp.sum(own_weights, axis=2)]
    pmax x0 -> x1, blocking collectives: none -> 25.1 us  [shards(): global_top = lax.pmax(page_top, 'req')]
    reshape x1 -> x6, local copies, waits for them, and re-layouts: 0.1 us -> 21 us  [the longest x1 7.1 us: shards(): page_keys = cache_keys.reshape(slot_count, PAGE, head_count, HD)]
    dot_general x18 -> x10, matrix products: 45.8 us -> 25.1 us  [the longest x1 4.62 us: shards(): jnp.einsum('zsbhd,sthd->zsbht', chosen, page_keys, preferred_element_type...]
    dynamic_slice x15 -> x0, local copies, waits for them, and re-layouts: 16.1 us -> none  [the longest x14 14.4 us: take(): part[k].astype(own.dtype)]
    convert_element_type x13 -> x5, other arithmetic: 4.1 us -> 17.1 us  [the longest x1 14.3 us: shards(): jax.nn.gelu(summed_all[:, triple_width:], approximate=False)]
    all_gather x4 -> x2, starting transfers between devices: 12.2 us -> 0.08 us  [the longest x1 0.04 us: shards(): gathered = lax.all_gather(next_in, 'mlp', axis=1, tiled=True)]
  transfers between devices with their start and end apart: 9 -> 6, of which waited for: 7 -> 5; matrix products, arithmetic and copies ran while one was open for 16% -> 12% of each run, Pallas kernels for 0% -> 0%
where the time goes in v1:
time: 449 us; the launch traced here: 447 us
  waiting for transfers between devices  255 us (57%)
  blocking collectives  63.5 us (14%)
  local copies, waits for them, and re-layouts  54 us (12%)
  other arithmetic  34.5 us (8%)
  matrix products  25.1 us (6%)
  between operations  14.9 us (3%)
    reduce_scatter x1, waiting for transfers between devices, shards(): lax.psum_scatter((jnp.dot(by_mlp(attended_all), dense_weight, preferred_e...  73.2 us
    psum x1, waiting for transfers between devices, shards(): lax.psum(partial_sums.astype(jnp.bfloat16), 'req').astype(jnp.float32)  61.8 us
    all_gather x1, waiting for transfers between devices, shards(): lax.all_gather(joined, 'mlp', axis=1, tiled=True)  43.9 us
    all_gather x1, waiting for transfers between devices, shards(): gathered = lax.all_gather(next_in, 'mlp', axis=1, tiled=True)  42.1 us
    reduce_scatter x1, waiting for transfers between devices, shards(): lax.psum_scatter(next_partial.astype(jnp.bfloat16), 'req', scatter_dimens...  33.9 us
    pmax x1, blocking collectives, shards(): global_top = lax.pmax(page_top, 'req')  25.1 us
    all_gather x2, blocking collectives, row_normalize(): stats = lax.all_gather(jnp.stack([local_mean, local_m2], axis=-1), 'req')  25 us
    convert_element_type x1, other arithmetic, shards(): jax.nn.gelu(summed_all[:, triple_width:], approximate=False)  14.3 us
  transfers between devices with their start and end apart: 6, of which 5 were waited for; matrix products, arithmetic and copies ran while one was open for 12% of the time, Pallas kernels for 0%

profile of v1, /device:TPU:0, one launch (start us, length us, event | category | flops | bytes accessed | tf_op | source)
XLA Modules:
  0.0 447.5 jit_solution(17252215852238983425)
XLA Ops:
  9.4 12.9 %all-gather = f32[16,48,2]{1,2,0:T(2,128)S(1)} all-gather(f32[2,48,2]{1,2,0:T(2,128)S(1)} %copy.245), channel_id=2, replica_groups=mesh['req'=8,'mlp'=16] {'req'}, dimensions={0}, use_global_device_ids=true | all-gather | bytes 6912 | tf_op jit(solution)/shard_map/all_gather | solution.py:35
  25.0 4.6 %gather_fusion.1 = s32[768]{0:T(1024)S(1)} fusion(s32[96]{0:T(128)} %param.21, s32[1024]{0:T(1024)S(1)} %pad_clamp_fusion.2), kind=kCustom, calls=%fused_computation.1 | custom fusion | bytes 9216 | tf_op jit(solution)/shard_map/gather | solution.py:71
  29.6 43.9 %all-gather.5.cloned.1.call-done = bf16[2,768,1024]{2,1,0:T(8,128)(2,1)} async-done(((bf16[2,48,1024]{2,1,0:T(8,128)(2,1)}), bf16[2,768,1024]{2,1,0:T(8,128)(2,1)}) %all-gather.5.cloned.1.call-update) | async-done | bytes 3145744 | tf_op jit(solution)/shard_map/all_gather | solution.py:90
  73.4 3.4 convolution_convert_fusion
  76.9 1.5 convolution_convert_fusion.2
  78.3 2.8 pad_maximum_fusion
  82.7 7.1 %reshape.445 = bf16[64,128,2,128]{3,2,1,0:T(2,128)(2,1)} reshape(bf16[64,128,256]{2,1,0:T(8,128)(2,1)} %param.19) | data formatting | bytes 8388608 | tf_op jit(solution)/shard_map/reshape | solution.py:82
  89.8 7.0 %reshape.446 = bf16[64,128,2,128]{3,2,1,0:T(2,128)(2,1)} reshape(bf16[64,128,256]{2,1,0:T(8,128)(2,1)} %param.20) | data formatting | bytes 8388608 | tf_op jit(solution)/shard_map/reshape | solution.py:83
  97.5 61.8 %all-reduce.2.cloned.1.call-done = bf16[1536,1792]{0,1:T(8,128)(2,1)} async-done(((bf16[1536,1792]{0,1:T(8,128)(2,1)}), bf16[1536,1792]{0,1:T(8,128)(2,1)}) %all-reduce.2.cloned.1.call-update) | async-done | bytes 5505040 | tf_op jit(solution)/shard_map/psum | solution.py:94
  159.2 4.5 %slice.183 = f32[1536,768]{0,1:T(8,128)} slice(bf16[1536,1792]{0,1:T(8,128)(2,1)} %all-reduce.2.cloned.1.call-done), slice={[0:1536], [0:768]} | slice | bytes 9437184 | tf_op jit(solution)/shard_map/slice | solution.py:95
  163.8 6.6 %reshape.444 = f32[2,768,2,3,128]{1,0,4,3,2:T(2,128)} reshape(f32[1536,768]{0,1:T(8,128)} %slice.183) | data formatting | bytes 9437184 | tf_op jit(solution)/shard_map/reshape | solution.py:95
  171.9 2.0 slice.184
  175.0 2.3 gather_fusion.2
  177.3 4.6 %fusion.101 = (f32[2,64,8,2]{2,0,3,1:T(2,128)S(1)}, f32[2,64,8,2,128]{4,2,0,3,1:T(8,128)S(1)}) fusion(bf16[64,128,2,128,1]{3,2,1,0,4:T(2,128)(2,1)} %bitcast.170, pred[64,128]{1,0:T(8,128)(4,1)S(1)} %fusion.74, bf16[512,2,2,128]{3,2,1,0:T(2,128)(2,1)S(1)} %gather_fusion.2), kind=kOutput, calls=%fused_computation.210 | convolution fusion | flops 67893248 | bytes 5783552 | tf_op jit(solution)/shard_map/zsbhd,sthd->zsbht/dot_general | solution.py:108
  184.8 25.1 %pmax.7 = f32[2,768,2]{1,2,0:T(2,128)S(1)} all-reduce(f32[2,768,2]{1,2,0:T(2,128)S(1)} %reshape.448), channel_id=1, replica_groups=mesh['req'=8,'mlp'=16] {'req'}, use_global_device_ids=true, to_apply=%region_8.9 | all-reduce | flops 3072 | bytes 24576 | tf_op jit(solution)/shard_map/pmax | solution.py:132
  211.6 3.6 fusion.30
  215.3 1.5 convolution_bitcast_fusion
  218.8 1.5 pad_maximum_fusion.1
  220.6 4.1 convert_element_type.70
  224.7 14.3 %fusion.2 = bf16[1536,1024]{0,1:T(8,128)(2,1)} fusion(f32[1536,1792]{0,1:T(8,128)S(1)} %convert_element_type.70), kind=kLoop, calls=%fused_computation.9 | loop fusion | flops 102236160 | bytes 9437184 | tf_op jit(solution)/shard_map/convert_element_type | solution.py:96
  239.3 1.9 dynamic-slice_convert_fusion
  242.5 4.8 %copy.278 = bf16[1536,1024]{1,0:T(8,128)(2,1)} copy(bf16[1536,1024]{0,1:T(8,128)(2,1)} %fusion.2) | data formatting | bytes 6291456 | tf_op jit(solution)/shard_map/convert_element_type | solution.py:96
  247.3 2.4 copy.279
  250.4 3.5 fusion.102
  255.5 13.5 %all_gather.24 = bf16[2,768,256]{2,1,0:T(8,128)(2,1)S(1)} all-gather(bf16[2,96,256]{2,1,0:T(8,128)(2,1)S(1)} %pad_maximum_fusion.7), channel_id=1, replica_groups=mesh['req'=8,'mlp'=16] {'req'}, dimensions={1}, use_global_device_ids=true | all-gather | bytes 884736 | tf_op jit(solution)/shard_map/all_gather | solution.py:174
  269.0 3.7 fusion.14
  272.8 73.2 %reduce-scatter.6.cloned.1.call-done = bf16[96,512]{1,0:T(8,128)(2,1)} async-done(((bf16[1536,512]{1,0:T(8,128)(2,1)}), bf16[96,512]{1,0:T(8,128)(2,1)}) %reduce-scatter.6.cloned.1.call-update) | async-done | bytes 98320 | tf_op jit(solution)/shard_map/reduce_scatter | solution.py:183
  347.2 12.1 %all-gather.1 = f32[16,48,2]{1,2,0:T(2,128)S(1)} all-gather(f32[2,48,2]{1,2,0:T(2,128)S(1)} %copy.280), channel_id=3, replica_groups=mesh['req'=8,'mlp'=16] {'req'}, dimensions={0}, use_global_device_ids=true | all-gather | bytes 6912 | tf_op jit(solution)/shard_map/all_gather | solution.py:35
  360.2 42.1 %all-gather.7.cloned.1.call-done = bf16[2,768,512]{2,1,0:T(8,128)(2,1)} async-done(((bf16[2,48,512]{2,1,0:T(8,128)(2,1)}), bf16[2,768,512]{2,1,0:T(8,128)(2,1)}) %all-gather.7.cloned.1.call-update) | async-done | bytes 1572880 | tf_op jit(solution)/shard_map/all_gather | solution.py:198
  402.3 1.6 copy.281
  403.9 2.8 convolution_convert_fusion.1
  406.7 33.9 %reduce-scatter.8.cloned.1.call-done = bf16[192,768]{1,0:T(8,128)(2,1)} async-done(((bf16[1536,768]{1,0:T(8,128)(2,1)}), bf16[192,768]{1,0:T(8,128)(2,1)}) %reduce-scatter.8.cloned.1.call-update) | async-done | bytes 294928 | tf_op jit(solution)/shard_map/reduce_scatter | solution.py:205
  (145 shorter events, 22.4 us)
Async XLA Ops:
  7.2 66.3 %copy-start = (bf16[512,1024]{1,0:T(8,128)(2,1)S(1)}, bf16[512,1024]{1,0:T(8,128)(2,1)}, u32[]{:S(2)}) copy-start(bf16[512,1024]{1,0:T(8,128)(2,1)} %param.15) | copy-start | bytes 3145732
  7.2 66.2 %all-gather.5.cloned.1.call-start = ((), (), s32[]{:S(2)}) async-start(), calls=%async_computation.3 | async-start | bytes 3342336 | tf_op jit(solution)/shard_map/all_gather | solution.py:90
  24.9 134.4 %all-reduce.2.cloned.1.call-start = ((), (), s32[]{:S(2)}) async-start(), calls=%async_computation.4 | async-start | bytes 11010048 | tf_op jit(solution)/shard_map/psum | solution.py:94
  73.4 3.4 copy-start.7
  73.4 3.4 copy-start.9
  78.3 3.4 copy-start.6
  78.3 3.6 copy-start.2
  81.2 172.7 %reduce-scatter.4.cloned.1.call-start = ((), (), s32[]{:S(2)}) async-start(), calls=%async_computation.5 | async-start | bytes 1769472 | tf_op jit(solution)/shard_map/reduce_scatter | solution.py:137
  89.8 7.0 %copy-start.11 = (s32[1,96]{1,0:T(1,128)S(1)}, s32[1,96]{1,0:T(1,128)}, u32[]{:S(2)}) copy-start(s32[1,96]{1,0:T(1,128)} %param.23) | copy-start | bytes 1156
  220.3 125.6 %reduce-scatter.6.cloned.1.call-start = ((), (), s32[]{:S(2)}) async-start(), calls=%async_computation.6 | async-start | bytes 1671168 | tf_op jit(solution)/shard_map/reduce_scatter | solution.py:183
  242.5 7.8 %copy-start.8 = (bf16[1024,512]{1,0:T(8,128)(2,1)S(1)}, bf16[1024,512]{1,0:T(8,128)(2,1)}, u32[]{:S(2)}) copy-start(bf16[1024,512]{1,0:T(8,128)(2,1)} %param.17) | copy-start | bytes 3145732
  250.3 18.7 %copy-start.5 = (bf16[256,512]{1,0:T(8,128)(2,1)S(1)}, bf16[256,512]{1,0:T(8,128)(2,1)}, u32[]{:S(2)}) copy-start(bf16[256,512]{1,0:T(8,128)(2,1)} %param.16) | copy-start | bytes 786436
  253.8 92.1 %copy-start.3 = (bf16[2,48,512]{2,1,0:T(8,128)(2,1)S(1)}, bf16[2,48,512]{2,1,0:T(8,128)(2,1)}, u32[]{:S(2)}) copy-start(bf16[2,48,512]{2,1,0:T(8,128)(2,1)} %param.12) | copy-start | bytes 294916
  268.9 134.9 %copy-start.10 = (bf16[512,768]{1,0:T(8,128)(2,1)S(1)}, bf16[512,768]{1,0:T(8,128)(2,1)}, u32[]{:S(2)}) copy-start(bf16[512,768]{1,0:T(8,128)(2,1)} %param.18) | copy-start | bytes 2359300
  272.7 129.6 %all-gather.7.cloned.1.call-start = ((), (), s32[]{:S(2)}) async-start(), calls=%async_computation.7 | async-start | bytes 1671168 | tf_op jit(solution)/shard_map/all_gather | solution.py:198
  347.0 59.7 %copy-start.4 = (bf16[2,48,512]{2,1,0:T(8,128)(2,1)}, bf16[2,48,512]{2,1,0:T(8,128)(2,1)S(1)}, u32[]{:S(2)}) copy-start(bf16[2,48,512]{2,1,0:T(8,128)(2,1)S(1)} %get-tuple-element.9) | copy-start | bytes 294916
  360.1 80.5 %reduce-scatter.8.cloned.1.call-start = ((), (), s32[]{:S(2)}) async-start(), calls=%async_computation.8 | async-start | bytes 2654208 | tf_op jit(solution)/shard_map/reduce_scatter | solution.py:205
  403.9 36.7 %copy-start.1 = (bf16[512,1024]{1,0:T(8,128)(2,1)S(1)}, bf16[512,1024]{1,0:T(8,128)(2,1)}, u32[]{:S(2)}) copy-start(bf16[512,1024]{1,0:T(8,128)(2,1)} %param.15) | copy-start | bytes 3145732
Sparse Core Ops, SparseCore 0:
  25.0 48.3 all-gather.4
  81.3 77.9 all-reduce.1
  220.5 31.5 reduce-scatter.3
  272.8 73.0 reduce-scatter.5
  360.2 42.0 all-gather.6
  406.9 33.7 reduce-scatter.7

commit v2 on v1

--- a/solution.py
+++ b/solution.py
@@ -1,9 +1,14 @@
+import functools
 import math
 
 import jax
 import jax.numpy as jnp
 from jax import lax
+from jax.experimental import pallas as pl
+from jax.experimental.pallas import tpu as pltpu
 from jax.sharding import PartitionSpec as P
+
+MESH = pl.DeviceIdType.MESH
 
 HD = 128
 ROT = 32
@@ -25,6 +30,52 @@
     turned = vectors[..., :ROT]
     swapped = jnp.concatenate([-turned[..., half:], turned[..., :half]], axis=-1)
     return jnp.concatenate([turned * cosine + swapped * sine, vectors[..., ROT:]], axis=-1)
+
+
+def exchange_kernel(axis, n, gather, x_ref, out_ref, send_sem, recv_sem, local_sem):
+    me = lax.axis_index(axis)
+    barrier = pltpu.get_barrier_semaphore()
+    for k in range(1, n):
+        pl.semaphore_signal(
+            barrier, inc=1, device_id={axis: lax.rem(me + k, n)}, device_id_type=MESH
+        )
+    pl.semaphore_wait(barrier, n - 1)
+    local = pltpu.make_async_copy(x_ref if gather else x_ref.at[me], out_ref.at[me], local_sem)
+    local.start()
+    copies = []
+    for k in range(1, n):
+        dest = lax.rem(me + k, n)
+        copy = pltpu.make_async_remote_copy(
+            src_ref=x_ref if gather else x_ref.at[dest],
+            dst_ref=out_ref.at[me],
+            send_sem=send_sem.at[k],
+            recv_sem=recv_sem.at[k],
+            device_id={axis: dest},
+            device_id_type=MESH,
+        )
+        copy.start()
+        copies.append(copy)
+    for copy in copies:
+        copy.wait()
+    local.wait()
+
+
+def exchange(x, axis, n, gather, collective_id):
+    shape = (n,) + (x.shape if gather else x.shape[1:])
+    return pl.pallas_call(
+        functools.partial(exchange_kernel, axis, n, gather),
+        out_shape=jax.ShapeDtypeStruct(shape, x.dtype),
+        in_specs=[pl.BlockSpec(memory_space=pltpu.VMEM)],
+        out_specs=pl.BlockSpec(memory_space=pltpu.VMEM),
+        scratch_shapes=[
+            pltpu.SemaphoreType.DMA((n,)),
+            pltpu.SemaphoreType.DMA((n,)),
+            pltpu.SemaphoreType.DMA(()),
+        ],
+        compiler_params=pltpu.CompilerParams(
+            collective_id=collective_id, has_side_effects=True
+        ),
+    )(x)
 
 
 def row_normalize(values):
@@ -87,17 +138,27 @@
     attn_in = (normed * norm_gains[0]).astype(jnp.bfloat16)
     mlp_in = (normed * norm_gains[1]).astype(jnp.bfloat16)
     joined = jnp.concatenate([attn_in, mlp_in], axis=-1)
-    piece = lax.all_gather(joined, "mlp", axis=1, tiled=True).reshape(steps * beam_total, -1)
+    piece = exchange(joined, "mlp", mlp_size, True, 0).reshape(steps * beam_total, -1)
     first = jnp.dot(piece[:, :local_width], attn_weight, preferred_element_type=jnp.float32)
     second = jnp.dot(piece[:, local_width:], up_weight, preferred_element_type=jnp.float32)
     partial_sums = jnp.concatenate([first, second], axis=1)
     summed_all = lax.psum(partial_sums.astype(jnp.bfloat16), "req").astype(jnp.float32)
-    mixed_all = summed_all[:, :triple_width].reshape(steps, beam_total, head_count, 3, HD)
+    mixed_msi = summed_all[:, :triple_width].reshape(
+        mlp_size, steps, local_rows, head_count, 3, HD
+    )
     activated_all = jax.nn.gelu(summed_all[:, triple_width:], approximate=False).astype(
         jnp.bfloat16
     )
-    queries_all = rotate(mixed_all[:, :, :, 0], all_positions).astype(jnp.bfloat16)
-    mixed_own = lax.dynamic_slice_in_dim(mixed_all, offset, own_count, 1)
+    mixed_all = mixed_msi[:, :, :, :, 0].transpose(1, 0, 2, 3, 4).reshape(
+        steps, beam_total, head_count, HD
+    )
+    queries_all = rotate(mixed_all, all_positions).astype(jnp.bfloat16)
+    per_own = own_count // local_rows
+    mixed_own = (
+        lax.dynamic_slice_in_dim(mixed_msi, lax.axis_index("req") * per_own, per_own, 0)
+        .transpose(1, 0, 2, 3, 4, 5)
+        .reshape(steps, own_count, head_count, 3, HD)
+    )
     own_positions = lax.dynamic_slice_in_dim(all_positions, offset, own_count, 1)
     queries_own = lax.dynamic_slice_in_dim(queries_all, offset, own_count, 1)
     keys_new = rotate(mixed_own[:, :, :, 1], own_positions).astype(jnp.bfloat16)
@@ -172,39 +233,37 @@
         )
     attended = jnp.stack(attended_steps)
     attended_all = lax.all_gather(attended, "req", axis=1, tiled=True)
-
-    def by_mlp(rows):
-        return (
-            rows.reshape(steps, mlp_size, local_rows, -1)
-            .transpose(1, 0, 2, 3)
-            .reshape(steps * beam_total, -1)
-        )
-
-    update = lax.psum_scatter(
-        (
-            jnp.dot(by_mlp(attended_all), dense_weight, preferred_element_type=jnp.float32)
-            + jnp.dot(
-                by_mlp(activated_all.reshape(steps, beam_total, -1)),
-                down_weight,
-                preferred_element_type=jnp.float32,
-            )
-        ).astype(jnp.bfloat16),
-        "mlp",
-        scatter_dimension=0,
-        tiled=True,
-    ).astype(jnp.float32)
+    attended_msi = (
+        attended_all.reshape(steps, mlp_size, local_rows, -1)
+        .transpose(1, 0, 2, 3)
+        .reshape(steps * beam_total, -1)
+    )
+    update_partial = (
+        jnp.dot(attended_msi, dense_weight, preferred_element_type=jnp.float32)
+        + jnp.dot(activated_all, down_weight, preferred_element_type=jnp.float32)
+    ).astype(jnp.bfloat16)
+    update = jnp.sum(
+        exchange(
+            update_partial.reshape(mlp_size, steps * local_rows, local_width),
+            "mlp",
+            mlp_size,
+            False,
+            1,
+        ).astype(jnp.float32),
+        axis=0,
+    )
     layer = (block + update.reshape(steps, local_rows, local_width)).astype(jnp.bfloat16)
     next_in = (row_normalize(layer.astype(jnp.float32)) * norm_gains[2]).astype(jnp.bfloat16)
-    gathered = lax.all_gather(next_in, "mlp", axis=1, tiled=True)
-    by_req = (
-        gathered.reshape(steps, req_size, own_count, local_width)
-        .transpose(1, 0, 2, 3)
-        .reshape(steps * beam_total, local_width)
-    )
-    next_partial = jnp.dot(by_req, next_weight, preferred_element_type=jnp.float32)
+    gathered = exchange(next_in, "mlp", mlp_size, True, 2).reshape(steps * beam_total, -1)
+    next_partial = jnp.dot(gathered, next_weight, preferred_element_type=jnp.float32)
     next_out = lax.psum_scatter(
         next_partial.astype(jnp.bfloat16), "req", scatter_dimension=0, tiled=True
-    ).reshape(steps, own_count, -1)
+    )
+    next_out = (
+        next_out.reshape(per_own, steps, local_rows, -1)
+        .transpose(1, 0, 2, 3)
+        .reshape(steps, own_count, -1)
+    )
     return (layer, next_out)
 
 

time: 449 us -> 463 us (1.031)
  waiting for transfers between devices: 255 us -> 107 us
  Pallas kernels: 0 us -> 134 us
  local copies, waits for them, and re-layouts: 54 us -> 73.3 us
  matrix products: 25.1 us -> 39.2 us
  other arithmetic: 34.5 us -> 27 us
    pallas_call x0 -> x3, Pallas kernels: none -> 134 us  [exchange(): pl.pallas_call(functools.partial(exchange_kernel, axis, n, gather), out_s...]
    all_gather x2 -> x0, waiting for transfers between devices: 86 us -> none  [the longest x1 43.9 us: shards(): lax.all_gather(joined, 'mlp', axis=1, tiled=True)]
    reduce_scatter x2 -> x0, waiting for transfers between devices: 73.2 us -> none  [the longest x1 73.2 us: shards(): lax.psum_scatter((jnp.dot(by_mlp(attended_all), dense_weight, preferred_e...]
    convert_element_type x1 -> x0, other arithmetic: 14.3 us -> none  [shards(): jax.nn.gelu(summed_all[:, triple_width:], approximate=False)]
    dot_general x3, matrix products: 9.92 us -> 24 us  [the longest x1 16.1 us: shards(): jnp.dot(activated_all, down_weight, preferred_element_type=jnp.float32)]
    slice x8 -> x6, local copies, waits for them, and re-layouts: 7.15 us -> 18.5 us  [the longest x2 10.5 us: shards(): summed_all[:, :triple_width]]
    unnamed x27 -> x48, local copies, waits for them, and re-layouts: 0.4 us -> 8.71 us
    unnamed x6 -> x4, waiting for transfers between devices: 0.1 us -> 7.39 us
  transfers between devices with their start and end apart: 6 -> 3, of which waited for: 5 -> 3; matrix products, arithmetic and copies ran while one was open for 12% -> 10% of each run, Pallas kernels for 0% -> 0%
where the time goes in v2:
time: 463 us; the launch traced here: 458 us
  Pallas kernels  134 us (29%)
  waiting for transfers between devices  107 us (23%)
  local copies, waits for them, and re-layouts  73.3 us (16%)
  blocking collectives  62.7 us (14%)
  matrix products  39.2 us (8%)
  other arithmetic  27 us (6%)
  between operations  14.8 us (3%)
    pallas_call x3, Pallas kernels, exchange(): pl.pallas_call(functools.partial(exchange_kernel, axis, n, gather), out_s...  134 us
    psum x1, waiting for transfers between devices, shards(): lax.psum(partial_sums.astype(jnp.bfloat16), 'req').astype(jnp.float32)  62.5 us
    reduce_scatter x1, waiting for transfers between devices, shards(): lax.psum_scatter(next_partial.astype(jnp.bfloat16), 'req', scatter_dimens...  36.7 us
    pmax x1, blocking collectives, shards(): global_top = lax.pmax(page_top, 'req')  25.2 us
    all_gather x2, blocking collectives, row_normalize(): stats = lax.all_gather(jnp.stack([local_mean, local_m2], axis=-1), 'req')  24.1 us
    dot_general x1, matrix products, shards(): jnp.dot(activated_all, down_weight, preferred_element_type=jnp.float32)  16.1 us
    all_gather x1, blocking collectives, shards(): attended_all = lax.all_gather(attended, 'req', axis=1, tiled=True)  13.5 us
    slice x2, local copies, waits for them, and re-layouts, shards(): summed_all[:, :triple_width]  10.5 us
  transfers between devices with their start and end apart: 3, of which 3 were waited for; matrix products, arithmetic and copies ran while one was open for 10% of the time, Pallas kernels for 0%

profile of v2, /device:TPU:0, one launch (start us, length us, event | category | flops | bytes accessed | tf_op | source)
XLA Modules:
  0.0 458.2 jit_solution(15611726108919034128)
XLA Ops:
  9.4 12.9 %all-gather = f32[16,48,2]{1,2,0:T(2,128)S(1)} all-gather(f32[2,48,2]{1,2,0:T(2,128)S(1)} %copy.230), channel_id=2, replica_groups=mesh['req'=8,'mlp'=16] {'req'}, dimensions={0}, use_global_device_ids=true | all-gather | bytes 6912 | tf_op jit(solution)/shard_map/all_gather | solution.py:86
  24.9 66.3 %shard_map.131 = bf16[16,2,48,1024]{3,2,1,0:T(8,128)(2,1)} custom-call(bf16[2,48,1024]{2,1,0:T(8,128)(2,1)} %pad_maximum_fusion.3.x_ref), custom_call_target="tpu_custom_call" | custom-call | tf_op jit(solution)/shard_map/pallas_call | solution.py:65
  91.2 3.4 convolution_convert_fusion
  96.1 2.7 pad_maximum_fusion
  99.4 4.8 %gather_fusion.1 = s32[768]{0:T(1024)S(1)} fusion(s32[96]{0:T(128)S(1)} %copy-done.2, s32[1024]{0:T(1024)S(1)} %pad_clamp_fusion.2), kind=kCustom, calls=%fused_computation.1 | custom fusion | bytes 9216 | tf_op jit(solution)/shard_map/gather | solution.py:122
  107.0 6.9 %reshape.449 = bf16[64,128,2,128]{3,2,1,0:T(2,128)(2,1)} reshape(bf16[64,128,256]{2,1,0:T(8,128)(2,1)} %param.19) | data formatting | bytes 8388608 | tf_op jit(solution)/shard_map/reshape | solution.py:133
  113.8 7.0 %reshape.450 = bf16[64,128,2,128]{3,2,1,0:T(2,128)(2,1)} reshape(bf16[64,128,256]{2,1,0:T(8,128)(2,1)} %param.20) | data formatting | bytes 8388608 | tf_op jit(solution)/shard_map/reshape | solution.py:134
  123.1 62.5 %all-reduce.2.cloned.1.call-done = bf16[1536,1792]{0,1:T(8,128)(2,1)} async-done(((bf16[1536,1792]{0,1:T(8,128)(2,1)}), bf16[1536,1792]{0,1:T(8,128)(2,1)}) %all-reduce.2.cloned.1.call-update) | async-done | bytes 5505040 | tf_op jit(solution)/shard_map/psum | solution.py:145
  185.5 4.4 slice.183
  190.0 6.1 %copy.231 = f32[1536,768]{1,0:T(8,128)} copy(f32[1536,768]{0,1:T(8,128)} %slice.183) | data formatting | bytes 9437184 | tf_op jit(solution)/shard_map/slice | solution.py:146
  196.0 8.1 %reshape.447 = f32[16,2,48,2,3,128]{5,4,3,2,1,0:T(4,128)} reshape(f32[1536,768]{1,0:T(8,128)} %copy.231) | data formatting | bytes 9437184 | tf_op jit(solution)/shard_map/reshape | solution.py:146
  204.1 3.9 slice.184
  208.2 2.2 fusion.141
  213.8 3.7 copy_multiply_fusion
  217.5 2.4 copy.239
  220.0 1.8 copy.298
  224.3 1.9 copy.339
  226.6 2.1 pad_maximum_fusion.2
  229.9 2.5 gather_fusion.2
  232.3 4.6 %fusion.144 = (f32[2,64,8,2]{2,0,3,1:T(2,128)S(1)}, f32[2,64,8,2,128]{4,2,0,3,1:T(8,128)S(1)}) fusion(bf16[64,128,2,128,1]{3,2,1,0,4:T(2,128)(2,1)} %bitcast.191, pred[64,128]{1,0:T(8,128)(4,1)S(1)} %fusion.80, bf16[512,2,2,128]{3,2,1,0:T(2,128)(2,1)S(1)} %gather_fusion.2), kind=kOutput, calls=%fused_computation.252 | convolution fusion | flops 67893248 | bytes 5783552 | tf_op jit(solution)/shard_map/zsbhd,sthd->zsbht/dot_general | solution.py:169
  238.1 25.2 %pmax.7 = f32[2,768,2]{1,2,0:T(2,128)S(1)} all-reduce(f32[2,768,2]{1,2,0:T(2,128)S(1)} %reshape.452), channel_id=1, replica_groups=mesh['req'=8,'mlp'=16] {'req'}, use_global_device_ids=true, to_apply=%region_8.9 | all-reduce | flops 3072 | bytes 24576 | tf_op jit(solution)/shard_map/pmax | solution.py:193
  265.1 3.6 fusion.32
  276.2 4.2 convert_element_type.72
  280.4 16.1 %fusion.14 = f32[1536,512]{1,0:T(8,128)} fusion(bf16[1024,512]{1,0:T(8,128)(2,1)S(1)} %copy-done.16, f32[1536,1792]{0,1:T(8,128)S(1)} %convert_element_type.72), kind=kOutput, calls=%fused_computation.35 | convolution fusion | flops 1712848896 | bytes 10485760 | tf_op jit(solution)/shard_map/dot_general | solution.py:243
  299.5 7.3 %reduce-scatter.7.cloned.1.call-done = bf16[96,516]{1,0:T(8,128)(2,1)} async-done(((bf16[768,516]{1,0:T(8,128)(2,1)}), bf16[96,516]{1,0:T(8,128)(2,1)}) %reduce-scatter.7.cloned.1.call-update) | async-done | bytes 99088
  309.6 13.5 %all_gather.17 = bf16[2,768,256]{2,1,0:T(8,128)(2,1)S(1)} all-gather(bf16[2,96,256]{2,1,0:T(8,128)(2,1)S(1)} %pad_maximum_fusion.7), channel_id=1, replica_groups=mesh['req'=8,'mlp'=16] {'req'}, dimensions={1}, use_global_device_ids=true | all-gather | bytes 884736 | tf_op jit(solution)/shard_map/all_gather | solution.py:235
  323.2 3.7 fusion.16
  326.9 32.2 %shard_map.132 = bf16[16,96,512]{2,1,0:T(8,128)(2,1)} custom-call(bf16[16,96,512]{2,1,0:T(8,128)(2,1)} %bitcast.189), custom_call_target="tpu_custom_call" | custom-call | tf_op jit(solution)/shard_map/pallas_call | solution.py:65
  361.0 11.2 %all-gather.1 = f32[16,48,2]{1,2,0:T(2,128)S(1)} all-gather(f32[2,48,2]{1,2,0:T(2,128)S(1)} %copy.271), channel_id=3, replica_groups=mesh['req'=8,'mlp'=16] {'req'}, dimensions={0}, use_global_device_ids=true | all-gather | bytes 6912 | tf_op jit(solution)/shard_map/all_gather | solution.py:86
  373.1 35.6 %shard_map.133 = bf16[16,2,48,512]{3,2,1,0:T(8,128)(2,1)} custom-call(bf16[2,48,512]{2,1,0:T(8,128)(2,1)} %fusion.51.x_ref), custom_call_target="tpu_custom_call" | custom-call | tf_op jit(solution)/shard_map/pallas_call | solution.py:65
  408.7 4.3 convolution_convert_fusion.1
  413.0 36.7 %reduce-scatter.5.cloned.1.call-done = bf16[192,768]{1,0:T(8,128)(2,1)} async-done(((bf16[1536,768]{1,0:T(8,128)(2,1)}), bf16[192,768]{1,0:T(8,128)(2,1)}) %reduce-scatter.5.cloned.1.call-update) | async-done | bytes 294928 | tf_op jit(solution)/shard_map/reduce_scatter | solution.py:259
  (162 shorter events, 39.6 us)
Async XLA Ops:
  7.2 84.0 %copy-start = (bf16[512,1024]{1,0:T(8,128)(2,1)S(1)}, bf16[512,1024]{1,0:T(8,128)(2,1)}, u32[]{:S(2)}) copy-start(bf16[512,1024]{1,0:T(8,128)(2,1)} %param.15) | copy-start | bytes 3145732
  7.2 178.4 %all-reduce.2.cloned.1.call-start = ((), (), s32[]{:S(2)}) async-start(), calls=%async_computation.2 | async-start | bytes 11010048 | tf_op jit(solution)/shard_map/psum | solution.py:145
  91.2 3.4 copy-start.3
  91.2 3.4 copy-start.17
  96.1 3.3 copy-start.2
  98.8 7.1 %copy-start.15 = (s32[2,64]{1,0:T(2,128)S(1)}, s32[2,64]{1,0:T(2,128)}, u32[]{:S(2)}) copy-start(s32[2,64]{1,0:T(2,128)} %param.22) | copy-start | bytes 1540
  98.9 208.0 %reduce-scatter.7.cloned.1.call-start = ((), (), s32[]{:S(2)}) async-start(), calls=%async_computation.4 | async-start | bytes 1105920
  106.1 16.2 %copy-start.13 = (s32[64]{0:T(128)}, s32[64]{0:T(128)S(1)}, u32[]{:S(2)}) copy-start(s32[64]{0:T(128)S(1)} %get-tuple-element.48) | copy-start | bytes 772
  106.2 14.7 %copy-start.12 = (s32[1024]{0:T(1024)}, s32[1024]{0:T(1024)S(1)}, u32[]{:S(2)}) copy-start(s32[1024]{0:T(1024)S(1)} %pad_clamp_fusion.3) | copy-start | bytes 12292
  113.8 7.1 %copy-start.19 = (s32[1,96]{1,0:T(1,128)S(1)}, s32[1,96]{1,0:T(1,128)}, u32[]{:S(2)}) copy-start(s32[1,96]{1,0:T(1,128)} %param.23) | copy-start | bytes 1156
  226.3 10.8 %copy-start.11 = (pred[64,96]{1,0:T(8,128)(4,1)S(1)}, pred[64,96]{1,0:T(8,128)(4,1)}, u32[]{:S(2)}) copy-start(pred[64,96]{1,0:T(8,128)(4,1)} %iota_compare_fusion.1) | copy-start | bytes 18436
  265.1 3.6 copy-start.14
  276.1 4.2 copy-start.16
  276.2 173.6 %reduce-scatter.5.cloned.1.call-start = ((), (), s32[]{:S(2)}) async-start(), calls=%async_computation.3 | async-start | bytes 2654208 | tf_op jit(solution)/shard_map/reduce_scatter | solution.py:259
  280.4 16.1 %copy-start.8 = (f32[2,96,32]{1,2,0:T(8,128)S(1)}, f32[2,96,32]{1,2,0:T(8,128)}, u32[]{:S(2)}) copy-start(f32[2,96,32]{1,2,0:T(8,128)} %get-tuple-element.58) | copy-start | bytes 73732
  280.4 16.1 %copy-start.9 = (f32[2,96,2,16]{1,3,2,0:T(8,128)S(1)}, f32[2,96,2,16]{1,3,2,0:T(8,128)}, u32[]{:S(2)}) copy-start(f32[2,96,2,16]{1,3,2,0:T(8,128)} %get-tuple-element.24) | copy-start | bytes 73732
  280.4 16.1 %copy-start.10 = (f32[2,96,2,16]{1,3,2,0:T(8,128)S(1)}, f32[2,96,2,16]{1,3,2,0:T(8,128)}, u32[]{:S(2)}) copy-start(f32[2,96,2,16]{1,3,2,0:T(8,128)} %get-tuple-element.25) | copy-start | bytes 73732
  280.4 17.7 %copy-start.6 = (bf16[2,96,2,3,128]{4,2,1,3,0:T(2,128)(2,1)S(1)}, bf16[2,96,2,3,128]{4,2,1,3,0:T(2,128)(2,1)}, u32[]{:S(2)}) copy-start(bf16[2,96,2,3,128]{4,2,1,3,0:T(2,128)(2,1)} %copy.340) | copy-start | bytes 884740
  296.5 26.7 %copy-start.7 = (bf16[256,512]{1,0:T(8,128)(2,1)S(1)}, bf16[256,512]{1,0:T(8,128)(2,1)}, u32[]{:S(2)}) copy-start(bf16[256,512]{1,0:T(8,128)(2,1)} %param.16) | copy-start | bytes 786436
  323.1 37.6 %copy-start.4 = (bf16[2,48,512]{2,1,0:T(8,128)(2,1)S(1)}, bf16[2,48,512]{2,1,0:T(8,128)(2,1)}, u32[]{:S(2)}) copy-start(bf16[2,48,512]{2,1,0:T(8,128)(2,1)} %param.12) | copy-start | bytes 294916
  323.2 85.5 %copy-start.18 = (bf16[512,768]{1,0:T(8,128)(2,1)S(1)}, bf16[512,768]{1,0:T(8,128)(2,1)}, u32[]{:S(2)}) copy-start(bf16[512,768]{1,0:T(8,128)(2,1)} %param.18) | copy-start | bytes 2359300
  360.8 52.2 %copy-start.5 = (bf16[2,48,512]{2,1,0:T(8,128)(2,1)}, bf16[2,48,512]{2,1,0:T(8,128)(2,1)S(1)}, u32[]{:S(2)}) copy-start(bf16[2,48,512]{2,1,0:T(8,128)(2,1)S(1)} %get-tuple-element.7) | copy-start | bytes 294916
  408.7 42.7 %copy-start.1 = (bf16[512,1024]{1,0:T(8,128)(2,1)S(1)}, bf16[512,1024]{1,0:T(8,128)(2,1)}, u32[]{:S(2)}) copy-start(bf16[512,1024]{1,0:T(8,128)(2,1)} %param.15) | copy-start | bytes 3145732
Sparse Core Ops, SparseCore 0:
  99.0 86.5 all-reduce.1
  276.3 30.5 reduce-scatter.6
  413.1 36.5 reduce-scatter.4

commit v3 on v2

--- a/solution.py
+++ b/solution.py
@@ -130,15 +130,13 @@
     owner_mask = slot_owner[:, None] == jnp.arange(request_count, dtype=jnp.int32)[None, :]
     owner_float = owner_mask.astype(jnp.float32)
     gather_rows = valid_owner[:, None] * BEAM + jnp.arange(BEAM, dtype=jnp.int32)[None, :]
-    page_keys = cache_keys.reshape(slot_count, PAGE, head_count, HD)
-    page_values = cache_values.reshape(slot_count, PAGE, head_count, HD)
 
     block = inputs.astype(jnp.float32)
-    normed = row_normalize(block)
+    rows_all = exchange(inputs, "mlp", mlp_size, True, 0).reshape(steps * beam_total, -1)
+    normed = row_normalize(rows_all.astype(jnp.float32))
     attn_in = (normed * norm_gains[0]).astype(jnp.bfloat16)
     mlp_in = (normed * norm_gains[1]).astype(jnp.bfloat16)
-    joined = jnp.concatenate([attn_in, mlp_in], axis=-1)
-    piece = exchange(joined, "mlp", mlp_size, True, 0).reshape(steps * beam_total, -1)
+    piece = jnp.concatenate([attn_in, mlp_in], axis=-1)
     first = jnp.dot(piece[:, :local_width], attn_weight, preferred_element_type=jnp.float32)
     second = jnp.dot(piece[:, local_width:], up_weight, preferred_element_type=jnp.float32)
     partial_sums = jnp.concatenate([first, second], axis=1)
@@ -165,19 +163,32 @@
     values_new = mixed_own[:, :, :, 2].astype(jnp.bfloat16)
 
     chosen = queries_all[:, gather_rows]
-    scores = (
-        jnp.einsum("zsbhd,sthd->zsbht", chosen, page_keys, preferred_element_type=jnp.float32)
-        * scale
-    )
+    head_scores = [
+        jnp.einsum(
+            "zsbd,std->zsbt",
+            chosen[:, :, :, head],
+            cache_keys[:, :, head * HD : (head + 1) * HD],
+            preferred_element_type=jnp.float32,
+        )
+        for head in range(head_count)
+    ]
+    scores = jnp.stack(head_scores, axis=3) * scale
     masked = jnp.where(live_wide, scores, NEG_FILL)
     slot_top = jnp.max(masked, axis=4)
     weights = jnp.where(live_wide, jnp.exp(masked - slot_top[..., None]), 0.0)
     slot_total = jnp.sum(weights, axis=4)
-    slot_out = jnp.einsum(
-        "zsbht,sthd->zsbhd",
-        weights.astype(jnp.bfloat16),
-        page_values,
-        preferred_element_type=jnp.float32,
+    rounded = weights.astype(jnp.bfloat16)
+    slot_out = jnp.stack(
+        [
+            jnp.einsum(
+                "zsbt,std->zsbd",
+                rounded[:, :, :, head],
+                cache_values[:, :, head * HD : (head + 1) * HD],
+                preferred_element_type=jnp.float32,
+            )
+            for head in range(head_count)
+        ],
+        axis=3,
     )
     request_top = jnp.max(
         jnp.where(owner_mask[None, :, :, None, None], slot_top[:, :, None], NEG_FILL), axis=1

time: 463 us -> 424 us (0.916)
  Pallas kernels: 134 us -> 95.6 us
  local copies, waits for them, and re-layouts: 73.3 us -> 59 us
  waiting for transfers between devices: 107 us -> 118 us
    pallas_call x3, Pallas kernels: 134 us -> 95.6 us  [exchange(): pl.pallas_call(functools.partial(exchange_kernel, axis, n, gather), out_s...]
    reshape x3 -> x1, local copies, waits for them, and re-layouts: 14 us -> 0.11 us  [the longest x1 7.01 us: shards(): page_values = cache_values.reshape(slot_count, PAGE, head_count, HD)]
    psum x1, waiting for transfers between devices: 62.5 us -> 73.5 us  [shards(): lax.psum(partial_sums.astype(jnp.bfloat16), 'req').astype(jnp.float32)]
  transfers between devices with their start and end apart: 3 -> 3, of which waited for: 3 -> 3; matrix products, arithmetic and copies ran while one was open for 10% -> 8% of each run, Pallas kernels for 0% -> 0%
where the time goes in v3:
time: 424 us; the launch traced here: 418 us
  waiting for transfers between devices  118 us (28%)
  Pallas kernels  95.6 us (23%)
  blocking collectives  63.8 us (15%)
  local copies, waits for them, and re-layouts  59 us (14%)
  matrix products  37.8 us (9%)
  other arithmetic  28.4 us (7%)
  between operations  14.8 us (3%)
    pallas_call x3, Pallas kernels, exchange(): pl.pallas_call(functools.partial(exchange_kernel, axis, n, gather), out_s...  95.6 us
    psum x1, waiting for transfers between devices, shards(): lax.psum(partial_sums.astype(jnp.bfloat16), 'req').astype(jnp.float32)  73.5 us
    reduce_scatter x1, waiting for transfers between devices, shards(): lax.psum_scatter(next_partial.astype(jnp.bfloat16), 'req', scatter_dimens...  36.7 us
    all_gather x2, blocking collectives, row_normalize(): stats = lax.all_gather(jnp.stack([local_mean, local_m2], axis=-1), 'req')  25.2 us
    pmax x1, blocking collectives, shards(): global_top = lax.pmax(page_top, 'req')  25.2 us
    dot_general x1, matrix products, shards(): jnp.dot(activated_all, down_weight, preferred_element_type=jnp.float32)  16.1 us
    all_gather x1, blocking collectives, shards(): attended_all = lax.all_gather(attended, 'req', axis=1, tiled=True)  13.5 us
    slice x2, local copies, waits for them, and re-layouts, shards(): summed_all[:, :triple_width]  10.5 us
  transfers between devices with their start and end apart: 3, of which 3 were waited for; matrix products, arithmetic and copies ran while one was open for 8% of the time, Pallas kernels for 0%

profile of v3, /device:TPU:0, one launch (start us, length us, event | category | flops | bytes accessed | tf_op | source)
XLA Modules:
  0.0 417.8 jit_solution(8026796613952557153)
XLA Ops:
  7.2 29.2 %shard_map.131 = bf16[16,2,48,512]{3,2,1,0:T(8,128)(2,1)} custom-call(bf16[2,48,512]{2,1,0:T(8,128)(2,1)} %x_ref.1), custom_call_target="tpu_custom_call" | custom-call | tf_op jit(solution)/shard_map/pallas_call | solution.py:65
  38.3 2.1 multiply_reduce_fusion
  40.7 13.9 %all-gather = f32[12288,2]{0,1:T(2,128)S(1)} all-gather(f32[1536,2]{0,1:T(2,128)S(1)} %pad_maximum_fusion.9), channel_id=2, replica_groups=mesh['req'=8,'mlp'=16] {'req'}, dimensions={0}, use_global_device_ids=true | all-gather | bytes 110592 | tf_op jit(solution)/shard_map/all_gather | solution.py:86
  56.4 1.8 convolution_convert_fusion
  59.7 2.7 pad_maximum_fusion
  63.1 4.8 %gather_fusion.1 = s32[768]{0:T(1024)S(1)} fusion(s32[96]{0:T(128)S(1)} %copy-done.2, s32[1024]{0:T(1024)S(1)} %pad_clamp_fusion.2), kind=kCustom, calls=%fused_computation.1 | custom fusion | bytes 9216 | tf_op jit(solution)/shard_map/gather | solution.py:122
  71.6 73.5 %all-reduce.2.cloned.1.call-done = bf16[1536,1792]{0,1:T(8,128)(2,1)} async-done(((bf16[1536,1792]{0,1:T(8,128)(2,1)}), bf16[1536,1792]{0,1:T(8,128)(2,1)}) %all-reduce.2.cloned.1.call-update) | async-done | bytes 5505040 | tf_op jit(solution)/shard_map/psum | solution.py:143
  145.1 4.4 %slice.205 = f32[1536,768]{0,1:T(8,128)} slice(bf16[1536,1792]{0,1:T(8,128)(2,1)} %all-reduce.2.cloned.1.call-done), slice={[0:1536], [0:768]} | slice | bytes 9437184 | tf_op jit(solution)/shard_map/slice | solution.py:144
  149.5 6.1 %copy.218 = f32[1536,768]{1,0:T(8,128)} copy(f32[1536,768]{0,1:T(8,128)} %slice.205) | data formatting | bytes 9437184 | tf_op jit(solution)/shard_map/slice | solution.py:144
  155.6 8.1 %reshape.450 = f32[16,2,48,2,3,128]{5,4,3,2,1,0:T(4,128)} reshape(f32[1536,768]{1,0:T(8,128)} %copy.218) | data formatting | bytes 9437184 | tf_op jit(solution)/shard_map/reshape | solution.py:144
  163.7 3.9 slice.206
  167.8 2.2 fusion.133
  174.0 3.7 copy_multiply_fusion
  177.7 2.5 copy.226
  180.2 1.8 copy.283
  182.1 1.8 copy.223
  186.3 2.1 pad_maximum_fusion.2
  188.4 2.5 gather_fusion.2
  191.0 2.8 fusion.27
  193.7 2.8 fusion.30
  199.8 2.7 fusion.33
  203.5 25.2 %pmax.7 = f32[2,768,2]{1,2,0:T(2,128)S(1)} all-reduce(f32[2,768,2]{1,2,0:T(2,128)S(1)} %reshape.453), channel_id=1, replica_groups=mesh['req'=8,'mlp'=16] {'req'}, use_global_device_ids=true, to_apply=%region_8.9 | all-reduce | flops 3072 | bytes 24576 | tf_op jit(solution)/shard_map/pmax | solution.py:204
  237.2 4.2 convert_element_type.85
  241.4 16.1 %fusion.11 = f32[1536,512]{1,0:T(8,128)} fusion(bf16[1024,512]{1,0:T(8,128)(2,1)S(1)} %copy-done.20, f32[1536,1792]{0,1:T(8,128)S(1)} %convert_element_type.85), kind=kOutput, calls=%fused_computation.36 | convolution fusion | flops 1712848896 | bytes 10485760 | tf_op jit(solution)/shard_map/dot_general | solution.py:254
  260.4 7.5 %reduce-scatter.7.cloned.1.call-done = bf16[96,516]{1,0:T(8,128)(2,1)} async-done(((bf16[768,516]{1,0:T(8,128)(2,1)}), bf16[96,516]{1,0:T(8,128)(2,1)}) %reduce-scatter.7.cloned.1.call-update) | async-done | bytes 99088
  270.7 13.5 %all_gather.17 = bf16[2,768,256]{2,1,0:T(8,128)(2,1)S(1)} all-gather(bf16[2,96,256]{2,1,0:T(8,128)(2,1)S(1)} %pad_maximum_fusion.6), channel_id=1, replica_groups=mesh['req'=8,'mlp'=16] {'req'}, dimensions={1}, use_global_device_ids=true | all-gather | bytes 884736 | tf_op jit(solution)/shard_map/all_gather | solution.py:246
  284.3 3.6 fusion.13
  287.9 32.9 %shard_map.132 = bf16[16,96,512]{2,1,0:T(8,128)(2,1)} custom-call(bf16[16,96,512]{2,1,0:T(8,128)(2,1)} %bitcast.251), custom_call_target="tpu_custom_call" | custom-call | tf_op jit(solution)/shard_map/pallas_call | solution.py:65
  322.7 11.2 %all-gather.1 = f32[16,48,2]{1,2,0:T(2,128)S(1)} all-gather(f32[2,48,2]{1,2,0:T(2,128)S(1)} %copy.256), channel_id=3, replica_groups=mesh['req'=8,'mlp'=16] {'req'}, dimensions={0}, use_global_device_ids=true | all-gather | bytes 6912 | tf_op jit(solution)/shard_map/all_gather | solution.py:86
  334.8 33.5 %shard_map.133 = bf16[16,2,48,512]{3,2,1,0:T(8,128)(2,1)} custom-call(bf16[2,48,512]{2,1,0:T(8,128)(2,1)} %fusion.52.x_ref), custom_call_target="tpu_custom_call" | custom-call | tf_op jit(solution)/shard_map/pallas_call | solution.py:65
  368.3 4.3 %convolution_convert_fusion.1 = bf16[1536,768]{1,0:T(8,128)(2,1)} fusion(bf16[1536,512]{1,0:T(8,128)(2,1)} %bitcast.259, bf16[512,768]{1,0:T(8,128)(2,1)S(1)} %copy-done.22), kind=kOutput, calls=%fused_computation.27 | convolution fusion | flops 1209139200 | bytes 4718592 | tf_op jit(solution)/shard_map/dot_general | solution.py:269
  372.6 36.7 %reduce-scatter.5.cloned.1.call-done = bf16[192,768]{1,0:T(8,128)(2,1)} async-done(((bf16[1536,768]{1,0:T(8,128)(2,1)}), bf16[192,768]{1,0:T(8,128)(2,1)}) %reduce-scatter.5.cloned.1.call-update) | async-done | bytes 294928 | tf_op jit(solution)/shard_map/reduce_scatter | solution.py:270
  (174 shorter events, 38.9 us)
Async XLA Ops:
  7.2 49.2 %copy-start = (bf16[512,1024]{1,0:T(8,128)(2,1)S(1)}, bf16[512,1024]{1,0:T(8,128)(2,1)}, u32[]{:S(2)}) copy-start(bf16[512,1024]{1,0:T(8,128)(2,1)} %param.15) | copy-start | bytes 3145732
  7.2 47.5 %copy-start.16 = (f32[3,512]{1,0:T(4,128)S(1)}, f32[3,512]{1,0:T(4,128)}, u32[]{:S(2)}) copy-start(f32[3,512]{1,0:T(4,128)} %param.13) | copy-start | bytes 18436
  7.2 137.9 %all-reduce.2.cloned.1.call-start = ((), (), s32[]{:S(2)}) async-start(), calls=%async_computation.2 | async-start | bytes 11010048 | tf_op jit(solution)/shard_map/psum | solution.py:143
  36.5 18.9 %copy-start.3 = (bf16[16,2,48,512]{3,2,1,0:T(8,128)(2,1)S(1)}, bf16[16,2,48,512]{3,2,1,0:T(8,128)(2,1)}, u32[]{:S(2)}) copy-start(bf16[16,2,48,512]{3,2,1,0:T(8,128)(2,1)} %shard_map.131) | copy-start | bytes 4718596
  56.4 1.9 copy-start.21
  62.4 0.7 copy-start.2
  62.4 7.1 %copy-start.19 = (s32[2,64]{1,0:T(2,128)S(1)}, s32[2,64]{1,0:T(2,128)}, u32[]{:S(2)}) copy-start(s32[2,64]{1,0:T(2,128)} %param.22) | copy-start | bytes 1540
  62.4 8.2 %copy-start.23 = (s32[1,96]{1,0:T(1,128)S(1)}, s32[1,96]{1,0:T(1,128)}, u32[]{:S(2)}) copy-start(s32[1,96]{1,0:T(1,128)} %param.23) | copy-start | bytes 1156
  62.4 205.5 %reduce-scatter.7.cloned.1.call-start = ((), (), s32[]{:S(2)}) async-start(), calls=%async_computation.4 | async-start | bytes 1105920
  69.7 1.8 copy-start.17
  69.8 79.8 %copy-start.15 = (s32[1024]{0:T(1024)}, s32[1024]{0:T(1024)S(1)}, u32[]{:S(2)}) copy-start(s32[1024]{0:T(1024)S(1)} %pad_clamp_fusion.3) | copy-start | bytes 12292
  177.7 6.9 %copy-start.5 = (bf16[2,768,2,96]{3,1,2,0:T(8,128)(2,1)S(1)}, bf16[2,768,2,96]{3,1,2,0:T(8,128)(2,1)}, u32[]{:S(2)}) copy-start(bf16[2,768,2,96]{3,1,2,0:T(8,128)(2,1)} %slice.210) | copy-start | bytes 1769476
  197.7 5.4 %copy-start.10 = (bf16[2,96,2,128]{3,2,1,0:T(2,128)(2,1)S(1)}, bf16[2,96,2,128]{3,2,1,0:T(2,128)(2,1)}, u32[]{:S(2)}) copy-start(bf16[2,96,2,128]{3,2,1,0:T(2,128)(2,1)} %fusion.56) | copy-start | bytes 294916
  199.0 3.5 copy-start.4
  199.8 30.2 %copy-start.18 = (s32[64]{0:T(128)S(1)}, s32[64]{0:T(128)}, u32[]{:S(2)}) copy-start(s32[64]{0:T(128)} %copy-done.17) | copy-start | bytes 772
  237.1 4.2 %copy-start.20 = (bf16[1024,512]{1,0:T(8,128)(2,1)S(1)}, bf16[1024,512]{1,0:T(8,128)(2,1)}, u32[]{:S(2)}) copy-start(bf16[1024,512]{1,0:T(8,128)(2,1)} %param.17) | copy-start | bytes 3145732
  237.1 172.3 %reduce-scatter.5.cloned.1.call-start = ((), (), s32[]{:S(2)}) async-start(), calls=%async_computation.3 | async-start | bytes 2654208 | tf_op jit(solution)/shard_map/reduce_scatter | solution.py:270
  241.4 16.1 %copy-start.12 = (f32[2,96,2,16]{1,3,2,0:T(8,128)S(1)}, f32[2,96,2,16]{1,3,2,0:T(8,128)}, u32[]{:S(2)}) copy-start(f32[2,96,2,16]{1,3,2,0:T(8,128)} %get-tuple-element.28) | copy-start | bytes 73732
  241.4 16.1 %copy-start.13 = (f32[2,96,2,16]{1,3,2,0:T(8,128)S(1)}, f32[2,96,2,16]{1,3,2,0:T(8,128)}, u32[]{:S(2)}) copy-start(f32[2,96,2,16]{1,3,2,0:T(8,128)} %get-tuple-element.29) | copy-start | bytes 73732
  241.4 16.1 %copy-start.7 = (bf16[2,96,2,96]{1,3,2,0:T(8,128)(2,1)S(1)}, bf16[2,96,2,96]{1,3,2,0:T(8,128)(2,1)}, u32[]{:S(2)}) copy-start(bf16[2,96,2,96]{1,3,2,0:T(8,128)(2,1)} %slice.322) | copy-start | bytes 221188
  241.4 17.7 %copy-start.8 = (bf16[2,96,2,3,128]{4,2,1,3,0:T(2,128)(2,1)S(1)}, bf16[2,96,2,3,128]{4,2,1,3,0:T(2,128)(2,1)}, u32[]{:S(2)}) copy-start(bf16[2,96,2,3,128]{4,2,1,3,0:T(2,128)(2,1)} %copy.311) | copy-start | bytes 884740
  257.4 26.8 %copy-start.11 = (bf16[256,512]{1,0:T(8,128)(2,1)S(1)}, bf16[256,512]{1,0:T(8,128)(2,1)}, u32[]{:S(2)}) copy-start(bf16[256,512]{1,0:T(8,128)(2,1)} %param.16) | copy-start | bytes 786436
  284.2 38.2 %copy-start.9 = (bf16[2,48,512]{2,1,0:T(8,128)(2,1)S(1)}, bf16[2,48,512]{2,1,0:T(8,128)(2,1)}, u32[]{:S(2)}) copy-start(bf16[2,48,512]{2,1,0:T(8,128)(2,1)} %x_ref.1) | copy-start | bytes 294916
  284.3 49.8 %copy-start.14 = (f32[1,512]{1,0:T(1,128)S(1)}, f32[1,512]{1,0:T(1,128)}, u32[]{:S(2)}) copy-start(f32[1,512]{1,0:T(1,128)} %get-tuple-element.36) | copy-start | bytes 6148
  287.9 80.4 %copy-start.22 = (bf16[512,768]{1,0:T(8,128)(2,1)S(1)}, bf16[512,768]{1,0:T(8,128)(2,1)}, u32[]{:S(2)}) copy-start(bf16[512,768]{1,0:T(8,128)(2,1)} %param.18) | copy-start | bytes 2359300
  322.5 50.1 %copy-start.6 = (bf16[2,48,512]{2,1,0:T(8,128)(2,1)}, bf16[2,48,512]{2,1,0:T(8,128)(2,1)S(1)}, u32[]{:S(2)}) copy-start(bf16[2,48,512]{2,1,0:T(8,128)(2,1)S(1)} %get-tuple-element.7) | copy-start | bytes 294916
  368.3 42.8 %copy-start.1 = (bf16[512,1024]{1,0:T(8,128)(2,1)S(1)}, bf16[512,1024]{1,0:T(8,128)(2,1)}, u32[]{:S(2)}) copy-start(bf16[512,1024]{1,0:T(8,128)(2,1)} %param.15) | copy-start | bytes 3145732
Sparse Core Ops, SparseCore 0:
  62.6 82.4 all-reduce.1
  237.2 30.6 reduce-scatter.6
  372.8 36.5 reduce-scatter.4

commit v4 on v3

--- a/solution.py
+++ b/solution.py
@@ -78,12 +78,26 @@
     )(x)
 
 
-def row_normalize(values):
+def exchange_flat(x, axis, n, gather, collective_id):
+    lead = () if gather else x.shape[:1]
+    block_shape = x.shape if gather else x.shape[1:]
+    size = math.prod(block_shape)
+    padded = -(-size // 128) * 128
+    flat = x.reshape(lead + (size,))
+    flat = jnp.pad(flat, [(0, 0)] * len(lead) + [(0, padded - size)])
+    flat = flat.reshape(lead + (padded // 128, 128))
+    out = exchange(flat, axis, n, gather, collective_id)
+    return out.reshape(n, padded)[:, :size].reshape((n,) + block_shape)
+
+
+def row_normalize(values, collective_id):
     width = values.shape[-1]
     local_mean = jnp.mean(values, axis=-1)
     centred = values - local_mean[..., None]
     local_m2 = jnp.sum(centred * centred, axis=-1)
-    stats = lax.all_gather(jnp.stack([local_mean, local_m2], axis=-1), "req")
+    stats = jnp.stack([local_mean, local_m2], axis=0)
+    stats = exchange_flat(stats, "req", lax.axis_size("req"), True, collective_id)
+    stats = jnp.moveaxis(stats, 1, -1)
     means = stats[..., 0]
     row_mean = jnp.mean(means, axis=0)
     spread = means - row_mean
@@ -133,7 +147,7 @@
 
     block = inputs.astype(jnp.float32)
     rows_all = exchange(inputs, "mlp", mlp_size, True, 0).reshape(steps * beam_total, -1)
-    normed = row_normalize(rows_all.astype(jnp.float32))
+    normed = row_normalize(rows_all.astype(jnp.float32), 3)
     attn_in = (normed * norm_gains[0]).astype(jnp.bfloat16)
     mlp_in = (normed * norm_gains[1]).astype(jnp.bfloat16)
     piece = jnp.concatenate([attn_in, mlp_in], axis=-1)
@@ -193,25 +207,38 @@
     request_top = jnp.max(
         jnp.where(owner_mask[None, :, :, None, None], slot_top[:, :, None], NEG_FILL), axis=1
     )
-    factor = jnp.exp(slot_top - request_top[:, valid_owner])
+    top_high = request_top.astype(jnp.bfloat16)
+    top_low = (request_top - top_high.astype(jnp.float32)).astype(jnp.bfloat16)
+    request_top = top_high.astype(jnp.float32) + top_low.astype(jnp.float32)
+    factor = jnp.where(
+        slot_owner[None, :, None, None] >= 0,
+        jnp.exp(slot_top - request_top[:, valid_owner]),
+        0.0,
+    )
     page_total = jnp.einsum(
         "sr,zsbh->zrbh", owner_float, slot_total * factor, precision=highest
     ).reshape(steps, beam_total, head_count)
     page_out = jnp.einsum(
         "sr,zsbhd->zrbhd", owner_float, slot_out * factor[..., None], precision=highest
     ).reshape(steps, beam_total, head_count, HD)
-    page_top = request_top.reshape(steps, beam_total, head_count)
-    global_top = lax.pmax(page_top, "req")
-    rescale = jnp.exp(page_top - global_top)
-    partial = jnp.concatenate(
-        [page_out * rescale[..., None], (page_total * rescale)[..., None]], axis=-1
-    )
-    own_partial = lax.psum_scatter(
-        partial.astype(jnp.bfloat16), "req", scatter_dimension=1, tiled=True
-    ).astype(jnp.float32)
-    own_top = lax.dynamic_slice_in_dim(global_top, offset, own_count, 1)
-    own_out = own_partial[..., :HD]
-    own_total = own_partial[..., HD]
+    packed = jnp.concatenate(
+        [
+            page_out.astype(jnp.bfloat16),
+            page_total.astype(jnp.bfloat16)[..., None],
+            top_high.reshape(steps, beam_total, head_count, 1),
+            top_low.reshape(steps, beam_total, head_count, 1),
+        ],
+        axis=-1,
+    )
+    packed = packed.reshape(steps, req_size, own_count, head_count, HD + 3).transpose(
+        1, 0, 2, 3, 4
+    )
+    held = exchange_flat(packed, "req", req_size, False, 5).astype(jnp.float32)
+    held_top = held[..., HD + 1] + held[..., HD + 2]
+    own_top = jnp.max(held_top, axis=0)
+    rescale = jnp.exp(held_top - own_top)
+    own_out = jnp.sum(held[..., :HD] * rescale[..., None], axis=0)
+    own_total = jnp.sum(held[..., HD] * rescale, axis=0)
 
     source = own_group * BEAM + parents[0]
     attended_steps = []
@@ -243,10 +270,10 @@
             (summed / total[..., None]).astype(jnp.bfloat16).reshape(own_count, head_count * HD)
         )
     attended = jnp.stack(attended_steps)
-    attended_all = lax.all_gather(attended, "req", axis=1, tiled=True)
+    attended_all = exchange(attended, "req", req_size, True, 6)
     attended_msi = (
-        attended_all.reshape(steps, mlp_size, local_rows, -1)
-        .transpose(1, 0, 2, 3)
+        attended_all.reshape(req_size, steps, per_own, local_rows, -1)
+        .transpose(0, 2, 1, 3, 4)
         .reshape(steps * beam_total, -1)
     )
     update_partial = (
@@ -264,7 +291,7 @@
         axis=0,
     )
     layer = (block + update.reshape(steps, local_rows, local_width)).astype(jnp.bfloat16)
-    next_in = (row_normalize(layer.astype(jnp.float32)) * norm_gains[2]).astype(jnp.bfloat16)
+    next_in = (row_normalize(layer.astype(jnp.float32), 4) * norm_gains[2]).astype(jnp.bfloat16)
     gathered = exchange(next_in, "mlp", mlp_size, True, 2).reshape(steps * beam_total, -1)
     next_partial = jnp.dot(gathered, next_weight, preferred_element_type=jnp.float32)
     next_out = lax.psum_scatter(

time: 424 us -> 427 us (level)
  blocking collectives: 63.8 us -> 0 us
  Pallas kernels: 95.6 us -> 141 us
  local copies, waits for them, and re-layouts: 59 us -> 85 us
  waiting for transfers between devices: 118 us -> 107 us
  other arithmetic: 28.4 us -> 36.4 us
    pallas_call x3 -> x7, Pallas kernels: 95.6 us -> 141 us  [exchange(): pl.pallas_call(functools.partial(exchange_kernel, axis, n, gather), out_s...]
    all_gather x3 -> x0, blocking collectives: 38.7 us -> none  [the longest x2 25.2 us: row_normalize(): stats = lax.all_gather(jnp.stack([local_mean, local_m2], axis=-1), 'req')]
    pmax x1 -> x0, blocking collectives: 25.2 us -> none  [shards(): global_top = lax.pmax(page_top, 'req')]
    convert_element_type x0 -> x6, local copies, waits for them, and re-layouts: none -> 8.6 us  [the longest x1 6.55 us: shards(): held = exchange_flat(packed, 'req', req_size, False, 5).astype(jnp.float32)]
    unnamed x4 -> x2, waiting for transfers between devices: 7.5 us -> 0.03 us
    slice x0 -> x3, local copies, waits for them, and re-layouts: none -> 7.31 us  [the longest x2 6.73 us: shards(): own_total = jnp.sum(held[..., HD] * rescale, axis=0)]
    reshape x4 -> x6, local copies, waits for them, and re-layouts: 0.45 us -> 6.49 us  [the longest x3 5.12 us: exchange_flat(): flat = flat.reshape(lead + (padded // 128, 128))]
    unnamed x57 -> x70, local copies, waits for them, and re-layouts: 7.67 us -> 10.7 us
  transfers between devices with their start and end apart: 3 -> 2, of which waited for: 3 -> 2; matrix products, arithmetic and copies ran while one was open for 8% -> 2% of each run, Pallas kernels for 0% -> 0%
where the time goes in v4:
time: 427 us; the launch traced here: 421 us
  Pallas kernels  141 us (33%)
  waiting for transfers between devices  107 us (25%)
  local copies, waits for them, and re-layouts  85 us (20%)
  other arithmetic  36.4 us (9%)
  matrix products  35.1 us (8%)
  between operations  15.2 us (4%)
    pallas_call x7, Pallas kernels, exchange(): pl.pallas_call(functools.partial(exchange_kernel, axis, n, gather), out_s...  141 us
    psum x1, waiting for transfers between devices, shards(): lax.psum(partial_sums.astype(jnp.bfloat16), 'req').astype(jnp.float32)  71.5 us
    reduce_scatter x1, waiting for transfers between devices, shards(): lax.psum_scatter(next_partial.astype(jnp.bfloat16), 'req', scatter_dimens...  35.8 us
    dot_general x1, matrix products, shards(): jnp.dot(activated_all, down_weight, preferred_element_type=jnp.float32)  14.4 us
    unnamed x70, local copies, waits for them, and re-layouts  10.7 us
    slice x2, local copies, waits for them, and re-layouts, shards(): summed_all[:, :triple_width]  10.5 us
  transfers between devices with their start and end apart: 2, of which 2 were waited for; matrix products, arithmetic and copies ran while one was open for 2% of the time, Pallas kernels for 0%

profile of v4, /device:TPU:0, one launch (start us, length us, event | category | flops | bytes accessed | tf_op | source)
XLA Modules:
  0.0 420.7 jit_solution(13504630913612138136)
XLA Ops:
  7.2 29.2 %shard_map.131 = bf16[16,2,48,512]{3,2,1,0:T(8,128)(2,1)} custom-call(bf16[2,48,512]{2,1,0:T(8,128)(2,1)} %x_ref.1), custom_call_target="tpu_custom_call" | custom-call | tf_op jit(solution)/shard_map/pallas_call | solution.py:65
  36.5 1.8 convert_reduce_fusion.1
  38.3 2.1 multiply_reduce_fusion
  41.3 8.9 %shard_map.132 = f32[8,24,128]{2,1,0:T(8,128)} custom-call(f32[24,128]{1,0:T(8,128)} %reshape.532.x_ref), custom_call_target="tpu_custom_call" | custom-call | tf_op jit(solution)/shard_map/pallas_call | solution.py:65
  53.0 1.8 convolution_convert_fusion
  56.3 2.7 pad_maximum_fusion
  59.7 4.8 %gather_fusion.1 = s32[768]{0:T(1024)S(1)} fusion(s32[96]{0:T(128)S(1)} %copy-done.2, s32[1024]{0:T(1024)S(1)} %pad_clamp_fusion.2), kind=kCustom, calls=%fused_computation.1 | custom fusion | bytes 9216 | tf_op jit(solution)/shard_map/gather | solution.py:136
  69.5 71.5 %all-reduce.3.cloned.1.call-done = bf16[1536,1792]{0,1:T(8,128)(2,1)} async-done(((bf16[1536,1792]{0,1:T(8,128)(2,1)}), bf16[1536,1792]{0,1:T(8,128)(2,1)}) %all-reduce.3.cloned.1.call-update) | async-done | bytes 5505040 | tf_op jit(solution)/shard_map/psum | solution.py:157
  141.0 4.4 %slice.217 = f32[1536,768]{0,1:T(8,128)} slice(bf16[1536,1792]{0,1:T(8,128)(2,1)} %all-reduce.3.cloned.1.call-done), slice={[0:1536], [0:768]} | slice | bytes 9437184 | tf_op jit(solution)/shard_map/slice | solution.py:158
  145.4 6.1 %copy.252 = f32[1536,768]{1,0:T(8,128)} copy(f32[1536,768]{0,1:T(8,128)} %slice.217) | data formatting | bytes 9437184 | tf_op jit(solution)/shard_map/slice | solution.py:158
  151.5 8.1 %reshape.533 = f32[16,2,48,2,3,128]{5,4,3,2,1,0:T(4,128)} reshape(f32[1536,768]{1,0:T(8,128)} %copy.252) | data formatting | bytes 9437184 | tf_op jit(solution)/shard_map/reshape | solution.py:158
  167.5 3.7 copy_multiply_fusion
  171.2 2.5 copy.260
  173.7 1.8 copy.324
  178.7 2.1 pad_maximum_fusion.1
  180.8 2.5 gather_fusion.2
  183.4 2.8 fusion.28
  186.2 2.8 fusion.31
  190.5 2.6 fusion.34
  205.1 3.9 reshape.535.x_ref
  209.0 13.9 %shard_map.133 = bf16[8,393,128]{2,1,0:T(8,128)(2,1)} custom-call(bf16[8,393,128]{2,1,0:T(8,128)(2,1)} %reshape.535.x_ref), custom_call_target="tpu_custom_call" | custom-call | tf_op jit(solution)/shard_map/pallas_call | solution.py:65
  222.9 6.6 %reshape.551 = f32[8,2,96,2,131]{4,3,2,1,0:T(2,128)S(1)} reshape(bf16[8,393,128]{2,1,0:T(8,128)(2,1)} %shard_map.133) | data formatting | bytes 2414592 | tf_op jit(solution)/shard_map/convert_element_type | solution.py:236
  229.5 5.0 %fusion.140 = (f32[8,2,96,2,1]{4,3,2,1,0:T(2,128)}, f32[8,2,96,2,1]{4,3,2,1,0:T(2,128)}, f32[8,2,96,2,1]{4,3,2,1,0:T(2,128)}) fusion(f32[8,2,96,2,131]{4,3,2,1,0:T(2,128)S(1)} %reshape.551), kind=kLoop, calls=%fused_computation.263 | loop fusion | bytes 73728 | tf_op jit(solution)/shard_map/slice | solution.py:241
  248.0 3.5 fusion.26
  256.6 14.7 %shard_map.134 = bf16[8,2,96,256]{3,2,1,0:T(8,128)(2,1)} custom-call(bf16[2,96,256]{2,1,0:T(8,128)(2,1)} %pad_maximum_fusion.5.x_ref), custom_call_target="tpu_custom_call" | custom-call | tf_op jit(solution)/shard_map/pallas_call | solution.py:65
  272.5 4.2 convert_element_type.164
  276.7 14.4 %fusion.11 = f32[1536,512]{1,0:T(8,128)S(1)} fusion(bf16[1024,512]{1,0:T(8,128)(2,1)S(1)} %copy-done.24, f32[1536,1792]{0,1:T(8,128)S(1)} %convert_element_type.164), kind=kOutput, calls=%fused_computation.36 | convolution fusion | flops 1712848896 | bytes 10485760 | tf_op jit(solution)/shard_map/dot_general | solution.py:281
  292.9 33.5 %shard_map.135 = bf16[16,96,512]{2,1,0:T(8,128)(2,1)} custom-call(bf16[16,96,512]{2,1,0:T(8,128)(2,1)} %bitcast.270), custom_call_target="tpu_custom_call" | custom-call | tf_op jit(solution)/shard_map/pallas_call | solution.py:65
  329.0 6.7 %shard_map.136 = f32[8,2,128]{2,1,0:T(2,128)} custom-call(f32[2,128]{1,0:T(2,128)} %pad_bitcast_fusion.x_ref), custom_call_target="tpu_custom_call" | custom-call | tf_op jit(solution)/shard_map/pallas_call | solution.py:65
  337.2 34.5 %shard_map.137 = bf16[16,2,48,512]{3,2,1,0:T(8,128)(2,1)} custom-call(bf16[2,48,512]{2,1,0:T(8,128)(2,1)} %fusion.54.x_ref), custom_call_target="tpu_custom_call" | custom-call | tf_op jit(solution)/shard_map/pallas_call | solution.py:65
  371.8 4.3 %convolution_convert_fusion.1 = bf16[1536,768]{1,0:T(8,128)(2,1)} fusion(bf16[1536,512]{1,0:T(8,128)(2,1)} %bitcast.279, bf16[512,768]{1,0:T(8,128)(2,1)S(1)} %copy-done.26), kind=kOutput, calls=%fused_computation.27 | convolution fusion | flops 1209139200 | bytes 4718592 | tf_op jit(solution)/shard_map/dot_general | solution.py:296
  376.1 35.8 %reduce-scatter.2.cloned.1.call-done = bf16[192,768]{1,0:T(8,128)(2,1)} async-done(((bf16[1536,768]{1,0:T(8,128)(2,1)}), bf16[192,768]{1,0:T(8,128)(2,1)}) %reduce-scatter.2.cloned.1.call-update) | async-done | bytes 294928 | tf_op jit(solution)/shard_map/reduce_scatter | solution.py:297
  (199 shorter events, 62.3 us)
Async XLA Ops:
  7.2 45.8 %copy-start = (bf16[512,1024]{1,0:T(8,128)(2,1)S(1)}, bf16[512,1024]{1,0:T(8,128)(2,1)}, u32[]{:S(2)}) copy-start(bf16[512,1024]{1,0:T(8,128)(2,1)} %param.15) | copy-start | bytes 3145732
  7.2 44.1 %copy-start.18 = (f32[3,512]{1,0:T(4,128)S(1)}, f32[3,512]{1,0:T(4,128)}, u32[]{:S(2)}) copy-start(f32[3,512]{1,0:T(4,128)} %param.13) | copy-start | bytes 18436
  7.2 133.8 %all-reduce.3.cloned.1.call-start = ((), (), s32[]{:S(2)}) async-start(), calls=%async_computation.1 | async-start | bytes 11010048 | tf_op jit(solution)/shard_map/psum | solution.py:157
  36.5 15.5 %copy-start.3 = (bf16[16,2,48,512]{3,2,1,0:T(8,128)(2,1)S(1)}, bf16[16,2,48,512]{3,2,1,0:T(8,128)(2,1)}, u32[]{:S(2)}) copy-start(bf16[16,2,48,512]{3,2,1,0:T(8,128)(2,1)} %shard_map.131) | copy-start | bytes 4718596
  53.0 1.9 copy-start.25
  59.1 7.8 %copy-start.23 = (s32[2,64]{1,0:T(2,128)S(1)}, s32[2,64]{1,0:T(2,128)}, u32[]{:S(2)}) copy-start(s32[2,64]{1,0:T(2,128)} %param.22) | copy-start | bytes 1540
  59.1 8.8 %copy-start.27 = (s32[1,96]{1,0:T(1,128)S(1)}, s32[1,96]{1,0:T(1,128)}, u32[]{:S(2)}) copy-start(s32[1,96]{1,0:T(1,128)} %param.23) | copy-start | bytes 1156
  59.1 352.8 %reduce-scatter.2.cloned.1.call-start = ((), (), s32[]{:S(2)}) async-start(), calls=%async_computation.2 | async-start | bytes 2654208 | tf_op jit(solution)/shard_map/reduce_scatter | solution.py:297
  67.0 2.4 copy-start.19
  67.1 78.3 %copy-start.17 = (s32[1024]{0:T(1024)}, s32[1024]{0:T(1024)S(1)}, u32[]{:S(2)}) copy-start(s32[1024]{0:T(1024)S(1)} %pad_clamp_fusion.3) | copy-start | bytes 12292
  68.7 76.7 %copy-start.21 = (pred[64]{0:T(512)(128)(4,1)}, pred[64]{0:T(512)(128)(4,1)S(1)}, u32[]{:S(2)}) copy-start(pred[64]{0:T(512)(128)(4,1)S(1)} %broadcast_compare_fusion) | copy-start | bytes 196
  159.5 1.4 slice-start.2
  159.5 4.4 %slice-start = ((s8[6291456]{0:T(1024)(128)(4,1)}), s8[2097152]{0:T(1024)(128)(4,1)S(1)}, s32[]{:S(2)}) async-start(s8[6291456]{0:T(1024)(128)(4,1)} %bitcast.267), calls=%async_computation.3 | async-start | bytes 4194304
  161.1 2.9 slice-start.1
  164.3 0.8 copy-start.5
  171.2 6.4 %copy-start.7 = (bf16[2,768,2,96]{3,1,2,0:T(8,128)(2,1)S(1)}, bf16[2,768,2,96]{3,1,2,0:T(8,128)(2,1)}, u32[]{:S(2)}) copy-start(bf16[2,768,2,96]{3,1,2,0:T(8,128)(2,1)} %slice.222) | copy-start | bytes 1769476
  189.4 4.4 %copy-start.15 = (pred[64,96]{1,0:T(8,128)(4,1)S(1)}, pred[64,96]{1,0:T(8,128)(4,1)}, u32[]{:S(2)}) copy-start(pred[64,96]{1,0:T(8,128)(4,1)} %iota_compare_fusion.1) | copy-start | bytes 18436
  189.4 4.9 %copy-start.6 = (f32[2,2,48,2,3,128]{5,2,1,4,3,0:T(8,128)S(1)}, f32[2,2,48,2,3,128]{5,2,1,4,3,0:T(8,128)}, u32[]{:S(2)}) copy-start(f32[2,2,48,2,3,128]{5,2,1,4,3,0:T(8,128)} %copy-done.5) | copy-start | bytes 1769476
  189.6 3.5 copy-start.4
  190.5 5.2 %copy-start.12 = (f32[2,96,32]{1,2,0:T(8,128)S(1)}, f32[2,96,32]{1,2,0:T(8,128)}, u32[]{:S(2)}) copy-start(f32[2,96,32]{1,2,0:T(8,128)} %get-tuple-element.56) | copy-start | bytes 73732
  190.5 5.2 %copy-start.13 = (f32[2,96,2,16]{1,3,2,0:T(8,128)S(1)}, f32[2,96,2,16]{1,3,2,0:T(8,128)}, u32[]{:S(2)}) copy-start(f32[2,96,2,16]{1,3,2,0:T(8,128)} %get-tuple-element.27) | copy-start | bytes 73732
  190.5 5.2 %copy-start.14 = (f32[2,96,2,16]{1,3,2,0:T(8,128)S(1)}, f32[2,96,2,16]{1,3,2,0:T(8,128)}, u32[]{:S(2)}) copy-start(f32[2,96,2,16]{1,3,2,0:T(8,128)} %get-tuple-element.28) | copy-start | bytes 73732
  193.2 5.4 %copy-start.22 = (pred[64]{0:T(512)(128)(4,1)S(1)}, pred[64]{0:T(512)(128)(4,1)}, u32[]{:S(2)}) copy-start(pred[64]{0:T(512)(128)(4,1)} %copy-done.21) | copy-start | bytes 196
  193.8 5.2 %copy-start.20 = (s32[64]{0:T(128)S(1)}, s32[64]{0:T(128)}, u32[]{:S(2)}) copy-start(s32[64]{0:T(128)} %copy-done.19) | copy-start | bytes 772
  229.5 9.9 %copy-start.9 = (bf16[2,96,2,3,128]{4,2,1,3,0:T(2,128)(2,1)S(1)}, bf16[2,96,2,3,128]{4,2,1,3,0:T(2,128)(2,1)}, u32[]{:S(2)}) copy-start(bf16[2,96,2,3,128]{4,2,1,3,0:T(2,128)(2,1)} %copy.354) | copy-start | bytes 884740
  272.5 4.2 %copy-start.24 = (bf16[1024,512]{1,0:T(8,128)(2,1)S(1)}, bf16[1024,512]{1,0:T(8,128)(2,1)}, u32[]{:S(2)}) copy-start(bf16[1024,512]{1,0:T(8,128)(2,1)} %param.17) | copy-start | bytes 3145732
  276.7 14.4 %copy-start.11 = (bf16[256,512]{1,0:T(8,128)(2,1)S(1)}, bf16[256,512]{1,0:T(8,128)(2,1)}, u32[]{:S(2)}) copy-start(bf16[256,512]{1,0:T(8,128)(2,1)} %param.16) | copy-start | bytes 786436
  291.1 36.9 %copy-start.10 = (bf16[2,48,512]{2,1,0:T(8,128)(2,1)S(1)}, bf16[2,48,512]{2,1,0:T(8,128)(2,1)}, u32[]{:S(2)}) copy-start(bf16[2,48,512]{2,1,0:T(8,128)(2,1)} %x_ref.1) | copy-start | bytes 294916
  292.9 43.6 %copy-start.16 = (f32[1,512]{1,0:T(1,128)S(1)}, f32[1,512]{1,0:T(1,128)}, u32[]{:S(2)}) copy-start(f32[1,512]{1,0:T(1,128)} %get-tuple-element.37) | copy-start | bytes 6148
  292.9 78.9 %copy-start.26 = (bf16[512,768]{1,0:T(8,128)(2,1)S(1)}, bf16[512,768]{1,0:T(8,128)(2,1)}, u32[]{:S(2)}) copy-start(bf16[512,768]{1,0:T(8,128)(2,1)} %param.18) | copy-start | bytes 2359300
  328.1 48.0 %copy-start.8 = (bf16[2,48,512]{2,1,0:T(8,128)(2,1)}, bf16[2,48,512]{2,1,0:T(8,128)(2,1)S(1)}, u32[]{:S(2)}) copy-start(bf16[2,48,512]{2,1,0:T(8,128)(2,1)S(1)} %get-tuple-element.7) | copy-start | bytes 294916
  371.8 41.8 %copy-start.1 = (bf16[512,1024]{1,0:T(8,128)(2,1)S(1)}, bf16[512,1024]{1,0:T(8,128)(2,1)}, u32[]{:S(2)}) copy-start(bf16[512,1024]{1,0:T(8,128)(2,1)} %param.15) | copy-start | bytes 3145732
  (1 other events, 0.7 us)
Sparse Core Ops, SparseCore 0:
  59.2 81.7 all-reduce.2
  376.2 35.6 reduce-scatter.1

commit v5 on v4

--- a/solution.py
+++ b/solution.py
@@ -74,6 +74,9 @@
         ],
         compiler_params=pltpu.CompilerParams(
             collective_id=collective_id, has_side_effects=True
+        ),
+        cost_estimate=pl.CostEstimate(
+            flops=0, transcendentals=0, bytes_accessed=2 * n * x.size * x.dtype.itemsize
         ),
     )(x)
 
@@ -150,15 +153,15 @@
     normed = row_normalize(rows_all.astype(jnp.float32), 3)
     attn_in = (normed * norm_gains[0]).astype(jnp.bfloat16)
     mlp_in = (normed * norm_gains[1]).astype(jnp.bfloat16)
-    piece = jnp.concatenate([attn_in, mlp_in], axis=-1)
-    first = jnp.dot(piece[:, :local_width], attn_weight, preferred_element_type=jnp.float32)
-    second = jnp.dot(piece[:, local_width:], up_weight, preferred_element_type=jnp.float32)
-    partial_sums = jnp.concatenate([first, second], axis=1)
-    summed_all = lax.psum(partial_sums.astype(jnp.bfloat16), "req").astype(jnp.float32)
-    mixed_msi = summed_all[:, :triple_width].reshape(
+    first = jnp.dot(attn_in, attn_weight, preferred_element_type=jnp.float32)
+    second = jnp.dot(mlp_in, up_weight, preferred_element_type=jnp.float32)
+    mixed_sum = lax.psum(first.astype(jnp.bfloat16), "req")
+    mixed_sum, second = lax.optimization_barrier((mixed_sum, second.astype(jnp.bfloat16)))
+    hidden_sum = lax.psum(second, "req")
+    mixed_msi = mixed_sum.astype(jnp.float32).reshape(
         mlp_size, steps, local_rows, head_count, 3, HD
     )
-    activated_all = jax.nn.gelu(summed_all[:, triple_width:], approximate=False).astype(
+    activated_all = jax.nn.gelu(hidden_sum.astype(jnp.float32), approximate=False).astype(
         jnp.bfloat16
     )
     mixed_all = mixed_msi[:, :, :, :, 0].transpose(1, 0, 2, 3, 4).reshape(

time: 427 us -> 449 us (1.052)
  waiting for transfers between devices: 107 us -> 141 us
  local copies, waits for them, and re-layouts: 85 us -> 74.7 us
  matrix products: 35.1 us -> 40.5 us
  other arithmetic: 36.4 us -> 31.1 us
    psum x1 -> x2, waiting for transfers between devices: 71.5 us -> 104 us  [the longest x1 56 us: shards(): mixed_sum = lax.psum(first.astype(jnp.bfloat16), 'req')]
    slice x2 -> x0, local copies, waits for them, and re-layouts: 10.5 us -> none  [shards(): summed_all[:, :triple_width]]
    unnamed x70 -> x76, local copies, waits for them, and re-layouts: 10.7 us -> 10.7 us
  transfers between devices with their start and end apart: 2 -> 3, of which waited for: 2 -> 3; matrix products, arithmetic and copies ran while one was open for 2% -> 6% of each run, Pallas kernels for 0% -> 4%
where the time goes in v5:
time: 449 us; the launch traced here: 444 us
  Pallas kernels  142 us (32%)
  waiting for transfers between devices  141 us (31%)
  local copies, waits for them, and re-layouts  74.7 us (17%)
  matrix products  40.5 us (9%)
  other arithmetic  31.1 us (7%)
  between operations  14.9 us (3%)
    pallas_call x7, Pallas kernels, exchange(): pl.pallas_call(functools.partial(exchange_kernel, axis, n, gather), out_s...  142 us
    psum x1, waiting for transfers between devices, shards(): mixed_sum = lax.psum(first.astype(jnp.bfloat16), 'req')  56 us
    psum x1, waiting for transfers between devices, shards(): hidden_sum = lax.psum(second, 'req')  47.8 us
    reduce_scatter x1, waiting for transfers between devices, shards(): lax.psum_scatter(next_partial.astype(jnp.bfloat16), 'req', scatter_dimens...  37.1 us
    dot_general x1, matrix products, shards(): jnp.dot(activated_all, down_weight, preferred_element_type=jnp.float32)  15.4 us
    unnamed x76, local copies, waits for them, and re-layouts  10.7 us
  transfers between devices with their start and end apart: 3, of which 3 were waited for; matrix products, arithmetic and copies ran while one was open for 6% of the time, Pallas kernels for 4%

profile of v5, /device:TPU:0, one launch (start us, length us, event | category | flops | bytes accessed | tf_op | source)
XLA Modules:
  0.0 444.5 jit_solution(6705559588256289680)
XLA Ops:
  7.2 29.2 %shard_map.131 = bf16[16,2,48,512]{3,2,1,0:T(8,128)(2,1)} custom-call(bf16[2,48,512]{2,1,0:T(8,128)(2,1)} %x_ref.1), custom_call_target="tpu_custom_call" | custom-call | bytes 3145728 | tf_op jit(solution)/shard_map/pallas_call | solution.py:65
  36.5 1.8 convert_reduce_fusion.1
  38.3 2.1 multiply_reduce_fusion
  41.3 8.9 %shard_map.132 = f32[8,24,128]{2,1,0:T(8,128)} custom-call(f32[24,128]{1,0:T(8,128)} %reshape.535.x_ref), custom_call_target="tpu_custom_call" | custom-call | bytes 196608 | tf_op jit(solution)/shard_map/pallas_call | solution.py:65
  51.9 1.9 multiply_convert_fusion
  53.8 3.9 convolution_convert_fusion.2
  58.4 4.8 %gather_fusion.1 = s32[768]{0:T(1024)S(1)} fusion(s32[96]{0:T(128)S(1)} %copy-done.2, s32[1024]{0:T(1024)S(1)} %pad_clamp_fusion.2), kind=kCustom, calls=%fused_computation.1 | custom fusion | bytes 9216 | tf_op jit(solution)/shard_map/gather | solution.py:139
  68.2 3.5 convolution_convert_fusion
  71.7 56.0 %all-reduce.4.cloned.1.call-done = bf16[1536,768]{1,0:T(8,128)(2,1)} async-done(((bf16[1536,768]{1,0:T(8,128)(2,1)}), bf16[1536,768]{1,0:T(8,128)(2,1)}) %all-reduce.4.cloned.1.call-update) | async-done | bytes 2359312 | tf_op jit(solution)/shard_map/psum | solution.py:158
  127.8 7.5 %reshape.556 = f32[16,2,48,2,3,128]{5,4,3,2,1,0:T(4,128)} reshape(bf16[1536,768]{1,0:T(8,128)(2,1)} %all-reduce.4.cloned.1.call-done) | data formatting | bytes 7077888 | tf_op jit(solution)/shard_map/reshape | solution.py:161
  143.2 3.7 copy_multiply_fusion
  146.9 2.4 copy.253
  149.4 1.9 copy.317
  154.4 2.1 pad_maximum_fusion
  156.6 2.8 gather_fusion.2
  159.5 2.8 fusion.49
  162.2 2.8 fusion.52
  166.6 2.7 fusion.55
  181.2 3.7 reshape.539.x_ref
  184.9 13.9 %shard_map.133 = bf16[8,393,128]{2,1,0:T(8,128)(2,1)} custom-call(bf16[8,393,128]{2,1,0:T(8,128)(2,1)} %reshape.539.x_ref), custom_call_target="tpu_custom_call" | custom-call | bytes 12877824 | tf_op jit(solution)/shard_map/pallas_call | solution.py:65
  198.8 6.6 %reshape.557 = f32[8,2,96,2,131]{4,3,2,1,0:T(2,128)S(1)} reshape(bf16[8,393,128]{2,1,0:T(8,128)(2,1)} %shard_map.133) | data formatting | bytes 2414592 | tf_op jit(solution)/shard_map/convert_element_type | solution.py:239
  205.4 5.0 %fusion.161 = (f32[8,2,96,2,1]{4,3,2,1,0:T(2,128)}, f32[8,2,96,2,1]{4,3,2,1,0:T(2,128)}, f32[8,2,96,2,1]{4,3,2,1,0:T(2,128)}) fusion(f32[8,2,96,2,131]{4,3,2,1,0:T(2,128)S(1)} %reshape.557), kind=kLoop, calls=%fused_computation.277 | loop fusion | bytes 73728 | tf_op jit(solution)/shard_map/slice | solution.py:244
  224.2 1.9 copy.278
  229.2 3.7 fusion.47
  234.2 17.8 %shard_map.134 = bf16[8,2,96,256]{3,2,1,0:T(8,128)(2,1)} custom-call(bf16[2,96,256]{2,1,0:T(8,128)(2,1)} %pad_maximum_fusion.4.x_ref), custom_call_target="tpu_custom_call" | custom-call | bytes 1572864 | tf_op jit(solution)/shard_map/pallas_call | solution.py:65
  253.3 47.8 %all-reduce.6.cloned.1.call-done = bf16[1536,1024]{1,0:T(8,128)(2,1)} async-done(((bf16[1536,1024]{1,0:T(8,128)(2,1)}), bf16[1536,1024]{1,0:T(8,128)(2,1)}) %all-reduce.6.cloned.1.call-update) | async-done | bytes 3145744 | tf_op jit(solution)/shard_map/psum | solution.py:160
  301.1 15.4 %fusion.32 = f32[1536,512]{1,0:T(8,128)S(1)} fusion(bf16[1024,512]{1,0:T(8,128)(2,1)} %param.17, bf16[1536,1024]{1,0:T(8,128)(2,1)} %all-reduce.6.cloned.1.call-done), kind=kOutput, calls=%fused_computation.50 | convolution fusion | flops 1714421760 | bytes 7340032 | tf_op jit(solution)/shard_map/dot_general | solution.py:284
  318.3 25.1 %shard_map.135 = bf16[16,96,512]{2,1,0:T(8,128)(2,1)} custom-call(bf16[16,96,512]{2,1,0:T(8,128)(2,1)} %bitcast.270), custom_call_target="tpu_custom_call" | custom-call | bytes 50331648 | tf_op jit(solution)/shard_map/pallas_call | solution.py:65
  346.0 11.7 %shard_map.136 = f32[8,2,128]{2,1,0:T(2,128)} custom-call(f32[2,128]{1,0:T(2,128)} %pad_bitcast_fusion.x_ref), custom_call_target="tpu_custom_call" | custom-call | bytes 16384 | tf_op jit(solution)/shard_map/pallas_call | solution.py:65
  359.3 35.2 %shard_map.137 = bf16[16,2,48,512]{3,2,1,0:T(8,128)(2,1)} custom-call(bf16[2,48,512]{2,1,0:T(8,128)(2,1)} %fusion.75.x_ref), custom_call_target="tpu_custom_call" | custom-call | bytes 3145728 | tf_op jit(solution)/shard_map/pallas_call | solution.py:65
  394.6 4.3 convolution_convert_fusion.1
  398.9 37.1 %reduce-scatter.2.cloned.1.call-done = bf16[192,768]{1,0:T(8,128)(2,1)} async-done(((bf16[1536,768]{1,0:T(8,128)(2,1)}), bf16[192,768]{1,0:T(8,128)(2,1)}) %reduce-scatter.2.cloned.1.call-update) | async-done | bytes 294928 | tf_op jit(solution)/shard_map/reduce_scatter | solution.py:300
  (204 shorter events, 59.1 us)
Async XLA Ops:
  7.2 61.0 %copy-start = (bf16[512,1024]{1,0:T(8,128)(2,1)S(1)}, bf16[512,1024]{1,0:T(8,128)(2,1)}, u32[]{:S(2)}) copy-start(bf16[512,1024]{1,0:T(8,128)(2,1)} %param.15) | copy-start | bytes 3145732
  7.2 44.1 %copy-start.23 = (f32[3,512]{1,0:T(4,128)S(1)}, f32[3,512]{1,0:T(4,128)}, u32[]{:S(2)}) copy-start(f32[3,512]{1,0:T(4,128)} %param.13) | copy-start | bytes 18436
  7.2 120.6 %all-reduce.4.cloned.1.call-start = ((), (), s32[]{:S(2)}) async-start(), calls=%async_computation.1 | async-start | bytes 4718592 | tf_op jit(solution)/shard_map/psum | solution.py:158
  36.5 15.4 %copy-start.3 = (bf16[16,2,48,512]{3,2,1,0:T(8,128)(2,1)S(1)}, bf16[16,2,48,512]{3,2,1,0:T(8,128)(2,1)}, u32[]{:S(2)}) copy-start(bf16[16,2,48,512]{3,2,1,0:T(8,128)(2,1)} %shard_map.131) | copy-start | bytes 4718596
  53.8 4.4 copy-start.28
  57.8 8.0 %copy-start.30 = (s32[1,96]{1,0:T(1,128)S(1)}, s32[1,96]{1,0:T(1,128)}, u32[]{:S(2)}) copy-start(s32[1,96]{1,0:T(1,128)} %param.23) | copy-start | bytes 1156
  57.8 243.3 %all-reduce.6.cloned.1.call-start = ((), (), s32[]{:S(2)}) async-start(), calls=%async_computation.2 | async-start | bytes 6291456 | tf_op jit(solution)/shard_map/psum | solution.py:160
  58.2 9.2 %copy-start.24 = (s32[64]{0:T(128)}, s32[64]{0:T(128)S(1)}, u32[]{:S(2)}) copy-start(s32[64]{0:T(128)S(1)} %get-tuple-element.54) | copy-start | bytes 772
  58.4 9.8 %copy-start.8 = (bf16[1536,512]{1,0:T(8,128)(2,1)S(1)}, bf16[1536,512]{1,0:T(8,128)(2,1)}, u32[]{:S(2)}) copy-start(bf16[1536,512]{1,0:T(8,128)(2,1)} %get-tuple-element.23) | copy-start | bytes 4718596
  65.8 106.8 %copy-start.21 = (s32[1024]{0:T(1024)}, s32[1024]{0:T(1024)S(1)}, u32[]{:S(2)}) copy-start(s32[1024]{0:T(1024)S(1)} %pad_clamp_fusion) | copy-start | bytes 12292
  66.0 5.8 %copy-start.22 = (s32[1024]{0:T(1024)}, s32[1024]{0:T(1024)S(1)}, u32[]{:S(2)}) copy-start(s32[1024]{0:T(1024)S(1)} %pad_clamp_fusion.3) | copy-start | bytes 12292
  67.4 4.4 copy-start.26
  135.3 4.4 slice-start
  149.3 4.0 copy-start.7
  165.7 3.6 copy-start.4
  166.5 3.9 copy-start.6
  166.6 5.2 %copy-start.15 = (f32[2,96,32]{1,2,0:T(8,128)S(1)}, f32[2,96,32]{1,2,0:T(8,128)}, u32[]{:S(2)}) copy-start(f32[2,96,32]{1,2,0:T(8,128)} %get-tuple-element.60) | copy-start | bytes 73732
  166.6 5.2 %copy-start.16 = (f32[2,96,2,16]{1,3,2,0:T(8,128)S(1)}, f32[2,96,2,16]{1,3,2,0:T(8,128)}, u32[]{:S(2)}) copy-start(f32[2,96,2,16]{1,3,2,0:T(8,128)} %get-tuple-element.31) | copy-start | bytes 73732
  166.6 5.2 %copy-start.17 = (f32[2,96,2,16]{1,3,2,0:T(8,128)S(1)}, f32[2,96,2,16]{1,3,2,0:T(8,128)}, u32[]{:S(2)}) copy-start(f32[2,96,2,16]{1,3,2,0:T(8,128)} %get-tuple-element.32) | copy-start | bytes 73732
  169.3 5.4 %copy-start.27 = (pred[64]{0:T(512)(128)(4,1)S(1)}, pred[64]{0:T(512)(128)(4,1)}, u32[]{:S(2)}) copy-start(pred[64]{0:T(512)(128)(4,1)} %copy-done.26) | copy-start | bytes 196
  170.4 4.7 %copy-start.25 = (s32[64]{0:T(128)S(1)}, s32[64]{0:T(128)}, u32[]{:S(2)}) copy-start(s32[64]{0:T(128)} %copy-done.24) | copy-start | bytes 772
  210.4 4.9 %copy-start.10 = (bf16[2,96,2,3,128]{4,2,1,3,0:T(2,128)(2,1)S(1)}, bf16[2,96,2,3,128]{4,2,1,3,0:T(2,128)(2,1)}, u32[]{:S(2)}) copy-start(bf16[2,96,2,3,128]{4,2,1,3,0:T(2,128)(2,1)} %copy.347) | copy-start | bytes 884740
  213.9 6.8 %copy-start.18 = (f32[2,96,2]{1,2,0:T(2,128)}, f32[2,96,2]{1,2,0:T(2,128)S(1)}, u32[]{:S(2)}) copy-start(f32[2,96,2]{1,2,0:T(2,128)S(1)} %get-tuple-element.16) | copy-start | bytes 4612
  222.9 213.1 %reduce-scatter.2.cloned.1.call-start = ((), (), s32[]{:S(2)}) async-start(), calls=%async_computation.3 | async-start | bytes 2654208 | tf_op jit(solution)/shard_map/reduce_scatter | solution.py:300
  226.1 6.8 %copy-start.13 = (f32[96,2]{1,0:T(8,128)S(1)}, f32[96,2]{1,0:T(8,128)}, u32[]{:S(2)}) copy-start(f32[96,2]{1,0:T(8,128)} %copy.288) | copy-start | bytes 2308
  226.1 6.8 %copy-start.14 = (f32[96,2]{1,0:T(8,128)S(1)}, f32[96,2]{1,0:T(8,128)}, u32[]{:S(2)}) copy-start(f32[96,2]{1,0:T(8,128)} %copy.289) | copy-start | bytes 2308
  253.3 63.3 %copy-start.12 = (bf16[256,512]{1,0:T(8,128)(2,1)S(1)}, bf16[256,512]{1,0:T(8,128)(2,1)}, u32[]{:S(2)}) copy-start(bf16[256,512]{1,0:T(8,128)(2,1)} %param.16) | copy-start | bytes 786436
  318.3 26.8 %copy-start.11 = (bf16[2,48,512]{2,1,0:T(8,128)(2,1)S(1)}, bf16[2,48,512]{2,1,0:T(8,128)(2,1)}, u32[]{:S(2)}) copy-start(bf16[2,48,512]{2,1,0:T(8,128)(2,1)} %x_ref.1) | copy-start | bytes 294916
  318.3 40.3 %copy-start.20 = (f32[1,512]{1,0:T(1,128)S(1)}, f32[1,512]{1,0:T(1,128)}, u32[]{:S(2)}) copy-start(f32[1,512]{1,0:T(1,128)} %get-tuple-element.41) | copy-start | bytes 6148
  318.3 76.3 %copy-start.29 = (bf16[512,768]{1,0:T(8,128)(2,1)S(1)}, bf16[512,768]{1,0:T(8,128)(2,1)}, u32[]{:S(2)}) copy-start(bf16[512,768]{1,0:T(8,128)(2,1)} %param.18) | copy-start | bytes 2359300
  345.1 53.8 %copy-start.9 = (bf16[2,48,512]{2,1,0:T(8,128)(2,1)}, bf16[2,48,512]{2,1,0:T(8,128)(2,1)S(1)}, u32[]{:S(2)}) copy-start(bf16[2,48,512]{2,1,0:T(8,128)(2,1)S(1)} %get-tuple-element.11) | copy-start | bytes 294916
  394.6 43.1 %copy-start.1 = (bf16[512,1024]{1,0:T(8,128)(2,1)S(1)}, bf16[512,1024]{1,0:T(8,128)(2,1)}, u32[]{:S(2)}) copy-start(bf16[512,1024]{1,0:T(8,128)(2,1)} %param.15) | copy-start | bytes 3145732
  (5 other events, 9.2 us)
Sparse Core Ops, SparseCore 0:
  57.9 69.8 all-reduce.3
  223.0 78.0 all-reduce.5
  399.1 36.9 reduce-scatter.1

commit v6 on v5

--- a/solution.py
+++ b/solution.py
@@ -30,6 +30,21 @@
     turned = vectors[..., :ROT]
     swapped = jnp.concatenate([-turned[..., half:], turned[..., :half]], axis=-1)
     return jnp.concatenate([turned * cosine + swapped * sine, vectors[..., ROT:]], axis=-1)
+
+
+def rotate_rows(rows, positions, head_count):
+    half = ROT // 2
+    freq = jnp.exp(jnp.arange(half, dtype=jnp.float32) * (-2.0 * math.log(10000.0) / ROT))
+    angles = positions.astype(jnp.float32)[:, None] * freq[None, :]
+    cosine = jnp.concatenate([jnp.cos(angles), jnp.cos(angles)], axis=1)
+    sine = jnp.concatenate([jnp.sin(angles), jnp.sin(angles)], axis=1)
+    parts = []
+    for head in range(head_count):
+        base = head * HD
+        turned = rows[:, base : base + ROT]
+        swapped = jnp.concatenate([-turned[:, half:], turned[:, :half]], axis=1)
+        parts += [turned * cosine + swapped * sine, rows[:, base + ROT : base + HD]]
+    return jnp.concatenate(parts, axis=1)
 
 
 def exchange_kernel(axis, n, gather, x_ref, out_ref, send_sem, recv_sem, local_sem):
@@ -153,37 +168,53 @@
     normed = row_normalize(rows_all.astype(jnp.float32), 3)
     attn_in = (normed * norm_gains[0]).astype(jnp.bfloat16)
     mlp_in = (normed * norm_gains[1]).astype(jnp.bfloat16)
-    first = jnp.dot(attn_in, attn_weight, preferred_element_type=jnp.float32)
+    grouped = (
+        attn_weight.reshape(local_width, head_count, 3, HD)
+        .transpose(0, 2, 1, 3)
+        .reshape(local_width, triple_width)
+    )
+    first = jnp.dot(attn_in, grouped, preferred_element_type=jnp.float32)
     second = jnp.dot(mlp_in, up_weight, preferred_element_type=jnp.float32)
-    mixed_sum = lax.psum(first.astype(jnp.bfloat16), "req")
-    mixed_sum, second = lax.optimization_barrier((mixed_sum, second.astype(jnp.bfloat16)))
-    hidden_sum = lax.psum(second, "req")
-    mixed_msi = mixed_sum.astype(jnp.float32).reshape(
-        mlp_size, steps, local_rows, head_count, 3, HD
-    )
-    activated_all = jax.nn.gelu(hidden_sum.astype(jnp.float32), approximate=False).astype(
-        jnp.bfloat16
-    )
-    mixed_all = mixed_msi[:, :, :, :, 0].transpose(1, 0, 2, 3, 4).reshape(
-        steps, beam_total, head_count, HD
-    )
-    queries_all = rotate(mixed_all, all_positions).astype(jnp.bfloat16)
+    partial_sums = jnp.concatenate([first, second], axis=1)
+    summed_all = lax.psum(partial_sums.astype(jnp.bfloat16), "req")
+    width = head_count * HD
+    activated_all = jax.nn.gelu(
+        summed_all[:, triple_width:].astype(jnp.float32), approximate=False
+    ).astype(jnp.bfloat16)
+    row = jnp.arange(steps * beam_total, dtype=jnp.int32)
+    row_beam = (row // (steps * local_rows)) * local_rows + row % local_rows
+    row_positions = lengths[row_beam // BEAM] + (row // local_rows) % steps
+    queries_rows = rotate_rows(
+        summed_all[:, :width].astype(jnp.float32), row_positions, head_count
+    ).astype(jnp.bfloat16)
+    keys_rows = rotate_rows(
+        summed_all[:, width : 2 * width].astype(jnp.float32), row_positions, head_count
+    ).astype(jnp.bfloat16)
     per_own = own_count // local_rows
-    mixed_own = (
-        lax.dynamic_slice_in_dim(mixed_msi, lax.axis_index("req") * per_own, per_own, 0)
-        .transpose(1, 0, 2, 3, 4, 5)
-        .reshape(steps, own_count, head_count, 3, HD)
-    )
-    own_positions = lax.dynamic_slice_in_dim(all_positions, offset, own_count, 1)
-    queries_own = lax.dynamic_slice_in_dim(queries_all, offset, own_count, 1)
-    keys_new = rotate(mixed_own[:, :, :, 1], own_positions).astype(jnp.bfloat16)
-    values_new = mixed_own[:, :, :, 2].astype(jnp.bfloat16)
-
-    chosen = queries_all[:, gather_rows]
+    own_start = lax.axis_index("req") * (per_own * steps * local_rows)
+
+    def own_of(rows):
+        return (
+            lax.dynamic_slice_in_dim(rows, own_start, per_own * steps * local_rows, 0)
+            .reshape(per_own, steps, local_rows, -1)
+            .transpose(1, 0, 2, 3)
+            .reshape(steps, own_count, head_count, HD)
+        )
+
+    queries_own = own_of(queries_rows)
+    keys_new = own_of(keys_rows)
+    values_new = own_of(summed_all[:, 2 * width : 3 * width])
+
+    chosen_rows = (
+        (gather_rows // local_rows) * (steps * local_rows)
+        + jnp.arange(steps, dtype=jnp.int32)[:, None, None] * local_rows
+        + gather_rows % local_rows
+    )
+    chosen = queries_rows[chosen_rows]
     head_scores = [
         jnp.einsum(
             "zsbd,std->zsbt",
-            chosen[:, :, :, head],
+            chosen[..., head * HD : (head + 1) * HD],
             cache_keys[:, :, head * HD : (head + 1) * HD],
             preferred_element_type=jnp.float32,
         )

time: 449 us -> 398 us (0.89)
  waiting for transfers between devices: 141 us -> 105 us
  local copies, waits for them, and re-layouts: 74.7 us -> 63.8 us
    psum x2 -> x1, waiting for transfers between devices: 104 us -> 69.7 us  [shards(): summed_all = lax.psum(partial_sums.astype(jnp.bfloat16), 'req')]
    reshape x2 -> x0, local copies, waits for them, and re-layouts: 8.71 us -> none  [the longest x1 7.54 us: shards(): mixed_sum.astype(jnp.float32)]
    gather x3 -> x2, local copies, waits for them, and re-layouts: 7.66 us -> 14 us  [the longest x1 9.03 us: shards(): row_positions = lengths[row_beam // BEAM] + row // local_rows % steps]
    unnamed x76 -> x74, local copies, waits for them, and re-layouts: 10.7 us -> 5.35 us
    dot_general x3 -> x4, matrix products: 9.5 us -> 7.31 us  [the longest x2 5.55 us: shards(): jnp.einsum('zsbd,std->zsbt', chosen[..., head * HD:(head + 1) * HD], cach...]
  transfers between devices with their start and end apart: 3 -> 2, of which waited for: 3 -> 2; matrix products, arithmetic and copies ran while one was open for 6% -> 3% of each run, Pallas kernels for 4% -> 0%
where the time goes in v6:
time: 398 us; the launch traced here: 397 us
  Pallas kernels  142 us (36%)
  waiting for transfers between devices  105 us (26%)
  local copies, waits for them, and re-layouts  63.8 us (16%)
  matrix products  40.2 us (10%)
  other arithmetic  31.2 us (8%)
  between operations  15 us (4%)
    pallas_call x7, Pallas kernels, exchange(): pl.pallas_call(functools.partial(exchange_kernel, axis, n, gather), out_s...  142 us
    psum x1, waiting for transfers between devices, shards(): summed_all = lax.psum(partial_sums.astype(jnp.bfloat16), 'req')  69.7 us
    reduce_scatter x1, waiting for transfers between devices, shards(): lax.psum_scatter(next_partial.astype(jnp.bfloat16), 'req', scatter_dimens...  35.5 us
    dot_general x1, matrix products, shards(): jnp.dot(activated_all, down_weight, preferred_element_type=jnp.float32)  16.3 us
    gather x1, local copies, waits for them, and re-layouts, shards(): row_positions = lengths[row_beam // BEAM] + row // local_rows % steps  9.03 us
    slice x2, local copies, waits for them, and re-layouts, shards(): own_total = jnp.sum(held[..., HD] * rescale, axis=0)  7.98 us
  transfers between devices with their start and end apart: 2, of which 2 were waited for; matrix products, arithmetic and copies ran while one was open for 3% of the time, Pallas kernels for 0%

profile of v6, /device:TPU:0, one launch (start us, length us, event | category | flops | bytes accessed | tf_op | source)
XLA Modules:
  0.0 397.3 jit_solution(4671151079244144307)
XLA Ops:
  7.2 29.2 %shard_map.131 = bf16[16,2,48,512]{3,2,1,0:T(8,128)(2,1)} custom-call(bf16[2,48,512]{2,1,0:T(8,128)(2,1)} %x_ref.1), custom_call_target="tpu_custom_call" | custom-call | bytes 3145728 | tf_op jit(solution)/shard_map/pallas_call | solution.py:80
  36.5 1.8 convert_reduce_fusion.1
  38.4 2.1 multiply_reduce_fusion
  44.3 8.9 %shard_map.132 = f32[8,24,128]{2,1,0:T(8,128)} custom-call(f32[24,128]{1,0:T(8,128)} %reshape.678.x_ref), custom_call_target="tpu_custom_call" | custom-call | bytes 196608 | tf_op jit(solution)/shard_map/pallas_call | solution.py:80
  59.7 1.8 convolution_convert_fusion
  61.6 2.8 pad_maximum_fusion
  65.9 9.0 %gather_fusion.1 = s32[1536]{0:T(1024)S(1)} fusion(s32[96]{0:T(128)S(1)} %copy-done.2, s32[2048]{0:T(1024)S(1)} %pad_clamp_fusion), kind=kCustom, calls=%fused_computation.1 | custom fusion | bytes 18432 | tf_op jit(solution)/shard_map/gather | solution.py:186
  76.6 69.7 %all-reduce.3.cloned.1.call-done = bf16[1536,1792]{0,1:T(8,128)(2,1)} async-done(((bf16[1536,1792]{0,1:T(8,128)(2,1)}), bf16[1536,1792]{0,1:T(8,128)(2,1)}) %all-reduce.3.cloned.1.call-update) | async-done | bytes 5505040 | tf_op jit(solution)/shard_map/psum | solution.py:179
  146.3 2.8 fusion.178
  150.0 2.1 fusion.179
  152.4 4.9 %gather_fusion.2 = bf16[1024,256]{1,0:T(8,128)(2,1)} fusion(bf16[1536,256]{1,0:T(8,128)(2,1)S(1)} %copy.176, s32[1024]{0:T(1024)S(1)} %broadcast_clamp_fusion), kind=kCustom, calls=%fused_computation.2 | custom fusion | bytes 1052672 | tf_op jit(solution)/shard_map/gather | solution.py:213
  158.4 2.8 fusion.51
  161.2 2.8 fusion.54
  164.5 2.0 fusion.67
  167.1 3.2 fusion.60
  170.3 3.2 fusion.57
  178.2 2.2 gather_fusion.5
  193.3 3.8 reshape.681.x_ref
  197.0 14.0 %shard_map.133 = bf16[8,393,128]{2,1,0:T(8,128)(2,1)} custom-call(bf16[8,393,128]{2,1,0:T(8,128)(2,1)} %reshape.681.x_ref), custom_call_target="tpu_custom_call" | custom-call | bytes 12877824 | tf_op jit(solution)/shard_map/pallas_call | solution.py:80
  211.0 7.7 %reshape.700 = f32[8,2,96,2,131]{4,3,2,1,0:T(2,128)} reshape(bf16[8,393,128]{2,1,0:T(8,128)(2,1)} %shard_map.133) | data formatting | bytes 2414592 | tf_op jit(solution)/shard_map/convert_element_type | solution.py:270
  218.7 6.3 %fusion.180 = (f32[8,2,96,2,1]{4,3,2,1,0:T(2,128)}, f32[8,2,96,2,1]{4,3,2,1,0:T(2,128)}, f32[8,2,96,2,1]{4,3,2,1,0:T(2,128)S(1)}) fusion(f32[8,2,96,2,131]{4,3,2,1,0:T(2,128)} %reshape.700), kind=kLoop, calls=%fused_computation.305 | loop fusion | bytes 73728 | tf_op jit(solution)/shard_map/slice | solution.py:275
  225.0 1.7 copy.203
  226.7 1.7 copy.232
  230.2 3.6 fusion.49
  235.7 14.5 %shard_map.134 = bf16[8,2,96,256]{3,2,1,0:T(8,128)(2,1)} custom-call(bf16[2,96,256]{2,1,0:T(8,128)(2,1)} %pad_maximum_fusion.6.x_ref), custom_call_target="tpu_custom_call" | custom-call | bytes 1572864 | tf_op jit(solution)/shard_map/pallas_call | solution.py:80
  251.5 16.3 %fusion.34 = f32[1536,512]{1,0:T(8,128)S(1)} fusion(bf16[1024,512]{1,0:T(8,128)(2,1)S(1)} %copy-done.31, bf16[1536,1792]{0,1:T(8,128)(2,1)} %all-reduce.3.cloned.1.call-done), kind=kOutput, calls=%fused_computation.52 | convolution fusion | flops 1714421760 | bytes 7340032 | tf_op jit(solution)/shard_map/dot_general | solution.py:315
  267.9 1.7 fusion.36
  269.6 33.7 %shard_map.135 = bf16[16,96,512]{2,1,0:T(8,128)(2,1)} custom-call(bf16[16,96,512]{2,1,0:T(8,128)(2,1)} %bitcast.276), custom_call_target="tpu_custom_call" | custom-call | bytes 50331648 | tf_op jit(solution)/shard_map/pallas_call | solution.py:80
  305.9 6.7 %shard_map.136 = f32[8,2,128]{2,1,0:T(2,128)} custom-call(f32[2,128]{1,0:T(2,128)} %pad_bitcast_fusion.x_ref), custom_call_target="tpu_custom_call" | custom-call | bytes 16384 | tf_op jit(solution)/shard_map/pallas_call | solution.py:80
  314.2 34.7 %shard_map.137 = bf16[16,2,48,512]{3,2,1,0:T(8,128)(2,1)} custom-call(bf16[2,48,512]{2,1,0:T(8,128)(2,1)} %fusion.75.x_ref), custom_call_target="tpu_custom_call" | custom-call | bytes 3145728 | tf_op jit(solution)/shard_map/pallas_call | solution.py:80
  348.9 4.3 %convolution_convert_fusion.1 = bf16[1536,768]{1,0:T(8,128)(2,1)} fusion(bf16[1536,512]{1,0:T(8,128)(2,1)} %bitcast.282, bf16[512,768]{1,0:T(8,128)(2,1)S(1)} %copy-done.32), kind=kOutput, calls=%fused_computation.42 | convolution fusion | flops 1209139200 | bytes 4718592 | tf_op jit(solution)/shard_map/dot_general | solution.py:330
  353.2 35.5 %reduce-scatter.2.cloned.1.call-done = bf16[192,768]{1,0:T(8,128)(2,1)} async-done(((bf16[1536,768]{1,0:T(8,128)(2,1)}), bf16[192,768]{1,0:T(8,128)(2,1)}) %reduce-scatter.2.cloned.1.call-update) | async-done | bytes 294928 | tf_op jit(solution)/shard_map/reduce_scatter | solution.py:331
  (198 shorter events, 44.5 us)
Async XLA Ops:
  7.2 52.6 %copy-start = (bf16[512,1024]{1,0:T(8,128)(2,1)S(1)}, bf16[512,1024]{1,0:T(8,128)(2,1)}, u32[]{:S(2)}) copy-start(bf16[512,1024]{1,0:T(8,128)(2,1)} %param.15) | copy-start | bytes 3145732
  7.2 33.4 %copy-start.25 = (f32[3,512]{1,0:T(4,128)S(1)}, f32[3,512]{1,0:T(4,128)}, u32[]{:S(2)}) copy-start(f32[3,512]{1,0:T(4,128)} %param.13) | copy-start | bytes 18436
  7.2 139.1 %all-reduce.3.cloned.1.call-start = ((), (), s32[]{:S(2)}) async-start(), calls=%async_computation.1 | async-start | bytes 11010048 | tf_op jit(solution)/shard_map/psum | solution.py:179
  36.5 19.3 %copy-start.3 = (bf16[16,2,48,512]{3,2,1,0:T(8,128)(2,1)S(1)}, bf16[16,2,48,512]{3,2,1,0:T(8,128)(2,1)}, u32[]{:S(2)}) copy-start(bf16[16,2,48,512]{3,2,1,0:T(8,128)(2,1)} %shard_map.131) | copy-start | bytes 4718596
  43.5 14.8 %copy-start.13 = (bf16[512,3,2,128]{0,3,2,1:T(8,128)(2,1)S(1)}, bf16[512,3,2,128]{0,3,2,1:T(8,128)(2,1)}, u32[]{:S(2)}) copy-start(bf16[512,3,2,128]{0,3,2,1:T(8,128)(2,1)} %copy.175) | copy-start | bytes 2359300
  64.4 324.3 %reduce-scatter.2.cloned.1.call-start = ((), (), s32[]{:S(2)}) async-start(), calls=%async_computation.2 | async-start | bytes 2654208 | tf_op jit(solution)/shard_map/reduce_scatter | solution.py:331
  65.1 10.8 %copy-start.26 = (s32[64]{0:T(128)}, s32[64]{0:T(128)S(1)}, u32[]{:S(2)}) copy-start(s32[64]{0:T(128)S(1)} %get-tuple-element.61) | copy-start | bytes 772
  65.1 9.9 %copy-start.24 = (s32[1024]{0:T(1024)}, s32[1024]{0:T(1024)S(1)}, u32[]{:S(2)}) copy-start(s32[1024]{0:T(1024)S(1)} %pad_clamp_fusion.2) | copy-start | bytes 12292
  65.9 9.4 %copy-start.33 = (s32[1,96]{1,0:T(1,128)S(1)}, s32[1,96]{1,0:T(1,128)}, u32[]{:S(2)}) copy-start(s32[1,96]{1,0:T(1,128)} %param.23) | copy-start | bytes 1156
  75.9 74.0 %copy-start.29 = (pred[64]{0:T(512)(128)(4,1)}, pred[64]{0:T(512)(128)(4,1)S(1)}, u32[]{:S(2)}) copy-start(pred[64]{0:T(512)(128)(4,1)S(1)} %broadcast_compare_fusion) | copy-start | bytes 196
  76.6 73.4 %copy-start.8 = (f32[1536,16]{0,1:T(8,128)}, f32[1536,16]{0,1:T(8,128)S(1)}, u32[]{:S(2)}) copy-start(f32[1536,16]{0,1:T(8,128)S(1)} %get-tuple-element.52) | copy-start | bytes 294916
  76.6 73.4 %copy-start.10 = (f32[1536,16]{0,1:T(8,128)}, f32[1536,16]{0,1:T(8,128)S(1)}, u32[]{:S(2)}) copy-start(f32[1536,16]{0,1:T(8,128)S(1)} %get-tuple-element.53) | copy-start | bytes 294916
  166.4 10.3 %copy-start.9 = (f32[1536,16]{0,1:T(8,128)S(1)}, f32[1536,16]{0,1:T(8,128)}, u32[]{:S(2)}) copy-start(f32[1536,16]{0,1:T(8,128)} %copy-done.8) | copy-start | bytes 294916
  166.4 10.3 %copy-start.11 = (f32[1536,16]{0,1:T(8,128)S(1)}, f32[1536,16]{0,1:T(8,128)}, u32[]{:S(2)}) copy-start(f32[1536,16]{0,1:T(8,128)} %copy-done.10) | copy-start | bytes 294916
  167.0 10.9 %copy-start.6 = (bf16[1536,96]{0,1:T(8,128)(2,1)S(1)}, bf16[1536,96]{0,1:T(8,128)(2,1)}, u32[]{:S(2)}) copy-start(bf16[1536,96]{0,1:T(8,128)(2,1)} %get-tuple-element.17) | copy-start | bytes 884740
  167.0 10.9 %copy-start.7 = (bf16[1536,96]{0,1:T(8,128)(2,1)S(1)}, bf16[1536,96]{0,1:T(8,128)(2,1)}, u32[]{:S(2)}) copy-start(bf16[1536,96]{0,1:T(8,128)(2,1)} %get-tuple-element.18) | copy-start | bytes 884740
  170.3 14.0 %copy-start.14 = (f32[2,64,8,2]{2,0,1,3:T(2,128)S(1)}, f32[2,64,8,2]{2,0,1,3:T(2,128)}, u32[]{:S(2)}) copy-start(f32[2,64,8,2]{2,0,1,3:T(2,128)} %get-tuple-element.37) | copy-start | bytes 24580
  174.3 13.2 %copy-start.4 = (f32[2,64,8,1,128]{4,2,0,1,3:T(8,128)S(1)}, f32[2,64,8,1,128]{4,2,0,1,3:T(8,128)}, u32[]{:S(2)}) copy-start(f32[2,64,8,1,128]{4,2,0,1,3:T(8,128)} %fusion.60) | copy-start | bytes 1572868
  177.8 9.6 %copy-start.5 = (f32[2,64,8,1,128]{4,2,0,1,3:T(8,128)S(1)}, f32[2,64,8,1,128]{4,2,0,1,3:T(8,128)}, u32[]{:S(2)}) copy-start(f32[2,64,8,1,128]{4,2,0,1,3:T(8,128)} %fusion.57) | copy-start | bytes 1572868
  177.8 10.0 %copy-start.27 = (s32[64]{0:T(128)S(1)}, s32[64]{0:T(128)}, u32[]{:S(2)}) copy-start(s32[64]{0:T(128)} %copy-done.26) | copy-start | bytes 772
  225.0 4.3 %copy-start.22 = (f32[96,2,1,2]{0,3,1,2:T(2,128)S(1)}, f32[96,2,1,2]{0,3,1,2:T(2,128)}, u32[]{:S(2)}) copy-start(f32[96,2,1,2]{0,3,1,2:T(2,128)} %copy-done.21) | copy-start | bytes 4612
  225.0 8.8 %copy-start.19 = (bf16[1,96,2,128]{3,2,1,0:T(2,128)(2,1)S(1)}, bf16[1,96,2,128]{3,2,1,0:T(2,128)(2,1)}, u32[]{:S(2)}) copy-start(bf16[1,96,2,128]{3,2,1,0:T(2,128)(2,1)} %slice.241) | copy-start | bytes 147460
  225.0 8.8 %copy-start.20 = (bf16[96,2,128]{2,1,0:T(2,128)(2,1)S(1)}, bf16[96,2,128]{2,1,0:T(2,128)(2,1)}, u32[]{:S(2)}) copy-start(bf16[96,2,128]{2,1,0:T(2,128)(2,1)} %gather_fusion.5) | copy-start | bytes 147460
  226.7 7.6 %copy-start.18 = (f32[96,2]{1,0:T(8,128)S(1)}, f32[96,2]{1,0:T(8,128)}, u32[]{:S(2)}) copy-start(f32[96,2]{1,0:T(8,128)} %fusion.96) | copy-start | bytes 2308
  226.7 7.7 %copy-start.15 = (bf16[96,2,128]{2,1,0:T(2,128)(2,1)S(1)}, bf16[96,2,128]{2,1,0:T(2,128)(2,1)}, u32[]{:S(2)}) copy-start(bf16[96,2,128]{2,1,0:T(2,128)(2,1)} %reshape.686) | copy-start | bytes 147460
  229.4 22.1 %copy-start.31 = (bf16[1024,512]{1,0:T(8,128)(2,1)S(1)}, bf16[1024,512]{1,0:T(8,128)(2,1)}, u32[]{:S(2)}) copy-start(bf16[1024,512]{1,0:T(8,128)(2,1)} %param.17) | copy-start | bytes 3145732
  251.5 16.3 %copy-start.17 = (bf16[256,512]{1,0:T(8,128)(2,1)S(1)}, bf16[256,512]{1,0:T(8,128)(2,1)}, u32[]{:S(2)}) copy-start(bf16[256,512]{1,0:T(8,128)(2,1)} %param.16) | copy-start | bytes 786436
  267.9 37.1 %copy-start.16 = (bf16[2,48,512]{2,1,0:T(8,128)(2,1)S(1)}, bf16[2,48,512]{2,1,0:T(8,128)(2,1)}, u32[]{:S(2)}) copy-start(bf16[2,48,512]{2,1,0:T(8,128)(2,1)} %x_ref.1) | copy-start | bytes 294916
  269.6 43.8 %copy-start.23 = (f32[1,512]{1,0:T(1,128)S(1)}, f32[1,512]{1,0:T(1,128)}, u32[]{:S(2)}) copy-start(f32[1,512]{1,0:T(1,128)} %get-tuple-element.54) | copy-start | bytes 6148
  269.6 79.3 %copy-start.32 = (bf16[512,768]{1,0:T(8,128)(2,1)S(1)}, bf16[512,768]{1,0:T(8,128)(2,1)}, u32[]{:S(2)}) copy-start(bf16[512,768]{1,0:T(8,128)(2,1)} %param.18) | copy-start | bytes 2359300
  305.1 48.1 %copy-start.12 = (bf16[2,48,512]{2,1,0:T(8,128)(2,1)}, bf16[2,48,512]{2,1,0:T(8,128)(2,1)S(1)}, u32[]{:S(2)}) copy-start(bf16[2,48,512]{2,1,0:T(8,128)(2,1)S(1)} %get-tuple-element.7) | copy-start | bytes 294916
  348.9 41.6 %copy-start.1 = (bf16[512,1024]{1,0:T(8,128)(2,1)S(1)}, bf16[512,1024]{1,0:T(8,128)(2,1)}, u32[]{:S(2)}) copy-start(bf16[512,1024]{1,0:T(8,128)(2,1)} %param.15) | copy-start | bytes 3145732
  (4 other events, 6.3 us)
Sparse Core Ops, SparseCore 0:
  64.6 81.7 all-reduce.2
  353.3 35.3 reduce-scatter.1

commit v7 on v6

--- a/solution.py
+++ b/solution.py
@@ -30,6 +30,13 @@
     turned = vectors[..., :ROT]
     swapped = jnp.concatenate([-turned[..., half:], turned[..., :half]], axis=-1)
     return jnp.concatenate([turned * cosine + swapped * sine, vectors[..., ROT:]], axis=-1)
+
+
+def pick_rows(table, index):
+    flat = table.reshape(table.shape[0], -1)
+    hot = (index.reshape(-1)[:, None] == jnp.arange(table.shape[0], dtype=jnp.int32)[None, :])
+    taken = jnp.dot(hot.astype(table.dtype), flat, preferred_element_type=jnp.float32)
+    return taken.astype(table.dtype).reshape(index.shape + table.shape[1:])
 
 
 def rotate_rows(rows, positions, head_count):
@@ -178,12 +185,18 @@
     partial_sums = jnp.concatenate([first, second], axis=1)
     summed_all = lax.psum(partial_sums.astype(jnp.bfloat16), "req")
     width = head_count * HD
-    activated_all = jax.nn.gelu(
-        summed_all[:, triple_width:].astype(jnp.float32), approximate=False
-    ).astype(jnp.bfloat16)
+    activated_all = lax.optimization_barrier(
+        jax.nn.gelu(summed_all[:, triple_width:].astype(jnp.float32), approximate=False).astype(
+            jnp.bfloat16
+        )
+    )
     row = jnp.arange(steps * beam_total, dtype=jnp.int32)
-    row_beam = (row // (steps * local_rows)) * local_rows + row % local_rows
-    row_positions = lengths[row_beam // BEAM] + (row // local_rows) % steps
+    beam_lengths = jnp.broadcast_to(lengths[:, None], (request_count, BEAM)).reshape(
+        mlp_size, 1, local_rows
+    )
+    row_positions = (
+        beam_lengths + jnp.arange(steps, dtype=jnp.int32)[None, :, None]
+    ).reshape(steps * beam_total)
     queries_rows = rotate_rows(
         summed_all[:, :width].astype(jnp.float32), row_positions, head_count
     ).astype(jnp.bfloat16)
@@ -210,7 +223,7 @@
         + jnp.arange(steps, dtype=jnp.int32)[:, None, None] * local_rows
         + gather_rows % local_rows
     )
-    chosen = queries_rows[chosen_rows]
+    chosen = pick_rows(queries_rows, chosen_rows)
     head_scores = [
         jnp.einsum(
             "zsbd,std->zsbt",
@@ -255,30 +268,43 @@
     page_out = jnp.einsum(
         "sr,zsbhd->zrbhd", owner_float, slot_out * factor[..., None], precision=highest
     ).reshape(steps, beam_total, head_count, HD)
+    stats = jnp.concatenate(
+        [
+            page_total.astype(jnp.bfloat16),
+            top_high.reshape(steps, beam_total, head_count),
+            top_low.reshape(steps, beam_total, head_count),
+        ],
+        axis=-1,
+    )
     packed = jnp.concatenate(
         [
-            page_out.astype(jnp.bfloat16),
-            page_total.astype(jnp.bfloat16)[..., None],
-            top_high.reshape(steps, beam_total, head_count, 1),
-            top_low.reshape(steps, beam_total, head_count, 1),
+            page_out.astype(jnp.bfloat16).reshape(steps, beam_total, head_count * HD),
+            jnp.pad(stats, ((0, 0), (0, 0), (0, HD - 3 * head_count))),
         ],
         axis=-1,
     )
-    packed = packed.reshape(steps, req_size, own_count, head_count, HD + 3).transpose(
-        1, 0, 2, 3, 4
-    )
-    held = exchange_flat(packed, "req", req_size, False, 5).astype(jnp.float32)
-    held_top = held[..., HD + 1] + held[..., HD + 2]
+    packed = packed.reshape(steps, req_size, own_count, -1).transpose(1, 0, 2, 3)
+    held = exchange(packed, "req", req_size, False, 5).astype(jnp.float32)
+    base = head_count * HD
+    held_top = held[..., base + head_count : base + 2 * head_count] + held[
+        ..., base + 2 * head_count : base + 3 * head_count
+    ]
     own_top = jnp.max(held_top, axis=0)
     rescale = jnp.exp(held_top - own_top)
-    own_out = jnp.sum(held[..., :HD] * rescale[..., None], axis=0)
-    own_total = jnp.sum(held[..., HD] * rescale, axis=0)
+    own_total = jnp.sum(held[..., base : base + head_count] * rescale, axis=0)
+    own_out = jnp.stack(
+        [
+            jnp.sum(held[..., head * HD : (head + 1) * HD] * rescale[..., head : head + 1], axis=0)
+            for head in range(head_count)
+        ],
+        axis=2,
+    )
 
     source = own_group * BEAM + parents[0]
     attended_steps = []
     for step_index in range(steps):
-        tail_keys = [keys_new[prior][source] for prior in range(step_index)]
-        tail_values = [values_new[prior][source] for prior in range(step_index)]
+        tail_keys = [pick_rows(keys_new[prior], source) for prior in range(step_index)]
+        tail_values = [pick_rows(values_new[prior], source) for prior in range(step_index)]
         history_keys = jnp.stack(tail_keys + [keys_new[step_index]], axis=0)
         history_values = jnp.stack(tail_values + [values_new[step_index]], axis=0)
         own_scores = (

time: 398 us -> 380 us (0.955)
  local copies, waits for them, and re-layouts: 63.8 us -> 34.3 us
  matrix products: 40.2 us -> 22.6 us
  other arithmetic: 31.2 us -> 46.8 us
  waiting for transfers between devices: 105 us -> 114 us
  Pallas kernels: 142 us -> 146 us
    gather x4 -> x0, local copies, waits for them, and re-layouts: 17 us -> none  [the longest x1 9.03 us: shards(): row_positions = lengths[row_beam // BEAM] + row // local_rows % steps]
    convert_element_type x0 -> x2, other arithmetic: none -> 16.3 us  [the longest x1 14.7 us: shards(): jax.nn.gelu(summed_all[:, triple_width:].astype(jnp.float32), approximate...]
    dot_general x1, matrix products: 16.3 us -> 1.84 us  [shards(): jnp.dot(activated_all, down_weight, preferred_element_type=jnp.float32)]
    convert_element_type x6 -> x4, local copies, waits for them, and re-layouts: 9.75 us -> 0.91 us  [the longest x1 0.51 us: shards(): page_out.astype(jnp.bfloat16).reshape(steps, beam_total, head_count * HD)]
    psum x1, waiting for transfers between devices: 69.7 us -> 78.6 us  [shards(): summed_all = lax.psum(partial_sums.astype(jnp.bfloat16), 'req')]
    pallas_call x7, Pallas kernels: 142 us -> 146 us  [exchange(): pl.pallas_call(functools.partial(exchange_kernel, axis, n, gather), out_s...]
    slice x2 -> x3, local copies, waits for them, and re-layouts: 7.98 us -> 4.25 us  [shards(): rescale[..., head:head + 1]]
  transfers between devices with their start and end apart: 2 -> 2, of which waited for: 2 -> 2; matrix products, arithmetic and copies ran while one was open for 3% -> 1% of each run, Pallas kernels for 0% -> 0%
where the time goes in v7:
time: 380 us; the launch traced here: 379 us
  Pallas kernels  146 us (38%)
  waiting for transfers between devices  114 us (30%)
  other arithmetic  46.8 us (12%)
  local copies, waits for them, and re-layouts  34.3 us (9%)
  matrix products  22.6 us (6%)
  between operations  14.9 us (4%)
    pallas_call x7, Pallas kernels, exchange(): pl.pallas_call(functools.partial(exchange_kernel, axis, n, gather), out_s...  146 us
    psum x1, waiting for transfers between devices, shards(): summed_all = lax.psum(partial_sums.astype(jnp.bfloat16), 'req')  78.6 us
    reduce_scatter x1, waiting for transfers between devices, shards(): lax.psum_scatter(next_partial.astype(jnp.bfloat16), 'req', scatter_dimens...  35.7 us
    convert_element_type x1, other arithmetic, shards(): jax.nn.gelu(summed_all[:, triple_width:].astype(jnp.float32), approximate...  14.7 us
  transfers between devices with their start and end apart: 2, of which 2 were waited for; matrix products, arithmetic and copies ran while one was open for 1% of the time, Pallas kernels for 0%

profile of v7, /device:TPU:0, one launch (start us, length us, event | category | flops | bytes accessed | tf_op | source)
XLA Modules:
  0.0 378.8 jit_solution(2912238865565445724)
XLA Ops:
  7.2 29.2 %shard_map.131 = bf16[16,2,48,512]{3,2,1,0:T(8,128)(2,1)} custom-call(bf16[2,48,512]{2,1,0:T(8,128)(2,1)} %x_ref.1), custom_call_target="tpu_custom_call" | custom-call | bytes 3145728 | tf_op jit(solution)/shard_map/pallas_call | solution.py:87
  36.5 1.8 convert_reduce_fusion.1
  38.3 2.1 multiply_reduce_fusion
  41.3 8.9 %shard_map.132 = f32[8,24,128]{2,1,0:T(8,128)} custom-call(f32[24,128]{1,0:T(8,128)} %reshape.489.x_ref), custom_call_target="tpu_custom_call" | custom-call | bytes 196608 | tf_op jit(solution)/shard_map/pallas_call | solution.py:87
  52.1 1.4 copy.171
  54.8 1.4 convolution_convert_fusion.2
  56.2 1.8 convolution_convert_fusion
  58.0 2.8 pad_maximum_fusion
  64.2 78.6 %all-reduce.4.cloned.1.call-done = bf16[1536,1792]{0,1:T(8,128)(2,1)} async-done(((bf16[1536,1792]{0,1:T(8,128)(2,1)}), bf16[1536,1792]{0,1:T(8,128)(2,1)}) %all-reduce.4.cloned.1.call-update) | async-done | bytes 5505040 | tf_op jit(solution)/shard_map/psum | solution.py:186
  142.7 2.8 fusion.141
  146.5 2.1 fusion.142
  153.0 1.2 fusion.54
  155.7 2.7 fusion.57
  164.9 17.6 %shard_map.133 = bf16[8,2,96,384]{3,2,1,0:T(8,128)(2,1)} custom-call(bf16[8,2,96,384]{3,2,1,0:T(8,128)(2,1)} %copy_bitcast_fusion.x_ref), custom_call_target="tpu_custom_call" | custom-call | bytes 18874368 | tf_op jit(solution)/shard_map/pallas_call | solution.py:87
  182.7 1.6 convert_element_type.171
  192.7 1.5 fusion.145
  208.0 1.4 fusion.143
  209.4 1.4 copy.190
  210.9 1.4 copy.192
  213.3 1.2 fusion.104
  216.5 15.1 %shard_map.134 = bf16[8,2,96,256]{3,2,1,0:T(8,128)(2,1)} custom-call(bf16[2,96,256]{2,1,0:T(8,128)(2,1)} %pad_maximum_fusion.8.x_ref), custom_call_target="tpu_custom_call" | custom-call | bytes 1572864 | tf_op jit(solution)/shard_map/pallas_call | solution.py:87
  231.6 1.2 copy.201
  232.9 14.7 %fusion.1 = bf16[1536,1024]{0,1:T(8,128)(2,1)S(1)} fusion(bf16[1536,1792]{0,1:T(8,128)(2,1)} %all-reduce.4.cloned.1.call-done), kind=kLoop, calls=%fused_computation.6 | loop fusion | flops 103809024 | bytes 6291456 | tf_op jit(solution)/shard_map/convert_element_type | solution.py:189
  247.6 1.8 fusion.148
  249.5 1.7 fusion.36
  251.2 33.4 %shard_map.135 = bf16[16,96,512]{2,1,0:T(8,128)(2,1)} custom-call(bf16[16,96,512]{2,1,0:T(8,128)(2,1)} %bitcast.263), custom_call_target="tpu_custom_call" | custom-call | bytes 50331648 | tf_op jit(solution)/shard_map/pallas_call | solution.py:87
  284.6 1.6 convert_reduce_fusion
  287.3 6.7 %shard_map.136 = f32[8,2,128]{2,1,0:T(2,128)} custom-call(f32[2,128]{1,0:T(2,128)} %pad_bitcast_fusion.x_ref), custom_call_target="tpu_custom_call" | custom-call | bytes 16384 | tf_op jit(solution)/shard_map/pallas_call | solution.py:87
  295.5 34.7 %shard_map.137 = bf16[16,2,48,512]{3,2,1,0:T(8,128)(2,1)} custom-call(bf16[2,48,512]{2,1,0:T(8,128)(2,1)} %fusion.79.x_ref), custom_call_target="tpu_custom_call" | custom-call | bytes 3145728 | tf_op jit(solution)/shard_map/pallas_call | solution.py:87
  330.3 4.3 %convolution_convert_fusion.1 = bf16[1536,768]{1,0:T(8,128)(2,1)} fusion(bf16[1536,512]{1,0:T(8,128)(2,1)} %bitcast.268, bf16[512,768]{1,0:T(8,128)(2,1)S(1)} %copy-done.28), kind=kOutput, calls=%fused_computation.40 | convolution fusion | flops 1209139200 | bytes 4718592 | tf_op jit(solution)/shard_map/dot_general | solution.py:356
  334.6 35.7 %reduce-scatter.2.cloned.1.call-done = bf16[192,768]{1,0:T(8,128)(2,1)} async-done(((bf16[1536,768]{1,0:T(8,128)(2,1)}), bf16[192,768]{1,0:T(8,128)(2,1)}) %reduce-scatter.2.cloned.1.call-update) | async-done | bytes 294928 | tf_op jit(solution)/shard_map/reduce_scatter | solution.py:357
  370.3 1.7 copy.202
  (190 shorter events, 48.0 us)
Async XLA Ops:
  7.2 49.0 %copy-start = (bf16[512,1024]{1,0:T(8,128)(2,1)S(1)}, bf16[512,1024]{1,0:T(8,128)(2,1)}, u32[]{:S(2)}) copy-start(bf16[512,1024]{1,0:T(8,128)(2,1)} %param.15) | copy-start | bytes 3145732
  7.2 44.4 %copy-start.24 = (f32[3,512]{1,0:T(4,128)S(1)}, f32[3,512]{1,0:T(4,128)}, u32[]{:S(2)}) copy-start(f32[3,512]{1,0:T(4,128)} %param.13) | copy-start | bytes 18436
  7.2 135.6 %all-reduce.4.cloned.1.call-start = ((), (), s32[]{:S(2)}) async-start(), calls=%async_computation.1 | async-start | bytes 11010048 | tf_op jit(solution)/shard_map/psum | solution.py:186
  36.5 17.2 %copy-start.3 = (bf16[16,2,48,512]{3,2,1,0:T(8,128)(2,1)S(1)}, bf16[16,2,48,512]{3,2,1,0:T(8,128)(2,1)}, u32[]{:S(2)}) copy-start(bf16[16,2,48,512]{3,2,1,0:T(8,128)(2,1)} %shard_map.131) | copy-start | bytes 4718596
  60.9 0.7 copy-start.2
  60.9 1.0 copy-start.26
  60.9 2.1 copy-start.29
  60.9 309.4 %reduce-scatter.2.cloned.1.call-start = ((), (), s32[]{:S(2)}) async-start(), calls=%async_computation.2 | async-start | bytes 2654208 | tf_op jit(solution)/shard_map/reduce_scatter | solution.py:357
  64.2 82.3 %copy-start.9 = (f32[1536,16]{0,1:T(8,128)}, f32[1536,16]{0,1:T(8,128)S(1)}, u32[]{:S(2)}) copy-start(f32[1536,16]{0,1:T(8,128)S(1)} %get-tuple-element.55) | copy-start | bytes 294916
  145.6 3.1 copy-start.6
  149.6 2.2 copy-start.4
  154.8 3.5 copy-start.5
  182.6 3.3 copy-start.10
  182.6 3.3 copy-start.13
  182.6 3.3 copy-start.14
  182.6 3.3 copy-start.15
  182.6 3.3 copy-start.16
  182.6 4.4 %copy-start.7 = (bf16[1536,96]{0,1:T(8,128)(2,1)S(1)}, bf16[1536,96]{0,1:T(8,128)(2,1)}, u32[]{:S(2)}) copy-start(bf16[1536,96]{0,1:T(8,128)(2,1)} %get-tuple-element.19) | copy-start | bytes 884740
  182.6 4.4 %copy-start.8 = (bf16[1536,96]{0,1:T(8,128)(2,1)S(1)}, bf16[1536,96]{0,1:T(8,128)(2,1)}, u32[]{:S(2)}) copy-start(bf16[1536,96]{0,1:T(8,128)(2,1)} %get-tuple-element.20) | copy-start | bytes 884740
  184.3 5.1 %copy-start.25 = (s32[96]{0:T(128)S(1)}, s32[96]{0:T(128)}, u32[]{:S(2)}) copy-start(s32[96]{0:T(128)} %fusion.137) | copy-start | bytes 1156
  187.0 16.4 %copy-start.12 = (f32[2,96,2]{2,1,0:T(8,128)S(1)}, f32[2,96,2]{2,1,0:T(8,128)}, u32[]{:S(2)}) copy-start(f32[2,96,2]{2,1,0:T(8,128)} %get-tuple-element.12) | copy-start | bytes 4612
  208.0 4.4 %copy-start.22 = (bf16[1,96,2,128]{3,2,1,0:T(2,128)(2,1)S(1)}, bf16[1,96,2,128]{3,2,1,0:T(2,128)(2,1)}, u32[]{:S(2)}) copy-start(bf16[1,96,2,128]{3,2,1,0:T(2,128)(2,1)} %stack_reshape.14) | copy-start | bytes 147460
  208.0 7.0 %copy-start.19 = (f32[96,2]{1,0:T(8,128)S(1)}, f32[96,2]{1,0:T(8,128)}, u32[]{:S(2)}) copy-start(f32[96,2]{1,0:T(8,128)} %get-tuple-element.45) | copy-start | bytes 2308
  208.0 7.0 %copy-start.20 = (f32[96,2]{1,0:T(8,128)S(1)}, f32[96,2]{1,0:T(8,128)}, u32[]{:S(2)}) copy-start(f32[96,2]{1,0:T(8,128)} %copy.198) | copy-start | bytes 2308
  208.0 7.0 %copy-start.21 = (f32[96,2]{1,0:T(8,128)S(1)}, f32[96,2]{1,0:T(8,128)}, u32[]{:S(2)}) copy-start(f32[96,2]{1,0:T(8,128)} %copy.200) | copy-start | bytes 2308
  216.5 31.1 %copy-start.27 = (bf16[1024,512]{1,0:T(8,128)(2,1)S(1)}, bf16[1024,512]{1,0:T(8,128)(2,1)}, u32[]{:S(2)}) copy-start(bf16[1024,512]{1,0:T(8,128)(2,1)} %param.17) | copy-start | bytes 3145732
  247.6 1.9 copy-start.18
  249.4 36.8 %copy-start.17 = (bf16[2,48,512]{2,1,0:T(8,128)(2,1)S(1)}, bf16[2,48,512]{2,1,0:T(8,128)(2,1)}, u32[]{:S(2)}) copy-start(bf16[2,48,512]{2,1,0:T(8,128)(2,1)} %x_ref.1) | copy-start | bytes 294916
  251.2 43.6 %copy-start.23 = (f32[1,512]{1,0:T(1,128)S(1)}, f32[1,512]{1,0:T(1,128)}, u32[]{:S(2)}) copy-start(f32[1,512]{1,0:T(1,128)} %get-tuple-element.56) | copy-start | bytes 6148
  251.2 79.1 %copy-start.28 = (bf16[512,768]{1,0:T(8,128)(2,1)S(1)}, bf16[512,768]{1,0:T(8,128)(2,1)}, u32[]{:S(2)}) copy-start(bf16[512,768]{1,0:T(8,128)(2,1)} %param.18) | copy-start | bytes 2359300
  286.4 48.2 %copy-start.11 = (bf16[2,48,512]{2,1,0:T(8,128)(2,1)}, bf16[2,48,512]{2,1,0:T(8,128)(2,1)S(1)}, u32[]{:S(2)}) copy-start(bf16[2,48,512]{2,1,0:T(8,128)(2,1)S(1)} %get-tuple-element.9) | copy-start | bytes 294916
  330.3 41.7 %copy-start.1 = (bf16[512,1024]{1,0:T(8,128)(2,1)S(1)}, bf16[512,1024]{1,0:T(8,128)(2,1)}, u32[]{:S(2)}) copy-start(bf16[512,1024]{1,0:T(8,128)(2,1)} %param.15) | copy-start | bytes 3145732
Sparse Core Ops, SparseCore 0:
  61.0 81.6 all-reduce.3
  334.7 35.5 reduce-scatter.1

commit v8 on v7

--- a/solution.py
+++ b/solution.py
@@ -80,6 +80,68 @@
     for copy in copies:
         copy.wait()
     local.wait()
+
+
+def exchange_gelu_kernel(axis, n, x_ref, hidden_ref, out_ref, act_ref, send_sem, recv_sem, local_sem):
+    me = lax.axis_index(axis)
+    barrier = pltpu.get_barrier_semaphore()
+    for k in range(1, n):
+        pl.semaphore_signal(
+            barrier, inc=1, device_id={axis: lax.rem(me + k, n)}, device_id_type=MESH
+        )
+    pl.semaphore_wait(barrier, n - 1)
+    local = pltpu.make_async_copy(x_ref.at[me], out_ref.at[me], local_sem)
+    local.start()
+    copies = []
+    for k in range(1, n):
+        dest = lax.rem(me + k, n)
+        copy = pltpu.make_async_remote_copy(
+            src_ref=x_ref.at[dest],
+            dst_ref=out_ref.at[me],
+            send_sem=send_sem.at[k],
+            recv_sem=recv_sem.at[k],
+            device_id={axis: dest},
+            device_id_type=MESH,
+        )
+        copy.start()
+        copies.append(copy)
+    tile = 128
+
+    @pl.loop(0, hidden_ref.shape[0] // tile)
+    def _(index):
+        rows = pl.ds(pl.multiple_of(index * tile, tile), tile)
+        values = hidden_ref[rows, :].astype(jnp.float32)
+        gelu = 0.5 * values * (1.0 + lax.erf(values * (1.0 / math.sqrt(2.0))))
+        act_ref[rows, :] = gelu.astype(act_ref.dtype)
+
+    for copy in copies:
+        copy.wait()
+    local.wait()
+
+
+def exchange_gelu(x, hidden, axis, n, collective_id):
+    return pl.pallas_call(
+        functools.partial(exchange_gelu_kernel, axis, n),
+        out_shape=(
+            jax.ShapeDtypeStruct(x.shape, x.dtype),
+            jax.ShapeDtypeStruct(hidden.shape, jnp.bfloat16),
+        ),
+        in_specs=[pl.BlockSpec(memory_space=pltpu.VMEM)] * 2,
+        out_specs=(pl.BlockSpec(memory_space=pltpu.VMEM),) * 2,
+        scratch_shapes=[
+            pltpu.SemaphoreType.DMA((n,)),
+            pltpu.SemaphoreType.DMA((n,)),
+            pltpu.SemaphoreType.DMA(()),
+        ],
+        compiler_params=pltpu.CompilerParams(
+            collective_id=collective_id, has_side_effects=True
+        ),
+        cost_estimate=pl.CostEstimate(
+            flops=20 * hidden.size,
+            transcendentals=hidden.size,
+            bytes_accessed=2 * n * x.size * x.dtype.itemsize + 4 * hidden.size,
+        ),
+    )(x, hidden)
 
 
 def exchange(x, axis, n, gather, collective_id):
@@ -185,11 +247,6 @@
     partial_sums = jnp.concatenate([first, second], axis=1)
     summed_all = lax.psum(partial_sums.astype(jnp.bfloat16), "req")
     width = head_count * HD
-    activated_all = lax.optimization_barrier(
-        jax.nn.gelu(summed_all[:, triple_width:].astype(jnp.float32), approximate=False).astype(
-            jnp.bfloat16
-        )
-    )
     row = jnp.arange(steps * beam_total, dtype=jnp.int32)
     beam_lengths = jnp.broadcast_to(lengths[:, None], (request_count, BEAM)).reshape(
         mlp_size, 1, local_rows
@@ -284,7 +341,8 @@
         axis=-1,
     )
     packed = packed.reshape(steps, req_size, own_count, -1).transpose(1, 0, 2, 3)
-    held = exchange(packed, "req", req_size, False, 5).astype(jnp.float32)
+    held, activated_all = exchange_gelu(packed, summed_all[:, triple_width:], "req", req_size, 5)
+    held = held.astype(jnp.float32)
     base = head_count * HD
     held_top = held[..., base + head_count : base + 2 * head_count] + held[
         ..., base + 2 * head_count : base + 3 * head_count

time: 380 us -> 375 us (0.987)
  other arithmetic: 46.8 us -> 29.8 us
  local copies, waits for them, and re-layouts: 34.3 us -> 40.9 us
    pallas_call x0 -> x1, Pallas kernels: none -> 19.5 us  [exchange_gelu(): pl.pallas_call(functools.partial(exchange_gelu_kernel, axis, n), out_shap...]
    pallas_call x7 -> x6, Pallas kernels: 146 us -> 128 us  [exchange(): pl.pallas_call(functools.partial(exchange_kernel, axis, n, gather), out_s...]
    convert_element_type x2 -> x1, other arithmetic: 16.3 us -> 1.5 us  [shards(): held = held.astype(jnp.float32)]
where the time goes in v8:
time: 375 us; the launch traced here: 373 us
  Pallas kernels  147 us (39%)
  waiting for transfers between devices  114 us (30%)
  local copies, waits for them, and re-layouts  40.9 us (11%)
  other arithmetic  29.8 us (8%)
  matrix products  26.4 us (7%)
  between operations  14.9 us (4%)
    pallas_call x6, Pallas kernels, exchange(): pl.pallas_call(functools.partial(exchange_kernel, axis, n, gather), out_s...  128 us
    psum x1, waiting for transfers between devices, shards(): summed_all = lax.psum(partial_sums.astype(jnp.bfloat16), 'req')  78 us
    reduce_scatter x1, waiting for transfers between devices, shards(): lax.psum_scatter(next_partial.astype(jnp.bfloat16), 'req', scatter_dimens...  36 us
    pallas_call x1, Pallas kernels, exchange_gelu(): pl.pallas_call(functools.partial(exchange_gelu_kernel, axis, n), out_shap...  19.5 us
  transfers between devices with their start and end apart: 2, of which 2 were waited for; matrix products, arithmetic and copies ran while one was open for 1% of the time, Pallas kernels for 0%

profile of v8, /device:TPU:0, one launch (start us, length us, event | category | flops | bytes accessed | tf_op | source)
XLA Modules:
  0.0 373.4 jit_solution(4332702770467783123)
XLA Ops:
  7.2 29.2 %shard_map.131 = bf16[16,2,48,512]{3,2,1,0:T(8,128)(2,1)} custom-call(bf16[2,48,512]{2,1,0:T(8,128)(2,1)} %x_ref.1), custom_call_target="tpu_custom_call" | custom-call | bytes 3145728 | tf_op jit(solution)/shard_map/pallas_call | solution.py:149
  36.5 1.8 convert_reduce_fusion.1
  39.8 1.4 copy.204
  42.8 8.9 %shard_map.132 = f32[8,24,128]{2,1,0:T(8,128)} custom-call(f32[24,128]{1,0:T(8,128)} %reshape.489.x_ref), custom_call_target="tpu_custom_call" | custom-call | bytes 196608 | tf_op jit(solution)/shard_map/pallas_call | solution.py:149
  54.8 1.4 convolution_convert_fusion.2
  56.2 1.8 convolution_convert_fusion
  58.0 2.9 pad_maximum_fusion
  64.8 78.0 %all-reduce.4.cloned.1.call-done = bf16[1536,1792]{1,0:T(8,128)(2,1)} async-done(((bf16[1536,1792]{1,0:T(8,128)(2,1)}), bf16[1536,1792]{1,0:T(8,128)(2,1)}) %all-reduce.4.cloned.1.call-update) | async-done | bytes 5505040 | tf_op jit(solution)/shard_map/psum | solution.py:248
  142.9 2.9 fusion.107
  146.8 1.8 fusion.41
  148.6 2.8 fusion.108
  158.9 2.2 fusion.29
  161.2 2.4 fusion.26
  170.0 2.1 slice.279.hidden_ref
  172.2 19.5 %shard_map.133 = (bf16[8,2,96,384]{3,2,1,0:T(8,128)(2,1)}, bf16[1536,1024]{1,0:T(8,128)(2,1)}) custom-call(bf16[8,2,96,384]{3,2,1,0:T(8,128)(2,1)} %copy_bitcast_fusion.x_ref, bf16[1536,1024]{1,0:T(8,128)(2,1)} %slice.279.hidden_ref), custom_call_target="tpu_custom_call" | custom-call | flops 31457280 | bytes 25165824 | tf_op jit(solution)/shard_map/pallas_call | solution.py:123
  191.7 1.5 convert_element_type.165
  197.3 1.6 reshape.510
  200.3 1.4 stack_reshape.14
  203.3 1.4 slice.252
  206.2 1.4 stack_reshape.13
  217.8 1.4 copy.231
  219.2 1.4 copy.229
  224.0 15.0 %shard_map.134 = bf16[8,2,96,256]{3,2,1,0:T(8,128)(2,1)} custom-call(bf16[2,96,256]{2,1,0:T(8,128)(2,1)} %pad_maximum_fusion.8.x_ref), custom_call_target="tpu_custom_call" | custom-call | bytes 1572864 | tf_op jit(solution)/shard_map/pallas_call | solution.py:149
  240.2 3.7 %fusion.114 = f32[1536,512]{1,0:T(8,128)S(1)} fusion(bf16[1536,1024]{1,0:T(8,128)(2,1)} %get-tuple-element.5, bf16[1024,512]{1,0:T(8,128)(2,1)S(1)} %copy-done.20), kind=kOutput, calls=%fused_computation.227 | convolution fusion | flops 1610612736 | bytes 7340032 | tf_op jit(solution)/shard_map/dot_general | solution.py:399
  244.0 1.7 fusion.5
  245.7 33.4 %shard_map.135 = bf16[16,96,512]{2,1,0:T(8,128)(2,1)} custom-call(bf16[16,96,512]{2,1,0:T(8,128)(2,1)} %bitcast.266), custom_call_target="tpu_custom_call" | custom-call | bytes 50331648 | tf_op jit(solution)/shard_map/pallas_call | solution.py:149
  279.1 1.7 convert_reduce_fusion
  281.8 6.7 %shard_map.136 = f32[8,2,128]{2,1,0:T(2,128)} custom-call(f32[2,128]{1,0:T(2,128)} %pad_bitcast_fusion.x_ref), custom_call_target="tpu_custom_call" | custom-call | bytes 16384 | tf_op jit(solution)/shard_map/pallas_call | solution.py:149
  290.1 34.4 %shard_map.137 = bf16[16,2,48,512]{3,2,1,0:T(8,128)(2,1)} custom-call(bf16[2,48,512]{2,1,0:T(8,128)(2,1)} %fusion.56.x_ref), custom_call_target="tpu_custom_call" | custom-call | bytes 3145728 | tf_op jit(solution)/shard_map/pallas_call | solution.py:149
  324.6 4.3 %convolution_convert_fusion.1 = bf16[1536,768]{1,0:T(8,128)(2,1)} fusion(bf16[1536,512]{1,0:T(8,128)(2,1)} %bitcast.271, bf16[512,768]{1,0:T(8,128)(2,1)S(1)} %copy-done.21), kind=kOutput, calls=%fused_computation.6 | convolution fusion | flops 1209139200 | bytes 4718592 | tf_op jit(solution)/shard_map/dot_general | solution.py:414
  328.9 36.0 %reduce-scatter.2.cloned.1.call-done = bf16[192,768]{1,0:T(8,128)(2,1)} async-done(((bf16[1536,768]{1,0:T(8,128)(2,1)}), bf16[192,768]{1,0:T(8,128)(2,1)}) %reduce-scatter.2.cloned.1.call-update) | async-done | bytes 294928 | tf_op jit(solution)/shard_map/reduce_scatter | solution.py:415
  364.9 1.7 copy.242
  (180 shorter events, 50.3 us)
Async XLA Ops:
  7.2 49.1 %copy-start = (bf16[512,1024]{1,0:T(8,128)(2,1)S(1)}, bf16[512,1024]{1,0:T(8,128)(2,1)}, u32[]{:S(2)}) copy-start(bf16[512,1024]{1,0:T(8,128)(2,1)} %param.15) | copy-start | bytes 3145732
  7.2 32.0 %copy-start.17 = (f32[3,512]{1,0:T(4,128)S(1)}, f32[3,512]{1,0:T(4,128)}, u32[]{:S(2)}) copy-start(f32[3,512]{1,0:T(4,128)} %param.13) | copy-start | bytes 18436
  7.2 135.7 %all-reduce.4.cloned.1.call-start = ((), (), s32[]{:S(2)}) async-start(), calls=%async_computation.1 | async-start | bytes 11010048 | tf_op jit(solution)/shard_map/psum | solution.py:248
  36.5 1.9 copy-start.3
  53.7 1.1 copy-start.9
  60.9 0.7 copy-start.19
  60.9 0.7 copy-start.2
  61.0 3.1 copy-start.22
  61.0 303.9 %reduce-scatter.2.cloned.1.call-start = ((), (), s32[]{:S(2)}) async-start(), calls=%async_computation.2 | async-start | bytes 2654208 | tf_op jit(solution)/shard_map/reduce_scatter | solution.py:415
  151.9 1.2 copy-start.7
  151.9 2.5 copy-start.4
  158.1 0.8 copy-start.5
  161.2 8.8 %slice-start = ((s8[5505024]{0:T(1024)(128)(4,1)}), s8[1310720]{0:T(1024)(128)(4,1)S(1)}, s32[]{:S(2)}) async-start(s8[5505024]{0:T(1024)(128)(4,1)} %bitcast.264), calls=%async_computation.3 | async-start | bytes 2621440
  166.5 2.3 copy-start.6
  166.5 3.5 slice-start.1
  193.7 5.8 %copy-start.18 = (s32[96]{0:T(128)S(1)}, s32[96]{0:T(128)}, u32[]{:S(2)}) copy-start(s32[96]{0:T(128)} %fusion.103) | copy-start | bytes 1156
  199.5 13.4 %copy-start.13 = (f32[1,96,2]{2,1,0:T(8,128)S(1)}, f32[1,96,2]{2,1,0:T(8,128)}, u32[]{:S(2)}) copy-start(f32[1,96,2]{2,1,0:T(8,128)} %slice.304) | copy-start | bytes 2308
  216.4 4.3 %copy-start.14 = (bf16[1,96,2,128]{3,2,1,0:T(2,128)(2,1)S(1)}, bf16[1,96,2,128]{3,2,1,0:T(2,128)(2,1)}, u32[]{:S(2)}) copy-start(bf16[1,96,2,128]{3,2,1,0:T(2,128)(2,1)} %slice.254) | copy-start | bytes 147460
  216.4 4.3 %copy-start.15 = (bf16[1,96,2,128]{3,2,1,0:T(2,128)(2,1)S(1)}, bf16[1,96,2,128]{3,2,1,0:T(2,128)(2,1)}, u32[]{:S(2)}) copy-start(bf16[1,96,2,128]{3,2,1,0:T(2,128)(2,1)} %stack_reshape.14) | copy-start | bytes 147460
  217.8 4.8 %copy-start.11 = (f32[96,2,128]{2,1,0:T(2,128)S(1)}, f32[96,2,128]{2,1,0:T(2,128)}, u32[]{:S(2)}) copy-start(f32[96,2,128]{2,1,0:T(2,128)} %reshape.510) | copy-start | bytes 294916
  222.5 17.7 %copy-start.20 = (bf16[1024,512]{1,0:T(8,128)(2,1)S(1)}, bf16[1024,512]{1,0:T(8,128)(2,1)}, u32[]{:S(2)}) copy-start(bf16[1024,512]{1,0:T(8,128)(2,1)} %param.17) | copy-start | bytes 3145732
  240.2 3.8 %copy-start.12 = (bf16[256,512]{1,0:T(8,128)(2,1)S(1)}, bf16[256,512]{1,0:T(8,128)(2,1)}, u32[]{:S(2)}) copy-start(bf16[256,512]{1,0:T(8,128)(2,1)} %param.16) | copy-start | bytes 786436
  245.7 35.1 %copy-start.10 = (bf16[2,48,512]{2,1,0:T(8,128)(2,1)S(1)}, bf16[2,48,512]{2,1,0:T(8,128)(2,1)}, u32[]{:S(2)}) copy-start(bf16[2,48,512]{2,1,0:T(8,128)(2,1)} %x_ref.1) | copy-start | bytes 294916
  245.7 43.6 %copy-start.16 = (f32[1,512]{1,0:T(1,128)S(1)}, f32[1,512]{1,0:T(1,128)}, u32[]{:S(2)}) copy-start(f32[1,512]{1,0:T(1,128)} %get-tuple-element.62) | copy-start | bytes 6148
  279.1 45.4 %copy-start.21 = (bf16[512,768]{1,0:T(8,128)(2,1)S(1)}, bf16[512,768]{1,0:T(8,128)(2,1)}, u32[]{:S(2)}) copy-start(bf16[512,768]{1,0:T(8,128)(2,1)} %param.18) | copy-start | bytes 2359300
  281.0 47.9 %copy-start.8 = (bf16[2,48,512]{2,1,0:T(8,128)(2,1)}, bf16[2,48,512]{2,1,0:T(8,128)(2,1)S(1)}, u32[]{:S(2)}) copy-start(bf16[2,48,512]{2,1,0:T(8,128)(2,1)S(1)} %get-tuple-element.13) | copy-start | bytes 294916
  324.5 42.0 %copy-start.1 = (bf16[512,1024]{1,0:T(8,128)(2,1)S(1)}, bf16[512,1024]{1,0:T(8,128)(2,1)}, u32[]{:S(2)}) copy-start(bf16[512,1024]{1,0:T(8,128)(2,1)} %param.15) | copy-start | bytes 3145732
Sparse Core Ops, SparseCore 0:
  61.1 81.7 all-reduce.3
  329.0 35.8 reduce-scatter.1

commit v9 on v8

--- a/solution.py
+++ b/solution.py
@@ -142,6 +142,70 @@
             bytes_accessed=2 * n * x.size * x.dtype.itemsize + 4 * hidden.size,
         ),
     )(x, hidden)
+
+
+def gather_grid_kernel(axis, side, x_ref, out_ref, send_sem, recv_sem, local_sem):
+    me = lax.axis_index(axis)
+    row, col = me // side, me % side
+    row_peers = [row * side + lax.rem(col + k, side) for k in range(1, side)]
+    col_peers = [lax.rem(row + k, side) * side + col for k in range(1, side)]
+    barrier = pltpu.get_barrier_semaphore()
+    for peer in row_peers + col_peers:
+        pl.semaphore_signal(barrier, inc=1, device_id={axis: peer}, device_id_type=MESH)
+    pl.semaphore_wait(barrier, 2 * (side - 1))
+    local = pltpu.make_async_copy(x_ref, out_ref.at[me], local_sem)
+    local.start()
+    first = []
+    for k, peer in enumerate(row_peers):
+        copy = pltpu.make_async_remote_copy(
+            src_ref=x_ref,
+            dst_ref=out_ref.at[me],
+            send_sem=send_sem.at[0, k],
+            recv_sem=recv_sem.at[0, k],
+            device_id={axis: peer},
+            device_id_type=MESH,
+        )
+        copy.start()
+        first.append(copy)
+    for copy in first:
+        copy.wait()
+    local.wait()
+    slab = out_ref.at[pl.ds(row * side, side)]
+    second = []
+    for k, peer in enumerate(col_peers):
+        copy = pltpu.make_async_remote_copy(
+            src_ref=slab,
+            dst_ref=slab,
+            send_sem=send_sem.at[1, k],
+            recv_sem=recv_sem.at[1, k],
+            device_id={axis: peer},
+            device_id_type=MESH,
+        )
+        copy.start()
+        second.append(copy)
+    for copy in second:
+        copy.wait()
+
+
+def gather_grid(x, axis, n, collective_id):
+    side = math.isqrt(n)
+    return pl.pallas_call(
+        functools.partial(gather_grid_kernel, axis, side),
+        out_shape=jax.ShapeDtypeStruct((n,) + x.shape, x.dtype),
+        in_specs=[pl.BlockSpec(memory_space=pltpu.VMEM)],
+        out_specs=pl.BlockSpec(memory_space=pltpu.VMEM),
+        scratch_shapes=[
+            pltpu.SemaphoreType.DMA((2, side - 1)),
+            pltpu.SemaphoreType.DMA((2, side - 1)),
+            pltpu.SemaphoreType.DMA(()),
+        ],
+        compiler_params=pltpu.CompilerParams(
+            collective_id=collective_id, has_side_effects=True
+        ),
+        cost_estimate=pl.CostEstimate(
+            flops=0, transcendentals=0, bytes_accessed=2 * n * x.size * x.dtype.itemsize
+        ),
+    )(x)
 
 
 def exchange(x, axis, n, gather, collective_id):
@@ -233,7 +297,7 @@
     gather_rows = valid_owner[:, None] * BEAM + jnp.arange(BEAM, dtype=jnp.int32)[None, :]
 
     block = inputs.astype(jnp.float32)
-    rows_all = exchange(inputs, "mlp", mlp_size, True, 0).reshape(steps * beam_total, -1)
+    rows_all = gather_grid(inputs, "mlp", mlp_size, 0).reshape(steps * beam_total, -1)
     normed = row_normalize(rows_all.astype(jnp.float32), 3)
     attn_in = (normed * norm_gains[0]).astype(jnp.bfloat16)
     mlp_in = (normed * norm_gains[1]).astype(jnp.bfloat16)
@@ -410,7 +474,7 @@
     )
     layer = (block + update.reshape(steps, local_rows, local_width)).astype(jnp.bfloat16)
     next_in = (row_normalize(layer.astype(jnp.float32), 4) * norm_gains[2]).astype(jnp.bfloat16)
-    gathered = exchange(next_in, "mlp", mlp_size, True, 2).reshape(steps * beam_total, -1)
+    gathered = gather_grid(next_in, "mlp", mlp_size, 2).reshape(steps * beam_total, -1)
     next_partial = jnp.dot(gathered, next_weight, preferred_element_type=jnp.float32)
     next_out = lax.psum_scatter(
         next_partial.astype(jnp.bfloat16), "req", scatter_dimension=0, tiled=True

time: 375 us -> 370 us (0.987)
  waiting for transfers between devices: 114 us -> 106 us
  Pallas kernels: 147 us -> 151 us
    pallas_call x0 -> x2, Pallas kernels: none -> 67 us  [gather_grid(): pl.pallas_call(functools.partial(gather_grid_kernel, axis, side), out_sha...]
    pallas_call x6 -> x4, Pallas kernels: 128 us -> 64 us  [exchange(): pl.pallas_call(functools.partial(exchange_kernel, axis, n, gather), out_s...]
    psum x1, waiting for transfers between devices: 78 us -> 73.6 us  [shards(): summed_all = lax.psum(partial_sums.astype(jnp.bfloat16), 'req')]
    reduce_scatter x1, waiting for transfers between devices: 36 us -> 32 us  [shards(): lax.psum_scatter(next_partial.astype(jnp.bfloat16), 'req', scatter_dimens...]
where the time goes in v9:
time: 370 us; the launch traced here: 368 us
  Pallas kernels  151 us (41%)
  waiting for transfers between devices  106 us (29%)
  local copies, waits for them, and re-layouts  40.9 us (11%)
  other arithmetic  29.8 us (8%)
  matrix products  26.4 us (7%)
  between operations  14.9 us (4%)
    psum x1, waiting for transfers between devices, shards(): summed_all = lax.psum(partial_sums.astype(jnp.bfloat16), 'req')  73.6 us
    pallas_call x2, Pallas kernels, gather_grid(): pl.pallas_call(functools.partial(gather_grid_kernel, axis, side), out_sha...  67 us
    pallas_call x4, Pallas kernels, exchange(): pl.pallas_call(functools.partial(exchange_kernel, axis, n, gather), out_s...  64 us
    reduce_scatter x1, waiting for transfers between devices, shards(): lax.psum_scatter(next_partial.astype(jnp.bfloat16), 'req', scatter_dimens...  32 us
    pallas_call x1, Pallas kernels, exchange_gelu(): pl.pallas_call(functools.partial(exchange_gelu_kernel, axis, n), out_shap...  19.5 us
  transfers between devices with their start and end apart: 2, of which 2 were waited for; matrix products, arithmetic and copies ran while one was open for 1% of the time, Pallas kernels for 0%

profile of v9, /device:TPU:0, one launch (start us, length us, event | category | flops | bytes accessed | tf_op | source)
XLA Modules:
  0.0 368.4 jit_solution(2160855414680782314)
XLA Ops:
  7.2 30.9 %shard_map.131 = bf16[16,2,48,512]{3,2,1,0:T(8,128)(2,1)} custom-call(bf16[2,48,512]{2,1,0:T(8,128)(2,1)} %x_ref.1), custom_call_target="tpu_custom_call" | custom-call | bytes 3145728 | tf_op jit(solution)/shard_map/pallas_call | solution.py:192
  38.1 1.8 convert_reduce_fusion.1
  41.4 1.4 copy.204
  44.5 8.9 %shard_map.132 = f32[8,24,128]{2,1,0:T(8,128)} custom-call(f32[24,128]{1,0:T(8,128)} %reshape.489.x_ref), custom_call_target="tpu_custom_call" | custom-call | bytes 196608 | tf_op jit(solution)/shard_map/pallas_call | solution.py:213
  56.5 1.4 convolution_convert_fusion.2
  57.9 1.8 convolution_convert_fusion
  59.7 2.9 pad_maximum_fusion
  66.5 73.6 %all-reduce.4.cloned.1.call-done = bf16[1536,1792]{1,0:T(8,128)(2,1)} async-done(((bf16[1536,1792]{1,0:T(8,128)(2,1)}), bf16[1536,1792]{1,0:T(8,128)(2,1)}) %all-reduce.4.cloned.1.call-update) | async-done | bytes 5505040 | tf_op jit(solution)/shard_map/psum | solution.py:312
  140.1 2.9 fusion.107
  144.0 1.8 fusion.41
  145.8 2.8 fusion.108
  156.2 2.2 fusion.29
  158.4 2.4 fusion.26
  167.3 2.1 slice.279.hidden_ref
  169.4 19.5 %shard_map.133 = (bf16[8,2,96,384]{3,2,1,0:T(8,128)(2,1)}, bf16[1536,1024]{1,0:T(8,128)(2,1)}) custom-call(bf16[8,2,96,384]{3,2,1,0:T(8,128)(2,1)} %copy_bitcast_fusion.x_ref, bf16[1536,1024]{1,0:T(8,128)(2,1)} %slice.279.hidden_ref), custom_call_target="tpu_custom_call" | custom-call | flops 31457280 | bytes 25165824 | tf_op jit(solution)/shard_map/pallas_call | solution.py:123
  188.9 1.5 convert_element_type.165
  194.5 1.6 reshape.510
  197.6 1.4 stack_reshape.14
  200.6 1.4 slice.252
  203.5 1.4 stack_reshape.13
  215.0 1.4 copy.231
  216.5 1.4 copy.229
  221.2 15.0 %shard_map.134 = bf16[8,2,96,256]{3,2,1,0:T(8,128)(2,1)} custom-call(bf16[2,96,256]{2,1,0:T(8,128)(2,1)} %pad_maximum_fusion.8.x_ref), custom_call_target="tpu_custom_call" | custom-call | bytes 1572864 | tf_op jit(solution)/shard_map/pallas_call | solution.py:213
  237.5 3.7 %fusion.114 = f32[1536,512]{1,0:T(8,128)S(1)} fusion(bf16[1536,1024]{1,0:T(8,128)(2,1)} %get-tuple-element.5, bf16[1024,512]{1,0:T(8,128)(2,1)S(1)} %copy-done.20), kind=kOutput, calls=%fused_computation.227 | convolution fusion | flops 1610612736 | bytes 7340032 | tf_op jit(solution)/shard_map/dot_general | solution.py:463
  241.2 1.7 fusion.5
  243.0 33.4 %shard_map.135 = bf16[16,96,512]{2,1,0:T(8,128)(2,1)} custom-call(bf16[16,96,512]{2,1,0:T(8,128)(2,1)} %bitcast.266), custom_call_target="tpu_custom_call" | custom-call | bytes 50331648 | tf_op jit(solution)/shard_map/pallas_call | solution.py:213
  276.4 1.7 convert_reduce_fusion
  279.1 6.7 %shard_map.136 = f32[8,2,128]{2,1,0:T(2,128)} custom-call(f32[2,128]{1,0:T(2,128)} %pad_bitcast_fusion.x_ref), custom_call_target="tpu_custom_call" | custom-call | bytes 16384 | tf_op jit(solution)/shard_map/pallas_call | solution.py:213
  287.3 36.1 %shard_map.137 = bf16[16,2,48,512]{3,2,1,0:T(8,128)(2,1)} custom-call(bf16[2,48,512]{2,1,0:T(8,128)(2,1)} %fusion.56.x_ref), custom_call_target="tpu_custom_call" | custom-call | bytes 3145728 | tf_op jit(solution)/shard_map/pallas_call | solution.py:192
  323.5 4.3 %convolution_convert_fusion.1 = bf16[1536,768]{1,0:T(8,128)(2,1)} fusion(bf16[1536,512]{1,0:T(8,128)(2,1)} %bitcast.271, bf16[512,768]{1,0:T(8,128)(2,1)S(1)} %copy-done.21), kind=kOutput, calls=%fused_computation.6 | convolution fusion | flops 1209139200 | bytes 4718592 | tf_op jit(solution)/shard_map/dot_general | solution.py:478
  327.8 32.0 %reduce-scatter.2.cloned.1.call-done = bf16[192,768]{1,0:T(8,128)(2,1)} async-done(((bf16[1536,768]{1,0:T(8,128)(2,1)}), bf16[192,768]{1,0:T(8,128)(2,1)}) %reduce-scatter.2.cloned.1.call-update) | async-done | bytes 294928 | tf_op jit(solution)/shard_map/reduce_scatter | solution.py:479
  359.8 1.7 copy.242
  (180 shorter events, 50.3 us)
Async XLA Ops:
  7.2 50.7 %copy-start = (bf16[512,1024]{1,0:T(8,128)(2,1)S(1)}, bf16[512,1024]{1,0:T(8,128)(2,1)}, u32[]{:S(2)}) copy-start(bf16[512,1024]{1,0:T(8,128)(2,1)} %param.15) | copy-start | bytes 3145732
  7.2 33.7 %copy-start.17 = (f32[3,512]{1,0:T(4,128)S(1)}, f32[3,512]{1,0:T(4,128)}, u32[]{:S(2)}) copy-start(f32[3,512]{1,0:T(4,128)} %param.13) | copy-start | bytes 18436
  7.2 132.9 %all-reduce.4.cloned.1.call-start = ((), (), s32[]{:S(2)}) async-start(), calls=%async_computation.1 | async-start | bytes 11010048 | tf_op jit(solution)/shard_map/psum | solution.py:312
  38.1 1.9 copy-start.3
  55.3 1.1 copy-start.9
  62.6 0.7 copy-start.19
  62.6 0.7 copy-start.2
  62.6 3.1 copy-start.22
  62.7 297.2 %reduce-scatter.2.cloned.1.call-start = ((), (), s32[]{:S(2)}) async-start(), calls=%async_computation.2 | async-start | bytes 2654208 | tf_op jit(solution)/shard_map/reduce_scatter | solution.py:479
  149.2 1.2 copy-start.7
  149.2 2.5 copy-start.4
  155.3 0.8 copy-start.5
  158.4 8.8 %slice-start = ((s8[5505024]{0:T(1024)(128)(4,1)}), s8[1310720]{0:T(1024)(128)(4,1)S(1)}, s32[]{:S(2)}) async-start(s8[5505024]{0:T(1024)(128)(4,1)} %bitcast.264), calls=%async_computation.3 | async-start | bytes 2621440
  163.7 2.2 copy-start.6
  163.7 3.5 slice-start.1
  190.9 5.8 %copy-start.18 = (s32[96]{0:T(128)S(1)}, s32[96]{0:T(128)}, u32[]{:S(2)}) copy-start(s32[96]{0:T(128)} %fusion.103) | copy-start | bytes 1156
  196.7 13.4 %copy-start.13 = (f32[1,96,2]{2,1,0:T(8,128)S(1)}, f32[1,96,2]{2,1,0:T(8,128)}, u32[]{:S(2)}) copy-start(f32[1,96,2]{2,1,0:T(8,128)} %slice.304) | copy-start | bytes 2308
  213.6 4.3 %copy-start.14 = (bf16[1,96,2,128]{3,2,1,0:T(2,128)(2,1)S(1)}, bf16[1,96,2,128]{3,2,1,0:T(2,128)(2,1)}, u32[]{:S(2)}) copy-start(bf16[1,96,2,128]{3,2,1,0:T(2,128)(2,1)} %slice.254) | copy-start | bytes 147460
  213.6 4.3 %copy-start.15 = (bf16[1,96,2,128]{3,2,1,0:T(2,128)(2,1)S(1)}, bf16[1,96,2,128]{3,2,1,0:T(2,128)(2,1)}, u32[]{:S(2)}) copy-start(bf16[1,96,2,128]{3,2,1,0:T(2,128)(2,1)} %stack_reshape.14) | copy-start | bytes 147460
  215.0 4.8 %copy-start.11 = (f32[96,2,128]{2,1,0:T(2,128)S(1)}, f32[96,2,128]{2,1,0:T(2,128)}, u32[]{:S(2)}) copy-start(f32[96,2,128]{2,1,0:T(2,128)} %reshape.510) | copy-start | bytes 294916
  219.8 17.7 %copy-start.20 = (bf16[1024,512]{1,0:T(8,128)(2,1)S(1)}, bf16[1024,512]{1,0:T(8,128)(2,1)}, u32[]{:S(2)}) copy-start(bf16[1024,512]{1,0:T(8,128)(2,1)} %param.17) | copy-start | bytes 3145732
  237.5 3.8 %copy-start.12 = (bf16[256,512]{1,0:T(8,128)(2,1)S(1)}, bf16[256,512]{1,0:T(8,128)(2,1)}, u32[]{:S(2)}) copy-start(bf16[256,512]{1,0:T(8,128)(2,1)} %param.16) | copy-start | bytes 786436
  243.0 35.2 %copy-start.10 = (bf16[2,48,512]{2,1,0:T(8,128)(2,1)S(1)}, bf16[2,48,512]{2,1,0:T(8,128)(2,1)}, u32[]{:S(2)}) copy-start(bf16[2,48,512]{2,1,0:T(8,128)(2,1)} %x_ref.1) | copy-start | bytes 294916
  243.0 43.6 %copy-start.16 = (f32[1,512]{1,0:T(1,128)S(1)}, f32[1,512]{1,0:T(1,128)}, u32[]{:S(2)}) copy-start(f32[1,512]{1,0:T(1,128)} %get-tuple-element.62) | copy-start | bytes 6148
  276.4 47.1 %copy-start.21 = (bf16[512,768]{1,0:T(8,128)(2,1)S(1)}, bf16[512,768]{1,0:T(8,128)(2,1)}, u32[]{:S(2)}) copy-start(bf16[512,768]{1,0:T(8,128)(2,1)} %param.18) | copy-start | bytes 2359300
  278.2 49.6 %copy-start.8 = (bf16[2,48,512]{2,1,0:T(8,128)(2,1)}, bf16[2,48,512]{2,1,0:T(8,128)(2,1)S(1)}, u32[]{:S(2)}) copy-start(bf16[2,48,512]{2,1,0:T(8,128)(2,1)S(1)} %get-tuple-element.13) | copy-start | bytes 294916
  323.5 38.1 %copy-start.1 = (bf16[512,1024]{1,0:T(8,128)(2,1)S(1)}, bf16[512,1024]{1,0:T(8,128)(2,1)}, u32[]{:S(2)}) copy-start(bf16[512,1024]{1,0:T(8,128)(2,1)} %param.15) | copy-start | bytes 3145732
Sparse Core Ops, SparseCore 0:
  62.8 77.3 all-reduce.3
  327.9 31.8 reduce-scatter.1

commit v10 on v9

--- a/solution.py
+++ b/solution.py
@@ -476,9 +476,14 @@
     next_in = (row_normalize(layer.astype(jnp.float32), 4) * norm_gains[2]).astype(jnp.bfloat16)
     gathered = gather_grid(next_in, "mlp", mlp_size, 2).reshape(steps * beam_total, -1)
     next_partial = jnp.dot(gathered, next_weight, preferred_element_type=jnp.float32)
-    next_out = lax.psum_scatter(
-        next_partial.astype(jnp.bfloat16), "req", scatter_dimension=0, tiled=True
-    )
+    next_parts = exchange(
+        next_partial.astype(jnp.bfloat16).reshape(req_size, -1, next_partial.shape[1]),
+        "req",
+        req_size,
+        False,
+        7,
+    )
+    next_out = jnp.sum(next_parts.astype(jnp.float32), axis=0).astype(jnp.bfloat16)
     next_out = (
         next_out.reshape(per_own, steps, local_rows, -1)
         .transpose(1, 0, 2, 3)

time: 370 us -> 373 us (level)
  waiting for transfers between devices: 106 us -> 73.6 us
  Pallas kernels: 151 us -> 182 us
    reduce_scatter x1 -> x0, waiting for transfers between devices: 32 us -> none  [shards(): lax.psum_scatter(next_partial.astype(jnp.bfloat16), 'req', scatter_dimens...]
    pallas_call x4 -> x5, Pallas kernels: 64 us -> 94.9 us  [exchange(): pl.pallas_call(functools.partial(exchange_kernel, axis, n, gather), out_s...]
  transfers between devices with their start and end apart: 2 -> 1, of which waited for: 2 -> 1; matrix products, arithmetic and copies ran while one was open for 1% -> 1% of each run, Pallas kernels for 0% -> 0%
where the time goes in v10:
time: 373 us; the launch traced here: 368 us
  Pallas kernels  182 us (49%)
  waiting for transfers between devices  73.6 us (20%)
  local copies, waits for them, and re-layouts  39.9 us (11%)
  other arithmetic  32 us (9%)
  matrix products  26.3 us (7%)
  between operations  14.8 us (4%)
    pallas_call x5, Pallas kernels, exchange(): pl.pallas_call(functools.partial(exchange_kernel, axis, n, gather), out_s...  94.9 us
    psum x1, waiting for transfers between devices, shards(): summed_all = lax.psum(partial_sums.astype(jnp.bfloat16), 'req')  73.6 us
    pallas_call x2, Pallas kernels, gather_grid(): pl.pallas_call(functools.partial(gather_grid_kernel, axis, side), out_sha...  67.2 us
    pallas_call x1, Pallas kernels, exchange_gelu(): pl.pallas_call(functools.partial(exchange_gelu_kernel, axis, n), out_shap...  19.5 us
  transfers between devices with their start and end apart: 1, of which 1 were waited for; matrix products, arithmetic and copies ran while one was open for 1% of the time, Pallas kernels for 0%

profile of v10, /device:TPU:0, one launch (start us, length us, event | category | flops | bytes accessed | tf_op | source)
XLA Modules:
  0.0 368.4 jit_solution(3360848349296897982)
XLA Ops:
  7.2 30.9 %shard_map.131 = bf16[16,2,48,512]{3,2,1,0:T(8,128)(2,1)} custom-call(bf16[2,48,512]{2,1,0:T(8,128)(2,1)} %x_ref.1), custom_call_target="tpu_custom_call" | custom-call | bytes 3145728 | tf_op jit(solution)/shard_map/pallas_call | solution.py:192
  38.1 1.8 convert_reduce_fusion.1
  41.4 1.4 copy.202
  44.5 8.9 %shard_map.132 = f32[8,24,128]{2,1,0:T(8,128)} custom-call(f32[24,128]{1,0:T(8,128)} %reshape.492.x_ref), custom_call_target="tpu_custom_call" | custom-call | bytes 196608 | tf_op jit(solution)/shard_map/pallas_call | solution.py:213
  56.5 1.4 convolution_convert_fusion.2
  57.9 1.8 convolution_convert_fusion
  59.7 2.9 pad_maximum_fusion
  66.5 73.6 %all-reduce.4.cloned.1.call-done = bf16[1536,1792]{1,0:T(8,128)(2,1)} async-done(((bf16[1536,1792]{1,0:T(8,128)(2,1)}), bf16[1536,1792]{1,0:T(8,128)(2,1)}) %all-reduce.4.cloned.1.call-update) | async-done | bytes 5505040 | tf_op jit(solution)/shard_map/psum | solution.py:312
  140.1 2.9 fusion.107
  144.0 1.8 fusion.41
  145.8 2.8 fusion.108
  156.3 2.2 fusion.29
  158.6 2.4 fusion.26
  167.2 2.1 slice.279.hidden_ref
  169.4 19.5 %shard_map.133 = (bf16[8,2,96,384]{3,2,1,0:T(8,128)(2,1)}, bf16[1536,1024]{1,0:T(8,128)(2,1)}) custom-call(bf16[8,2,96,384]{3,2,1,0:T(8,128)(2,1)} %copy_bitcast_fusion.x_ref, bf16[1536,1024]{1,0:T(8,128)(2,1)} %slice.279.hidden_ref), custom_call_target="tpu_custom_call" | custom-call | flops 31457280 | bytes 25165824 | tf_op jit(solution)/shard_map/pallas_call | solution.py:123
  188.9 1.5 convert_element_type.167
  194.5 1.6 reshape.514
  197.5 1.4 stack_reshape.14
  200.6 1.4 slice.252
  203.4 1.4 stack_reshape.13
  215.0 1.4 copy.229
  216.4 1.4 copy.227
  221.2 15.2 %shard_map.134 = bf16[8,2,96,256]{3,2,1,0:T(8,128)(2,1)} custom-call(bf16[2,96,256]{2,1,0:T(8,128)(2,1)} %pad_maximum_fusion.8.x_ref), custom_call_target="tpu_custom_call" | custom-call | bytes 1572864 | tf_op jit(solution)/shard_map/pallas_call | solution.py:213
  237.7 3.7 %fusion.114 = f32[1536,512]{1,0:T(8,128)S(1)} fusion(bf16[1536,1024]{1,0:T(8,128)(2,1)} %get-tuple-element.5, bf16[1024,512]{1,0:T(8,128)(2,1)S(1)} %copy-done.20), kind=kOutput, calls=%fused_computation.227 | convolution fusion | flops 1610612736 | bytes 7340032 | tf_op jit(solution)/shard_map/dot_general | solution.py:463
  241.4 1.7 fusion.5
  243.1 33.4 %shard_map.135 = bf16[16,96,512]{2,1,0:T(8,128)(2,1)} custom-call(bf16[16,96,512]{2,1,0:T(8,128)(2,1)} %bitcast.267), custom_call_target="tpu_custom_call" | custom-call | bytes 50331648 | tf_op jit(solution)/shard_map/pallas_call | solution.py:213
  276.6 1.7 convert_reduce_fusion
  279.3 6.7 %shard_map.136 = f32[8,2,128]{2,1,0:T(2,128)} custom-call(f32[2,128]{1,0:T(2,128)} %pad_bitcast_fusion.x_ref), custom_call_target="tpu_custom_call" | custom-call | bytes 16384 | tf_op jit(solution)/shard_map/pallas_call | solution.py:213
  287.5 36.3 %shard_map.137 = bf16[16,2,48,512]{3,2,1,0:T(8,128)(2,1)} custom-call(bf16[2,48,512]{2,1,0:T(8,128)(2,1)} %fusion.56.x_ref), custom_call_target="tpu_custom_call" | custom-call | bytes 3145728 | tf_op jit(solution)/shard_map/pallas_call | solution.py:192
  323.8 4.2 %convolution_convert_fusion.1 = bf16[1536,768]{1,0:T(8,128)(2,1)} fusion(bf16[1536,512]{1,0:T(8,128)(2,1)} %bitcast.273, bf16[512,768]{1,0:T(8,128)(2,1)S(1)} %copy-done.21), kind=kOutput, calls=%fused_computation.6 | convolution fusion | flops 1209139200 | bytes 4718592 | tf_op jit(solution)/shard_map/dot_general | solution.py:478
  328.1 30.7 %shard_map.138 = bf16[8,192,768]{2,1,0:T(8,128)(2,1)} custom-call(bf16[8,192,768]{2,1,0:T(8,128)(2,1)} %bitcast.272), custom_call_target="tpu_custom_call" | custom-call | bytes 37748736 | tf_op jit(solution)/shard_map/pallas_call | solution.py:213
  358.8 2.1 reduce_sum.176
  (179 shorter events, 51.0 us)
Async XLA Ops:
  7.2 50.7 %copy-start = (bf16[512,1024]{1,0:T(8,128)(2,1)S(1)}, bf16[512,1024]{1,0:T(8,128)(2,1)}, u32[]{:S(2)}) copy-start(bf16[512,1024]{1,0:T(8,128)(2,1)} %param.15) | copy-start | bytes 3145732
  7.2 33.7 %copy-start.17 = (f32[3,512]{1,0:T(4,128)S(1)}, f32[3,512]{1,0:T(4,128)}, u32[]{:S(2)}) copy-start(f32[3,512]{1,0:T(4,128)} %param.13) | copy-start | bytes 18436
  7.2 132.9 %all-reduce.4.cloned.1.call-start = ((), (), s32[]{:S(2)}) async-start(), calls=%async_computation | async-start | bytes 11010048 | tf_op jit(solution)/shard_map/psum | solution.py:312
  38.1 1.9 copy-start.3
  55.3 1.1 copy-start.9
  62.6 0.7 copy-start.19
  62.6 0.7 copy-start.2
  63.3 2.5 copy-start.22
  149.2 1.2 copy-start.7
  149.2 2.5 copy-start.4
  155.5 0.8 copy-start.5
  158.6 8.6 %slice-start = ((s8[5505024]{0:T(1024)(128)(4,1)}), s8[1310720]{0:T(1024)(128)(4,1)S(1)}, s32[]{:S(2)}) async-start(s8[5505024]{0:T(1024)(128)(4,1)} %bitcast.265), calls=%async_computation.1 | async-start | bytes 2621440
  163.9 2.0 copy-start.6
  163.9 3.3 slice-start.1
  190.9 5.8 %copy-start.18 = (s32[96]{0:T(128)S(1)}, s32[96]{0:T(128)}, u32[]{:S(2)}) copy-start(s32[96]{0:T(128)} %fusion.103) | copy-start | bytes 1156
  196.7 13.4 %copy-start.13 = (f32[1,96,2]{2,1,0:T(8,128)S(1)}, f32[1,96,2]{2,1,0:T(8,128)}, u32[]{:S(2)}) copy-start(f32[1,96,2]{2,1,0:T(8,128)} %slice.304) | copy-start | bytes 2308
  213.6 4.3 %copy-start.14 = (bf16[1,96,2,128]{3,2,1,0:T(2,128)(2,1)S(1)}, bf16[1,96,2,128]{3,2,1,0:T(2,128)(2,1)}, u32[]{:S(2)}) copy-start(bf16[1,96,2,128]{3,2,1,0:T(2,128)(2,1)} %slice.254) | copy-start | bytes 147460
  213.6 4.3 %copy-start.15 = (bf16[1,96,2,128]{3,2,1,0:T(2,128)(2,1)S(1)}, bf16[1,96,2,128]{3,2,1,0:T(2,128)(2,1)}, u32[]{:S(2)}) copy-start(bf16[1,96,2,128]{3,2,1,0:T(2,128)(2,1)} %stack_reshape.14) | copy-start | bytes 147460
  215.0 4.8 %copy-start.11 = (f32[96,2,128]{2,1,0:T(2,128)S(1)}, f32[96,2,128]{2,1,0:T(2,128)}, u32[]{:S(2)}) copy-start(f32[96,2,128]{2,1,0:T(2,128)} %reshape.514) | copy-start | bytes 294916
  219.7 17.9 %copy-start.20 = (bf16[1024,512]{1,0:T(8,128)(2,1)S(1)}, bf16[1024,512]{1,0:T(8,128)(2,1)}, u32[]{:S(2)}) copy-start(bf16[1024,512]{1,0:T(8,128)(2,1)} %param.17) | copy-start | bytes 3145732
  237.6 3.8 %copy-start.12 = (bf16[256,512]{1,0:T(8,128)(2,1)S(1)}, bf16[256,512]{1,0:T(8,128)(2,1)}, u32[]{:S(2)}) copy-start(bf16[256,512]{1,0:T(8,128)(2,1)} %param.16) | copy-start | bytes 786436
  243.1 35.2 %copy-start.10 = (bf16[2,48,512]{2,1,0:T(8,128)(2,1)S(1)}, bf16[2,48,512]{2,1,0:T(8,128)(2,1)}, u32[]{:S(2)}) copy-start(bf16[2,48,512]{2,1,0:T(8,128)(2,1)} %x_ref.1) | copy-start | bytes 294916
  243.1 43.6 %copy-start.16 = (f32[1,512]{1,0:T(1,128)S(1)}, f32[1,512]{1,0:T(1,128)}, u32[]{:S(2)}) copy-start(f32[1,512]{1,0:T(1,128)} %get-tuple-element.62) | copy-start | bytes 6148
  276.6 47.3 %copy-start.21 = (bf16[512,768]{1,0:T(8,128)(2,1)S(1)}, bf16[512,768]{1,0:T(8,128)(2,1)}, u32[]{:S(2)}) copy-start(bf16[512,768]{1,0:T(8,128)(2,1)} %param.18) | copy-start | bytes 2359300
  278.4 49.6 %copy-start.8 = (bf16[2,48,512]{2,1,0:T(8,128)(2,1)}, bf16[2,48,512]{2,1,0:T(8,128)(2,1)S(1)}, u32[]{:S(2)}) copy-start(bf16[2,48,512]{2,1,0:T(8,128)(2,1)S(1)} %get-tuple-element.13) | copy-start | bytes 294916
  328.1 33.6 %copy-start.1 = (bf16[512,1024]{1,0:T(8,128)(2,1)S(1)}, bf16[512,1024]{1,0:T(8,128)(2,1)}, u32[]{:S(2)}) copy-start(bf16[512,1024]{1,0:T(8,128)(2,1)} %param.15) | copy-start | bytes 3145732
Sparse Core Ops, SparseCore 0:
  62.8 77.3 all-reduce.3

commit v11 on v9

--- a/solution.py
+++ b/solution.py
@@ -379,7 +379,7 @@
     top_low = (request_top - top_high.astype(jnp.float32)).astype(jnp.bfloat16)
     request_top = top_high.astype(jnp.float32) + top_low.astype(jnp.float32)
     factor = jnp.where(
-        slot_owner[None, :, None, None] >= 0,
+        (slot_owner[None, :, None, None] >= 0) & (slot_top > 0.5 * NEG_FILL),
         jnp.exp(slot_top - request_top[:, valid_owner]),
         0.0,
     )

time: 370 us -> 370 us (level)
  no operation moved by 1% of the time
where the time goes in v11:
time: 370 us; the launch traced here: 368 us
  Pallas kernels  151 us (41%)
  waiting for transfers between devices  106 us (29%)
  local copies, waits for them, and re-layouts  40.9 us (11%)
  other arithmetic  29.8 us (8%)
  matrix products  26.4 us (7%)
  between operations  14.9 us (4%)
    psum x1, waiting for transfers between devices, shards(): summed_all = lax.psum(partial_sums.astype(jnp.bfloat16), 'req')  73.6 us
    pallas_call x2, Pallas kernels, gather_grid(): pl.pallas_call(functools.partial(gather_grid_kernel, axis, side), out_sha...  67 us
    pallas_call x4, Pallas kernels, exchange(): pl.pallas_call(functools.partial(exchange_kernel, axis, n, gather), out_s...  64 us
    reduce_scatter x1, waiting for transfers between devices, shards(): lax.psum_scatter(next_partial.astype(jnp.bfloat16), 'req', scatter_dimens...  31.9 us
    pallas_call x1, Pallas kernels, exchange_gelu(): pl.pallas_call(functools.partial(exchange_gelu_kernel, axis, n), out_shap...  19.5 us
  transfers between devices with their start and end apart: 2, of which 2 were waited for; matrix products, arithmetic and copies ran while one was open for 1% of the time, Pallas kernels for 0%

profile of v11, /device:TPU:0, one launch (start us, length us, event | category | flops | bytes accessed | tf_op | source)
XLA Modules:
  0.0 368.3 jit_solution(8455543670892360839)
XLA Ops:
  7.2 30.9 %shard_map.131 = bf16[16,2,48,512]{3,2,1,0:T(8,128)(2,1)} custom-call(bf16[2,48,512]{2,1,0:T(8,128)(2,1)} %x_ref.1), custom_call_target="tpu_custom_call" | custom-call | bytes 3145728 | tf_op jit(solution)/shard_map/pallas_call | solution.py:192
  38.1 1.8 convert_reduce_fusion.1
  41.4 1.4 copy.207
  44.5 8.9 %shard_map.132 = f32[8,24,128]{2,1,0:T(8,128)} custom-call(f32[24,128]{1,0:T(8,128)} %reshape.491.x_ref), custom_call_target="tpu_custom_call" | custom-call | bytes 196608 | tf_op jit(solution)/shard_map/pallas_call | solution.py:213
  56.5 1.4 convolution_convert_fusion.2
  57.9 1.8 convolution_convert_fusion
  59.7 2.9 pad_maximum_fusion
  66.5 73.6 %all-reduce.4.cloned.1.call-done = bf16[1536,1792]{1,0:T(8,128)(2,1)} async-done(((bf16[1536,1792]{1,0:T(8,128)(2,1)}), bf16[1536,1792]{1,0:T(8,128)(2,1)}) %all-reduce.4.cloned.1.call-update) | async-done | bytes 5505040 | tf_op jit(solution)/shard_map/psum | solution.py:312
  140.1 2.9 fusion.107
  144.0 1.8 fusion.41
  145.8 2.8 fusion.108
  156.2 2.2 fusion.29
  158.4 2.4 fusion.26
  167.3 2.1 slice.279.hidden_ref
  169.4 19.5 %shard_map.133 = (bf16[8,2,96,384]{3,2,1,0:T(8,128)(2,1)}, bf16[1536,1024]{1,0:T(8,128)(2,1)}) custom-call(bf16[8,2,96,384]{3,2,1,0:T(8,128)(2,1)} %copy_bitcast_fusion.x_ref, bf16[1536,1024]{1,0:T(8,128)(2,1)} %slice.279.hidden_ref), custom_call_target="tpu_custom_call" | custom-call | flops 31457280 | bytes 25165824 | tf_op jit(solution)/shard_map/pallas_call | solution.py:123
  188.9 1.5 convert_element_type.165
  194.5 1.6 reshape.512
  197.6 1.4 stack_reshape.14
  200.6 1.4 slice.252
  203.5 1.4 stack_reshape.13
  215.0 1.4 copy.235
  216.5 1.4 copy.233
  221.2 15.0 %shard_map.134 = bf16[8,2,96,256]{3,2,1,0:T(8,128)(2,1)} custom-call(bf16[2,96,256]{2,1,0:T(8,128)(2,1)} %pad_maximum_fusion.8.x_ref), custom_call_target="tpu_custom_call" | custom-call | bytes 1572864 | tf_op jit(solution)/shard_map/pallas_call | solution.py:213
  237.5 3.7 %fusion.114 = f32[1536,512]{1,0:T(8,128)S(1)} fusion(bf16[1536,1024]{1,0:T(8,128)(2,1)} %get-tuple-element.5, bf16[1024,512]{1,0:T(8,128)(2,1)S(1)} %copy-done.20), kind=kOutput, calls=%fused_computation.227 | convolution fusion | flops 1610612736 | bytes 7340032 | tf_op jit(solution)/shard_map/dot_general | solution.py:463
  241.2 1.7 fusion.5
  243.0 33.4 %shard_map.135 = bf16[16,96,512]{2,1,0:T(8,128)(2,1)} custom-call(bf16[16,96,512]{2,1,0:T(8,128)(2,1)} %bitcast.266), custom_call_target="tpu_custom_call" | custom-call | bytes 50331648 | tf_op jit(solution)/shard_map/pallas_call | solution.py:213
  276.4 1.7 convert_reduce_fusion
  279.1 6.7 %shard_map.136 = f32[8,2,128]{2,1,0:T(2,128)} custom-call(f32[2,128]{1,0:T(2,128)} %pad_bitcast_fusion.x_ref), custom_call_target="tpu_custom_call" | custom-call | bytes 16384 | tf_op jit(solution)/shard_map/pallas_call | solution.py:213
  287.3 36.1 %shard_map.137 = bf16[16,2,48,512]{3,2,1,0:T(8,128)(2,1)} custom-call(bf16[2,48,512]{2,1,0:T(8,128)(2,1)} %fusion.56.x_ref), custom_call_target="tpu_custom_call" | custom-call | bytes 3145728 | tf_op jit(solution)/shard_map/pallas_call | solution.py:192
  323.5 4.3 %convolution_convert_fusion.1 = bf16[1536,768]{1,0:T(8,128)(2,1)} fusion(bf16[1536,512]{1,0:T(8,128)(2,1)} %bitcast.271, bf16[512,768]{1,0:T(8,128)(2,1)S(1)} %copy-done.21), kind=kOutput, calls=%fused_computation.6 | convolution fusion | flops 1209139200 | bytes 4718592 | tf_op jit(solution)/shard_map/dot_general | solution.py:478
  327.8 31.9 %reduce-scatter.2.cloned.1.call-done = bf16[192,768]{1,0:T(8,128)(2,1)} async-done(((bf16[1536,768]{1,0:T(8,128)(2,1)}), bf16[192,768]{1,0:T(8,128)(2,1)}) %reduce-scatter.2.cloned.1.call-update) | async-done | bytes 294928 | tf_op jit(solution)/shard_map/reduce_scatter | solution.py:479
  359.7 1.7 copy.246
  (180 shorter events, 50.3 us)
Async XLA Ops:
  7.2 50.7 %copy-start = (bf16[512,1024]{1,0:T(8,128)(2,1)S(1)}, bf16[512,1024]{1,0:T(8,128)(2,1)}, u32[]{:S(2)}) copy-start(bf16[512,1024]{1,0:T(8,128)(2,1)} %param.15) | copy-start | bytes 3145732
  7.2 33.7 %copy-start.17 = (f32[3,512]{1,0:T(4,128)S(1)}, f32[3,512]{1,0:T(4,128)}, u32[]{:S(2)}) copy-start(f32[3,512]{1,0:T(4,128)} %param.13) | copy-start | bytes 18436
  7.2 132.9 %all-reduce.4.cloned.1.call-start = ((), (), s32[]{:S(2)}) async-start(), calls=%async_computation.1 | async-start | bytes 11010048 | tf_op jit(solution)/shard_map/psum | solution.py:312
  38.1 1.9 copy-start.3
  55.3 1.1 copy-start.9
  62.6 0.7 copy-start.19
  62.6 0.7 copy-start.2
  62.6 3.1 copy-start.22
  62.7 297.1 %reduce-scatter.2.cloned.1.call-start = ((), (), s32[]{:S(2)}) async-start(), calls=%async_computation.2 | async-start | bytes 2654208 | tf_op jit(solution)/shard_map/reduce_scatter | solution.py:479
  149.2 1.2 copy-start.7
  149.2 2.5 copy-start.4
  155.3 0.8 copy-start.5
  158.4 8.8 %slice-start = ((s8[5505024]{0:T(1024)(128)(4,1)}), s8[1310720]{0:T(1024)(128)(4,1)S(1)}, s32[]{:S(2)}) async-start(s8[5505024]{0:T(1024)(128)(4,1)} %bitcast.264), calls=%async_computation.3 | async-start | bytes 2621440
  163.7 2.2 copy-start.6
  163.7 3.5 slice-start.1
  190.9 5.8 %copy-start.18 = (s32[96]{0:T(128)S(1)}, s32[96]{0:T(128)}, u32[]{:S(2)}) copy-start(s32[96]{0:T(128)} %fusion.103) | copy-start | bytes 1156
  196.7 13.4 %copy-start.13 = (f32[1,96,2]{2,1,0:T(8,128)S(1)}, f32[1,96,2]{2,1,0:T(8,128)}, u32[]{:S(2)}) copy-start(f32[1,96,2]{2,1,0:T(8,128)} %slice.304) | copy-start | bytes 2308
  213.6 4.3 %copy-start.14 = (bf16[1,96,2,128]{3,2,1,0:T(2,128)(2,1)S(1)}, bf16[1,96,2,128]{3,2,1,0:T(2,128)(2,1)}, u32[]{:S(2)}) copy-start(bf16[1,96,2,128]{3,2,1,0:T(2,128)(2,1)} %slice.254) | copy-start | bytes 147460
  213.6 4.3 %copy-start.15 = (bf16[1,96,2,128]{3,2,1,0:T(2,128)(2,1)S(1)}, bf16[1,96,2,128]{3,2,1,0:T(2,128)(2,1)}, u32[]{:S(2)}) copy-start(bf16[1,96,2,128]{3,2,1,0:T(2,128)(2,1)} %stack_reshape.14) | copy-start | bytes 147460
  215.0 4.8 %copy-start.11 = (f32[96,2,128]{2,1,0:T(2,128)S(1)}, f32[96,2,128]{2,1,0:T(2,128)}, u32[]{:S(2)}) copy-start(f32[96,2,128]{2,1,0:T(2,128)} %reshape.512) | copy-start | bytes 294916
  219.8 17.7 %copy-start.20 = (bf16[1024,512]{1,0:T(8,128)(2,1)S(1)}, bf16[1024,512]{1,0:T(8,128)(2,1)}, u32[]{:S(2)}) copy-start(bf16[1024,512]{1,0:T(8,128)(2,1)} %param.17) | copy-start | bytes 3145732
  237.5 3.8 %copy-start.12 = (bf16[256,512]{1,0:T(8,128)(2,1)S(1)}, bf16[256,512]{1,0:T(8,128)(2,1)}, u32[]{:S(2)}) copy-start(bf16[256,512]{1,0:T(8,128)(2,1)} %param.16) | copy-start | bytes 786436
  243.0 35.2 %copy-start.10 = (bf16[2,48,512]{2,1,0:T(8,128)(2,1)S(1)}, bf16[2,48,512]{2,1,0:T(8,128)(2,1)}, u32[]{:S(2)}) copy-start(bf16[2,48,512]{2,1,0:T(8,128)(2,1)} %x_ref.1) | copy-start | bytes 294916
  243.0 43.6 %copy-start.16 = (f32[1,512]{1,0:T(1,128)S(1)}, f32[1,512]{1,0:T(1,128)}, u32[]{:S(2)}) copy-start(f32[1,512]{1,0:T(1,128)} %get-tuple-element.62) | copy-start | bytes 6148
  276.4 47.1 %copy-start.21 = (bf16[512,768]{1,0:T(8,128)(2,1)S(1)}, bf16[512,768]{1,0:T(8,128)(2,1)}, u32[]{:S(2)}) copy-start(bf16[512,768]{1,0:T(8,128)(2,1)} %param.18) | copy-start | bytes 2359300
  278.2 49.6 %copy-start.8 = (bf16[2,48,512]{2,1,0:T(8,128)(2,1)}, bf16[2,48,512]{2,1,0:T(8,128)(2,1)S(1)}, u32[]{:S(2)}) copy-start(bf16[2,48,512]{2,1,0:T(8,128)(2,1)S(1)} %get-tuple-element.13) | copy-start | bytes 294916
  323.5 38.0 %copy-start.1 = (bf16[512,1024]{1,0:T(8,128)(2,1)S(1)}, bf16[512,1024]{1,0:T(8,128)(2,1)}, u32[]{:S(2)}) copy-start(bf16[512,1024]{1,0:T(8,128)(2,1)} %param.15) | copy-start | bytes 3145732
Sparse Core Ops, SparseCore 0:
  62.8 77.3 all-reduce.3
  327.9 31.7 reduce-scatter.1

commit v12 on v11

--- a/solution.py
+++ b/solution.py
@@ -206,6 +206,70 @@
             flops=0, transcendentals=0, bytes_accessed=2 * n * x.size * x.dtype.itemsize
         ),
     )(x)
+
+
+def gather_matmul_kernel(axis, n, x_ref, lhs_ref, rhs_ref, out_ref, prod_ref, send_sem, recv_sem, local_sem):
+    me = lax.axis_index(axis)
+    barrier = pltpu.get_barrier_semaphore()
+    for k in range(1, n):
+        pl.semaphore_signal(
+            barrier, inc=1, device_id={axis: lax.rem(me + k, n)}, device_id_type=MESH
+        )
+    pl.semaphore_wait(barrier, n - 1)
+    local = pltpu.make_async_copy(x_ref, out_ref.at[me], local_sem)
+    local.start()
+    copies = []
+    for k in range(1, n):
+        dest = lax.rem(me + k, n)
+        copy = pltpu.make_async_remote_copy(
+            src_ref=x_ref,
+            dst_ref=out_ref.at[me],
+            send_sem=send_sem.at[k],
+            recv_sem=recv_sem.at[k],
+            device_id={axis: dest},
+            device_id_type=MESH,
+        )
+        copy.start()
+        copies.append(copy)
+    tile = 256
+
+    @pl.loop(0, lhs_ref.shape[0] // tile)
+    def _(index):
+        rows = pl.ds(pl.multiple_of(index * tile, tile), tile)
+        prod_ref[rows, :] = jnp.dot(
+            lhs_ref[rows, :], rhs_ref[...], preferred_element_type=jnp.float32
+        )
+
+    for copy in copies:
+        copy.wait()
+    local.wait()
+
+
+def gather_matmul(x, lhs, rhs, axis, n, collective_id):
+    return pl.pallas_call(
+        functools.partial(gather_matmul_kernel, axis, n),
+        out_shape=(
+            jax.ShapeDtypeStruct((n,) + x.shape, x.dtype),
+            jax.ShapeDtypeStruct((lhs.shape[0], rhs.shape[1]), jnp.float32),
+        ),
+        in_specs=[pl.BlockSpec(memory_space=pltpu.VMEM)] * 3,
+        out_specs=(pl.BlockSpec(memory_space=pltpu.VMEM),) * 2,
+        scratch_shapes=[
+            pltpu.SemaphoreType.DMA((n,)),
+            pltpu.SemaphoreType.DMA((n,)),
+            pltpu.SemaphoreType.DMA(()),
+        ],
+        compiler_params=pltpu.CompilerParams(
+            collective_id=collective_id, has_side_effects=True
+        ),
+        cost_estimate=pl.CostEstimate(
+            flops=2 * lhs.shape[0] * lhs.shape[1] * rhs.shape[1],
+            transcendentals=0,
+            bytes_accessed=2 * n * x.size * x.dtype.itemsize
+            + 2 * (lhs.size + rhs.size)
+            + 4 * lhs.shape[0] * rhs.shape[1],
+        ),
+    )(x, lhs, rhs)
 
 
 def exchange(x, axis, n, gather, collective_id):
@@ -452,15 +516,16 @@
             (summed / total[..., None]).astype(jnp.bfloat16).reshape(own_count, head_count * HD)
         )
     attended = jnp.stack(attended_steps)
-    attended_all = exchange(attended, "req", req_size, True, 6)
+    attended_all, down_part = gather_matmul(
+        attended, activated_all, down_weight, "req", req_size, 6
+    )
     attended_msi = (
         attended_all.reshape(req_size, steps, per_own, local_rows, -1)
         .transpose(0, 2, 1, 3, 4)
         .reshape(steps * beam_total, -1)
     )
     update_partial = (
-        jnp.dot(attended_msi, dense_weight, preferred_element_type=jnp.float32)
-        + jnp.dot(activated_all, down_weight, preferred_element_type=jnp.float32)
+        jnp.dot(attended_msi, dense_weight, preferred_element_type=jnp.float32) + down_part
     ).astype(jnp.bfloat16)
     update = jnp.sum(
         exchange(

time: 370 us -> 370 us (level)
    pallas_call x0 -> x1, Pallas kernels: none -> 17.4 us  [gather_matmul(): pl.pallas_call(functools.partial(gather_matmul_kernel, axis, n), out_shap...]
    pallas_call x4 -> x3, Pallas kernels: 64 us -> 49 us  [exchange(): pl.pallas_call(functools.partial(exchange_kernel, axis, n, gather), out_s...]
    dot_general x1 -> x0, matrix products: 3.73 us -> none  [shards(): jnp.dot(activated_all, down_weight, preferred_element_type=jnp.float32)]
where the time goes in v12:
time: 370 us; the launch traced here: 369 us
  Pallas kernels  153 us (41%)
  waiting for transfers between devices  105 us (28%)
  local copies, waits for them, and re-layouts  40.9 us (11%)
  other arithmetic  29.8 us (8%)
  matrix products  24.5 us (7%)
  between operations  14.8 us (4%)
    psum x1, waiting for transfers between devices, shards(): summed_all = lax.psum(partial_sums.astype(jnp.bfloat16), 'req')  73.6 us
    pallas_call x2, Pallas kernels, gather_grid(): pl.pallas_call(functools.partial(gather_grid_kernel, axis, side), out_sha...  67.1 us
    pallas_call x3, Pallas kernels, exchange(): pl.pallas_call(functools.partial(exchange_kernel, axis, n, gather), out_s...  49 us
    reduce_scatter x1, waiting for transfers between devices, shards(): lax.psum_scatter(next_partial.astype(jnp.bfloat16), 'req', scatter_dimens...  31.8 us
    pallas_call x1, Pallas kernels, exchange_gelu(): pl.pallas_call(functools.partial(exchange_gelu_kernel, axis, n), out_shap...  19.5 us
    pallas_call x1, Pallas kernels, gather_matmul(): pl.pallas_call(functools.partial(gather_matmul_kernel, axis, n), out_shap...  17.4 us
  transfers between devices with their start and end apart: 2, of which 2 were waited for; matrix products, arithmetic and copies ran while one was open for 1% of the time, Pallas kernels for 0%

profile of v12, /device:TPU:0, one launch (start us, length us, event | category | flops | bytes accessed | tf_op | source)
XLA Modules:
  0.0 368.8 jit_solution(2832985607829483670)
XLA Ops:
  7.2 30.9 %shard_map.131 = bf16[16,2,48,512]{3,2,1,0:T(8,128)(2,1)} custom-call(bf16[2,48,512]{2,1,0:T(8,128)(2,1)} %x_ref.1), custom_call_target="tpu_custom_call" | custom-call | bytes 3145728 | tf_op jit(solution)/shard_map/pallas_call | solution.py:192
  38.1 1.8 convert_reduce_fusion.1
  41.4 1.4 copy.207
  44.5 8.9 %shard_map.132 = f32[8,24,128]{2,1,0:T(8,128)} custom-call(f32[24,128]{1,0:T(8,128)} %reshape.491.x_ref), custom_call_target="tpu_custom_call" | custom-call | bytes 196608 | tf_op jit(solution)/shard_map/pallas_call | solution.py:277
  56.5 1.4 convolution_convert_fusion.2
  57.9 1.8 convolution_convert_fusion
  59.7 2.9 pad_maximum_fusion
  66.5 73.6 %all-reduce.4.cloned.1.call-done = bf16[1536,1792]{1,0:T(8,128)(2,1)} async-done(((bf16[1536,1792]{1,0:T(8,128)(2,1)}), bf16[1536,1792]{1,0:T(8,128)(2,1)}) %all-reduce.4.cloned.1.call-update) | async-done | bytes 5505040 | tf_op jit(solution)/shard_map/psum | solution.py:376
  140.1 2.9 fusion.107
  144.0 1.8 fusion.41
  145.8 2.8 fusion.108
  156.2 2.2 fusion.29
  158.4 2.4 fusion.26
  167.3 2.1 slice.279.hidden_ref
  169.4 19.5 %shard_map.133 = (bf16[8,2,96,384]{3,2,1,0:T(8,128)(2,1)}, bf16[1536,1024]{1,0:T(8,128)(2,1)}) custom-call(bf16[8,2,96,384]{3,2,1,0:T(8,128)(2,1)} %copy_bitcast_fusion.x_ref, bf16[1536,1024]{1,0:T(8,128)(2,1)} %slice.279.hidden_ref), custom_call_target="tpu_custom_call" | custom-call | flops 31457280 | bytes 25165824 | tf_op jit(solution)/shard_map/pallas_call | solution.py:123
  188.9 1.5 convert_element_type.165
  194.5 1.6 reshape.512
  197.6 1.4 stack_reshape.14
  200.6 1.4 slice.252
  203.5 1.4 stack_reshape.13
  213.6 1.4 fusion.109
  215.0 1.4 copy.235
  216.5 1.4 copy.233
  221.2 17.4 %shard_map.134 = (bf16[8,2,96,256]{3,2,1,0:T(8,128)(2,1)}, f32[1536,512]{1,0:T(8,128)}) custom-call(bf16[2,96,256]{2,1,0:T(8,128)(2,1)} %pad_maximum_fusion.8.x_ref, bf16[1536,1024]{1,0:T(8,128)(2,1)} %get-tuple-element.7.lhs_ref, bf16[1024,512]{1,0:T(8,128)(2,1)} %rhs_ref.1), custom_call_target="tpu_custom_call" | custom-call | flops 1610612736 | bytes 8912896 | tf_op jit(solution)/shard_map/pallas_call | solution.py:249
  239.9 3.6 fusion.5
  243.5 33.4 %shard_map.135 = bf16[16,96,512]{2,1,0:T(8,128)(2,1)} custom-call(bf16[16,96,512]{2,1,0:T(8,128)(2,1)} %bitcast.264), custom_call_target="tpu_custom_call" | custom-call | bytes 50331648 | tf_op jit(solution)/shard_map/pallas_call | solution.py:277
  277.0 1.7 convert_reduce_fusion
  279.6 6.7 %shard_map.136 = f32[8,2,128]{2,1,0:T(2,128)} custom-call(f32[2,128]{1,0:T(2,128)} %pad_bitcast_fusion.x_ref), custom_call_target="tpu_custom_call" | custom-call | bytes 16384 | tf_op jit(solution)/shard_map/pallas_call | solution.py:277
  287.9 36.2 %shard_map.137 = bf16[16,2,48,512]{3,2,1,0:T(8,128)(2,1)} custom-call(bf16[2,48,512]{2,1,0:T(8,128)(2,1)} %fusion.56.x_ref), custom_call_target="tpu_custom_call" | custom-call | bytes 3145728 | tf_op jit(solution)/shard_map/pallas_call | solution.py:192
  324.2 4.3 %convolution_convert_fusion.1 = bf16[1536,768]{1,0:T(8,128)(2,1)} fusion(bf16[1536,512]{1,0:T(8,128)(2,1)} %bitcast.268, bf16[512,768]{1,0:T(8,128)(2,1)S(1)} %copy-done.20), kind=kOutput, calls=%fused_computation.6 | convolution fusion | flops 1209139200 | bytes 4718592 | tf_op jit(solution)/shard_map/dot_general | solution.py:543
  328.5 31.8 %reduce-scatter.2.cloned.1.call-done = bf16[192,768]{1,0:T(8,128)(2,1)} async-done(((bf16[1536,768]{1,0:T(8,128)(2,1)}), bf16[192,768]{1,0:T(8,128)(2,1)}) %reduce-scatter.2.cloned.1.call-update) | async-done | bytes 294928 | tf_op jit(solution)/shard_map/reduce_scatter | solution.py:544
  360.3 1.7 copy.246
  (177 shorter events, 48.9 us)
Async XLA Ops:
  7.2 50.7 %copy-start = (bf16[512,1024]{1,0:T(8,128)(2,1)S(1)}, bf16[512,1024]{1,0:T(8,128)(2,1)}, u32[]{:S(2)}) copy-start(bf16[512,1024]{1,0:T(8,128)(2,1)} %param.15) | copy-start | bytes 3145732
  7.2 33.7 %copy-start.17 = (f32[3,512]{1,0:T(4,128)S(1)}, f32[3,512]{1,0:T(4,128)}, u32[]{:S(2)}) copy-start(f32[3,512]{1,0:T(4,128)} %param.13) | copy-start | bytes 18436
  7.2 132.9 %all-reduce.4.cloned.1.call-start = ((), (), s32[]{:S(2)}) async-start(), calls=%async_computation.1 | async-start | bytes 11010048 | tf_op jit(solution)/shard_map/psum | solution.py:376
  38.1 1.9 copy-start.3
  55.3 1.1 copy-start.9
  62.6 0.7 copy-start.19
  62.6 0.7 copy-start.2
  62.6 3.1 copy-start.21
  62.7 297.6 %reduce-scatter.2.cloned.1.call-start = ((), (), s32[]{:S(2)}) async-start(), calls=%async_computation.2 | async-start | bytes 2654208 | tf_op jit(solution)/shard_map/reduce_scatter | solution.py:544
  149.2 1.2 copy-start.7
  149.2 2.5 copy-start.4
  155.3 0.8 copy-start.5
  158.4 8.8 %slice-start = ((s8[5505024]{0:T(1024)(128)(4,1)}), s8[1310720]{0:T(1024)(128)(4,1)S(1)}, s32[]{:S(2)}) async-start(s8[5505024]{0:T(1024)(128)(4,1)} %bitcast.262), calls=%async_computation.3 | async-start | bytes 2621440
  163.7 2.2 copy-start.6
  163.7 3.5 slice-start.1
  190.9 5.8 %copy-start.18 = (s32[96]{0:T(128)S(1)}, s32[96]{0:T(128)}, u32[]{:S(2)}) copy-start(s32[96]{0:T(128)} %fusion.103) | copy-start | bytes 1156
  196.7 13.4 %copy-start.13 = (f32[1,96,2]{2,1,0:T(8,128)S(1)}, f32[1,96,2]{2,1,0:T(8,128)}, u32[]{:S(2)}) copy-start(f32[1,96,2]{2,1,0:T(8,128)} %slice.304) | copy-start | bytes 2308
  213.6 4.3 %copy-start.14 = (bf16[1,96,2,128]{3,2,1,0:T(2,128)(2,1)S(1)}, bf16[1,96,2,128]{3,2,1,0:T(2,128)(2,1)}, u32[]{:S(2)}) copy-start(bf16[1,96,2,128]{3,2,1,0:T(2,128)(2,1)} %slice.254) | copy-start | bytes 147460
  213.6 4.3 %copy-start.15 = (bf16[1,96,2,128]{3,2,1,0:T(2,128)(2,1)S(1)}, bf16[1,96,2,128]{3,2,1,0:T(2,128)(2,1)}, u32[]{:S(2)}) copy-start(bf16[1,96,2,128]{3,2,1,0:T(2,128)(2,1)} %stack_reshape.14) | copy-start | bytes 147460
  215.0 4.8 %copy-start.11 = (f32[96,2,128]{2,1,0:T(2,128)S(1)}, f32[96,2,128]{2,1,0:T(2,128)}, u32[]{:S(2)}) copy-start(f32[96,2,128]{2,1,0:T(2,128)} %reshape.512) | copy-start | bytes 294916
  221.2 18.7 %copy-start.12 = (bf16[256,512]{1,0:T(8,128)(2,1)S(1)}, bf16[256,512]{1,0:T(8,128)(2,1)}, u32[]{:S(2)}) copy-start(bf16[256,512]{1,0:T(8,128)(2,1)} %param.16) | copy-start | bytes 786436
  243.5 35.1 %copy-start.10 = (bf16[2,48,512]{2,1,0:T(8,128)(2,1)S(1)}, bf16[2,48,512]{2,1,0:T(8,128)(2,1)}, u32[]{:S(2)}) copy-start(bf16[2,48,512]{2,1,0:T(8,128)(2,1)} %x_ref.1) | copy-start | bytes 294916
  243.5 43.6 %copy-start.16 = (f32[1,512]{1,0:T(1,128)S(1)}, f32[1,512]{1,0:T(1,128)}, u32[]{:S(2)}) copy-start(f32[1,512]{1,0:T(1,128)} %get-tuple-element.66) | copy-start | bytes 6148
  276.9 47.2 %copy-start.20 = (bf16[512,768]{1,0:T(8,128)(2,1)S(1)}, bf16[512,768]{1,0:T(8,128)(2,1)}, u32[]{:S(2)}) copy-start(bf16[512,768]{1,0:T(8,128)(2,1)} %param.18) | copy-start | bytes 2359300
  278.8 49.7 %copy-start.8 = (bf16[2,48,512]{2,1,0:T(8,128)(2,1)}, bf16[2,48,512]{2,1,0:T(8,128)(2,1)S(1)}, u32[]{:S(2)}) copy-start(bf16[2,48,512]{2,1,0:T(8,128)(2,1)S(1)} %get-tuple-element.17) | copy-start | bytes 294916
  324.1 37.8 %copy-start.1 = (bf16[512,1024]{1,0:T(8,128)(2,1)S(1)}, bf16[512,1024]{1,0:T(8,128)(2,1)}, u32[]{:S(2)}) copy-start(bf16[512,1024]{1,0:T(8,128)(2,1)} %param.15) | copy-start | bytes 3145732
Sparse Core Ops, SparseCore 0:
  62.8 77.3 all-reduce.3
  328.6 31.6 reduce-scatter.1

commit v13 on v11

--- a/solution.py
+++ b/solution.py
@@ -423,35 +423,43 @@
     )
 
     source = own_group * BEAM + parents[0]
-    attended_steps = []
-    for step_index in range(steps):
-        tail_keys = [pick_rows(keys_new[prior], source) for prior in range(step_index)]
-        tail_values = [pick_rows(values_new[prior], source) for prior in range(step_index)]
-        history_keys = jnp.stack(tail_keys + [keys_new[step_index]], axis=0)
-        history_values = jnp.stack(tail_values + [values_new[step_index]], axis=0)
-        own_scores = (
-            jnp.einsum(
-                "bhd,nbhd->bhn",
-                queries_own[step_index],
-                history_keys,
-                preferred_element_type=jnp.float32,
-            )
-            * scale
-        )
-        top = jnp.maximum(own_top[step_index], jnp.max(own_scores, axis=2))
-        page_factor = jnp.exp(own_top[step_index] - top)
-        own_weights = jnp.exp(own_scores - top[..., None])
-        total = own_total[step_index] * page_factor + jnp.sum(own_weights, axis=2)
-        summed = own_out[step_index] * page_factor[..., None] + jnp.einsum(
-            "bhn,nbhd->bhd",
-            own_weights.astype(jnp.bfloat16),
-            history_values,
-            preferred_element_type=jnp.float32,
-        )
-        attended_steps.append(
-            (summed / total[..., None]).astype(jnp.bfloat16).reshape(own_count, head_count * HD)
-        )
-    attended = jnp.stack(attended_steps)
+    def history(table):
+        empty = jnp.zeros_like(table[0])
+        return jnp.stack(
+            [
+                jnp.stack(
+                    [
+                        pick_rows(table[n], source) if n < s else table[s] if n == s else empty
+                        for n in range(steps)
+                    ]
+                )
+                for s in range(steps)
+            ]
+        )
+
+    filled = (
+        jnp.arange(steps, dtype=jnp.int32)[None, :] <= jnp.arange(steps, dtype=jnp.int32)[:, None]
+    )[:, None, None, :]
+    own_scores = (
+        jnp.einsum(
+            "zbhd,znbhd->zbhn", queries_own, history(keys_new), preferred_element_type=jnp.float32
+        )
+        * scale
+    )
+    own_scores = jnp.where(filled, own_scores, NEG_FILL)
+    top = jnp.maximum(own_top, jnp.max(own_scores, axis=3))
+    page_factor = jnp.exp(own_top - top)
+    own_weights = jnp.where(filled, jnp.exp(own_scores - top[..., None]), 0.0)
+    total = own_total * page_factor + jnp.sum(own_weights, axis=3)
+    summed = own_out * page_factor[..., None] + jnp.einsum(
+        "zbhn,znbhd->zbhd",
+        own_weights.astype(jnp.bfloat16),
+        history(values_new),
+        preferred_element_type=jnp.float32,
+    )
+    attended = (summed / total[..., None]).astype(jnp.bfloat16).reshape(
+        steps, own_count, head_count * HD
+    )
     attended_all = exchange(attended, "req", req_size, True, 6)
     attended_msi = (
         attended_all.reshape(req_size, steps, per_own, local_rows, -1)

time: 370 us -> 361 us (0.976)
  local copies, waits for them, and re-layouts: 40.9 us -> 36.8 us
  other arithmetic: 29.8 us -> 25.9 us
where the time goes in v13:
time: 361 us; the launch traced here: 360 us
  Pallas kernels  151 us (42%)
  waiting for transfers between devices  105 us (29%)
  local copies, waits for them, and re-layouts  36.8 us (10%)
  other arithmetic  25.9 us (7%)
  matrix products  25.6 us (7%)
  between operations  14.9 us (4%)
    psum x1, waiting for transfers between devices, shards(): summed_all = lax.psum(partial_sums.astype(jnp.bfloat16), 'req')  73.6 us
    pallas_call x2, Pallas kernels, gather_grid(): pl.pallas_call(functools.partial(gather_grid_kernel, axis, side), out_sha...  67.3 us
    pallas_call x4, Pallas kernels, exchange(): pl.pallas_call(functools.partial(exchange_kernel, axis, n, gather), out_s...  64 us
    reduce_scatter x1, waiting for transfers between devices, shards(): lax.psum_scatter(next_partial.astype(jnp.bfloat16), 'req', scatter_dimens...  31.5 us
    pallas_call x1, Pallas kernels, exchange_gelu(): pl.pallas_call(functools.partial(exchange_gelu_kernel, axis, n), out_shap...  19.5 us
  transfers between devices with their start and end apart: 2, of which 2 were waited for; matrix products, arithmetic and copies ran while one was open for 1% of the time, Pallas kernels for 0%

profile of v13, /device:TPU:0, one launch (start us, length us, event | category | flops | bytes accessed | tf_op | source)
XLA Modules:
  0.0 359.5 jit_solution(1106761544194094739)
XLA Ops:
  7.2 30.9 %shard_map.131 = bf16[16,2,48,512]{3,2,1,0:T(8,128)(2,1)} custom-call(bf16[2,48,512]{2,1,0:T(8,128)(2,1)} %x_ref.1), custom_call_target="tpu_custom_call" | custom-call | bytes 3145728 | tf_op jit(solution)/shard_map/pallas_call | solution.py:192
  38.1 1.8 convert_reduce_fusion.1
  41.4 1.4 copy.208
  44.5 8.9 %shard_map.132 = f32[8,24,128]{2,1,0:T(8,128)} custom-call(f32[24,128]{1,0:T(8,128)} %reshape.461.x_ref), custom_call_target="tpu_custom_call" | custom-call | bytes 196608 | tf_op jit(solution)/shard_map/pallas_call | solution.py:213
  56.5 1.4 convolution_convert_fusion.2
  57.9 1.8 convolution_convert_fusion
  59.7 2.9 pad_maximum_fusion
  66.5 73.6 %all-reduce.6.cloned.1.call-done = bf16[1536,1792]{1,0:T(8,128)(2,1)} async-done(((bf16[1536,1792]{1,0:T(8,128)(2,1)}), bf16[1536,1792]{1,0:T(8,128)(2,1)}) %all-reduce.6.cloned.1.call-update) | async-done | bytes 5505040 | tf_op jit(solution)/shard_map/psum | solution.py:312
  140.1 2.9 fusion.94
  144.0 1.8 fusion.41
  145.8 2.8 fusion.95
  156.2 2.2 fusion.29
  158.4 2.4 fusion.26
  167.3 2.1 slice.249.hidden_ref
  169.4 19.5 %shard_map.133 = (bf16[8,2,96,384]{3,2,1,0:T(8,128)(2,1)}, bf16[1536,1024]{1,0:T(8,128)(2,1)}) custom-call(bf16[8,2,96,384]{3,2,1,0:T(8,128)(2,1)} %copy_bitcast_fusion.x_ref, bf16[1536,1024]{1,0:T(8,128)(2,1)} %slice.249.hidden_ref), custom_call_target="tpu_custom_call" | custom-call | flops 31457280 | bytes 25165824 | tf_op jit(solution)/shard_map/pallas_call | solution.py:123
  188.9 1.5 convert_element_type.158
  198.8 1.6 reshape.512
  200.9 2.2 fusion.62
  205.5 1.4 fusion.96
  206.9 1.4 copy.236
  208.3 1.4 copy.234
  212.5 15.0 %shard_map.134 = bf16[8,2,96,256]{3,2,1,0:T(8,128)(2,1)} custom-call(bf16[2,96,256]{2,1,0:T(8,128)(2,1)} %reshape.469.x_ref), custom_call_target="tpu_custom_call" | custom-call | bytes 1572864 | tf_op jit(solution)/shard_map/pallas_call | solution.py:213
  227.5 1.2 copy.248
  228.8 3.7 %fusion.101 = f32[1536,512]{1,0:T(8,128)S(1)} fusion(bf16[1536,1024]{1,0:T(8,128)(2,1)} %get-tuple-element.5, bf16[1024,512]{1,0:T(8,128)(2,1)S(1)} %copy-done.20), kind=kOutput, calls=%fused_computation.208 | convolution fusion | flops 1610612736 | bytes 7340032 | tf_op jit(solution)/shard_map/dot_general | solution.py:471
  232.5 1.7 fusion.5
  234.3 33.5 %shard_map.135 = bf16[16,96,512]{2,1,0:T(8,128)(2,1)} custom-call(bf16[16,96,512]{2,1,0:T(8,128)(2,1)} %bitcast.220), custom_call_target="tpu_custom_call" | custom-call | bytes 50331648 | tf_op jit(solution)/shard_map/pallas_call | solution.py:213
  267.8 1.7 convert_reduce_fusion
  270.4 6.7 %shard_map.136 = f32[8,2,128]{2,1,0:T(2,128)} custom-call(f32[2,128]{1,0:T(2,128)} %pad_bitcast_fusion.2.x_ref), custom_call_target="tpu_custom_call" | custom-call | bytes 16384 | tf_op jit(solution)/shard_map/pallas_call | solution.py:213
  278.7 36.4 %shard_map.137 = bf16[16,2,48,512]{3,2,1,0:T(8,128)(2,1)} custom-call(bf16[2,48,512]{2,1,0:T(8,128)(2,1)} %fusion.56.x_ref), custom_call_target="tpu_custom_call" | custom-call | bytes 3145728 | tf_op jit(solution)/shard_map/pallas_call | solution.py:192
  315.2 4.3 %convolution_convert_fusion.1 = bf16[1536,768]{1,0:T(8,128)(2,1)} fusion(bf16[1536,512]{1,0:T(8,128)(2,1)} %bitcast.225, bf16[512,768]{1,0:T(8,128)(2,1)S(1)} %copy-done.21), kind=kOutput, calls=%fused_computation.6 | convolution fusion | flops 1209139200 | bytes 4718592 | tf_op jit(solution)/shard_map/dot_general | solution.py:486
  319.5 31.5 %reduce-scatter.2.cloned.1.call-done = bf16[192,768]{1,0:T(8,128)(2,1)} async-done(((bf16[1536,768]{1,0:T(8,128)(2,1)}), bf16[192,768]{1,0:T(8,128)(2,1)}) %reduce-scatter.2.cloned.1.call-update) | async-done | bytes 294928 | tf_op jit(solution)/shard_map/reduce_scatter | solution.py:487
  351.0 1.7 copy.249
  (177 shorter events, 41.1 us)
Async XLA Ops:
  7.2 50.7 %copy-start = (bf16[512,1024]{1,0:T(8,128)(2,1)S(1)}, bf16[512,1024]{1,0:T(8,128)(2,1)}, u32[]{:S(2)}) copy-start(bf16[512,1024]{1,0:T(8,128)(2,1)} %param.15) | copy-start | bytes 3145732
  7.2 33.7 %copy-start.17 = (f32[3,512]{1,0:T(4,128)S(1)}, f32[3,512]{1,0:T(4,128)}, u32[]{:S(2)}) copy-start(f32[3,512]{1,0:T(4,128)} %param.13) | copy-start | bytes 18436
  7.2 132.9 %all-reduce.6.cloned.1.call-start = ((), (), s32[]{:S(2)}) async-start(), calls=%async_computation.1 | async-start | bytes 11010048 | tf_op jit(solution)/shard_map/psum | solution.py:312
  38.1 1.9 copy-start.3
  55.3 1.1 copy-start.9
  62.6 0.7 copy-start.19
  62.6 0.7 copy-start.2
  62.6 3.7 %copy-start.22 = (s32[1,96]{1,0:T(1,128)S(1)}, s32[1,96]{1,0:T(1,128)}, u32[]{:S(2)}) copy-start(s32[1,96]{1,0:T(1,128)} %param.23) | copy-start | bytes 1156
  62.7 288.3 %reduce-scatter.2.cloned.1.call-start = ((), (), s32[]{:S(2)}) async-start(), calls=%async_computation.2 | async-start | bytes 2654208 | tf_op jit(solution)/shard_map/reduce_scatter | solution.py:487
  149.2 1.2 copy-start.7
  149.2 2.5 copy-start.4
  155.3 0.8 copy-start.5
  158.4 8.9 %slice-start = ((s8[5505024]{0:T(1024)(128)(4,1)}), s8[1310720]{0:T(1024)(128)(4,1)S(1)}, s32[]{:S(2)}) async-start(s8[5505024]{0:T(1024)(128)(4,1)} %bitcast.218), calls=%async_computation.3 | async-start | bytes 2621440
  163.7 2.3 copy-start.6
  163.7 3.5 slice-start.1
  195.4 8.6 %copy-start.18 = (pred[2,2]{1,0:T(4,128)(4,1)S(1)}, pred[2,2]{1,0:T(4,128)(4,1)}, u32[]{:S(2)}) copy-start(pred[2,2]{1,0:T(4,128)(4,1)} %iota_compare_fusion.10) | copy-start | bytes 16
  205.5 4.3 %copy-start.13 = (bf16[1,96,2,128]{3,2,1,0:T(2,128)(2,1)S(1)}, bf16[1,96,2,128]{3,2,1,0:T(2,128)(2,1)}, u32[]{:S(2)}) copy-start(bf16[1,96,2,128]{3,2,1,0:T(2,128)(2,1)} %slice.224) | copy-start | bytes 147460
  205.5 4.3 %copy-start.14 = (bf16[1,96,2,128]{3,2,1,0:T(2,128)(2,1)S(1)}, bf16[1,96,2,128]{3,2,1,0:T(2,128)(2,1)}, u32[]{:S(2)}) copy-start(bf16[1,96,2,128]{3,2,1,0:T(2,128)(2,1)} %slice.222) | copy-start | bytes 147460
  205.5 4.3 %copy-start.15 = (bf16[1,96,2,128]{3,2,1,0:T(2,128)(2,1)S(1)}, bf16[1,96,2,128]{3,2,1,0:T(2,128)(2,1)}, u32[]{:S(2)}) copy-start(bf16[1,96,2,128]{3,2,1,0:T(2,128)(2,1)} %stack_reshape.7) | copy-start | bytes 147460
  206.9 3.4 copy-start.12
  211.3 17.4 %copy-start.20 = (bf16[1024,512]{1,0:T(8,128)(2,1)S(1)}, bf16[1024,512]{1,0:T(8,128)(2,1)}, u32[]{:S(2)}) copy-start(bf16[1024,512]{1,0:T(8,128)(2,1)} %param.17) | copy-start | bytes 3145732
  228.8 3.8 %copy-start.11 = (bf16[256,512]{1,0:T(8,128)(2,1)S(1)}, bf16[256,512]{1,0:T(8,128)(2,1)}, u32[]{:S(2)}) copy-start(bf16[256,512]{1,0:T(8,128)(2,1)} %param.16) | copy-start | bytes 786436
  234.3 35.2 %copy-start.10 = (bf16[2,48,512]{2,1,0:T(8,128)(2,1)S(1)}, bf16[2,48,512]{2,1,0:T(8,128)(2,1)}, u32[]{:S(2)}) copy-start(bf16[2,48,512]{2,1,0:T(8,128)(2,1)} %x_ref.1) | copy-start | bytes 294916
  234.3 43.7 %copy-start.16 = (f32[1,512]{1,0:T(1,128)S(1)}, f32[1,512]{1,0:T(1,128)}, u32[]{:S(2)}) copy-start(f32[1,512]{1,0:T(1,128)} %get-tuple-element.56) | copy-start | bytes 6148
  267.7 47.4 %copy-start.21 = (bf16[512,768]{1,0:T(8,128)(2,1)S(1)}, bf16[512,768]{1,0:T(8,128)(2,1)}, u32[]{:S(2)}) copy-start(bf16[512,768]{1,0:T(8,128)(2,1)} %param.18) | copy-start | bytes 2359300
  269.6 49.9 %copy-start.8 = (bf16[2,48,512]{2,1,0:T(8,128)(2,1)}, bf16[2,48,512]{2,1,0:T(8,128)(2,1)S(1)}, u32[]{:S(2)}) copy-start(bf16[2,48,512]{2,1,0:T(8,128)(2,1)S(1)} %get-tuple-element.13) | copy-start | bytes 294916
  315.2 37.5 %copy-start.1 = (bf16[512,1024]{1,0:T(8,128)(2,1)S(1)}, bf16[512,1024]{1,0:T(8,128)(2,1)}, u32[]{:S(2)}) copy-start(bf16[512,1024]{1,0:T(8,128)(2,1)} %param.15) | copy-start | bytes 3145732
Sparse Core Ops, SparseCore 0:
  62.8 77.3 all-reduce.5
  319.6 31.3 reduce-scatter.1

commit v14 on v13

--- a/solution.py
+++ b/solution.py
@@ -82,7 +82,7 @@
     local.wait()
 
 
-def exchange_gelu_kernel(axis, n, x_ref, hidden_ref, out_ref, act_ref, send_sem, recv_sem, local_sem):
+def exchange_gelu_kernel(axis, n, start, x_ref, hidden_ref, out_ref, act_ref, send_sem, recv_sem, local_sem):
     me = lax.axis_index(axis)
     barrier = pltpu.get_barrier_semaphore()
     for k in range(1, n):
@@ -110,7 +110,7 @@
     @pl.loop(0, hidden_ref.shape[0] // tile)
     def _(index):
         rows = pl.ds(pl.multiple_of(index * tile, tile), tile)
-        values = hidden_ref[rows, :].astype(jnp.float32)
+        values = hidden_ref[rows, start : start + act_ref.shape[1]].astype(jnp.float32)
         gelu = 0.5 * values * (1.0 + lax.erf(values * (1.0 / math.sqrt(2.0))))
         act_ref[rows, :] = gelu.astype(act_ref.dtype)
 
@@ -119,12 +119,13 @@
     local.wait()
 
 
-def exchange_gelu(x, hidden, axis, n, collective_id):
+def exchange_gelu(x, summed, start, axis, n, collective_id):
+    hidden = jax.ShapeDtypeStruct((summed.shape[0], summed.shape[1] - start), jnp.bfloat16)
     return pl.pallas_call(
-        functools.partial(exchange_gelu_kernel, axis, n),
+        functools.partial(exchange_gelu_kernel, axis, n, start),
         out_shape=(
             jax.ShapeDtypeStruct(x.shape, x.dtype),
-            jax.ShapeDtypeStruct(hidden.shape, jnp.bfloat16),
+            hidden,
         ),
         in_specs=[pl.BlockSpec(memory_space=pltpu.VMEM)] * 2,
         out_specs=(pl.BlockSpec(memory_space=pltpu.VMEM),) * 2,
@@ -141,7 +142,7 @@
             transcendentals=hidden.size,
             bytes_accessed=2 * n * x.size * x.dtype.itemsize + 4 * hidden.size,
         ),
-    )(x, hidden)
+    )(x, summed)
 
 
 def gather_grid_kernel(axis, side, x_ref, out_ref, send_sem, recv_sem, local_sem):
@@ -321,23 +322,28 @@
     queries_rows = rotate_rows(
         summed_all[:, :width].astype(jnp.float32), row_positions, head_count
     ).astype(jnp.bfloat16)
-    keys_rows = rotate_rows(
-        summed_all[:, width : 2 * width].astype(jnp.float32), row_positions, head_count
-    ).astype(jnp.bfloat16)
     per_own = own_count // local_rows
     own_start = lax.axis_index("req") * (per_own * steps * local_rows)
 
-    def own_of(rows):
+    def own_rows(rows):
+        return lax.dynamic_slice_in_dim(rows, own_start, per_own * steps * local_rows, 0)
+
+    def by_step(rows):
         return (
-            lax.dynamic_slice_in_dim(rows, own_start, per_own * steps * local_rows, 0)
-            .reshape(per_own, steps, local_rows, -1)
+            rows.reshape(per_own, steps, local_rows, -1)
             .transpose(1, 0, 2, 3)
             .reshape(steps, own_count, head_count, HD)
         )
 
-    queries_own = own_of(queries_rows)
-    keys_new = own_of(keys_rows)
-    values_new = own_of(summed_all[:, 2 * width : 3 * width])
+    queries_own = by_step(own_rows(queries_rows))
+    keys_new = by_step(
+        rotate_rows(
+            own_rows(summed_all[:, width : 2 * width].astype(jnp.float32)),
+            own_rows(row_positions),
+            head_count,
+        ).astype(jnp.bfloat16)
+    )
+    values_new = by_step(own_rows(summed_all[:, 2 * width : 3 * width]))
 
     chosen_rows = (
         (gather_rows // local_rows) * (steps * local_rows)
@@ -405,7 +411,7 @@
         axis=-1,
     )
     packed = packed.reshape(steps, req_size, own_count, -1).transpose(1, 0, 2, 3)
-    held, activated_all = exchange_gelu(packed, summed_all[:, triple_width:], "req", req_size, 5)
+    held, activated_all = exchange_gelu(packed, summed_all, triple_width, "req", req_size, 5)
     held = held.astype(jnp.float32)
     base = head_count * HD
     held_top = held[..., base + head_count : base + 2 * head_count] + held[

time: 361 us -> 359 us (level)
  no operation moved by 1% of the time
where the time goes in v14:
time: 359 us; the launch traced here: 358 us
  Pallas kernels  151 us (42%)
  waiting for transfers between devices  103 us (29%)
  local copies, waits for them, and re-layouts  33.6 us (9%)
  other arithmetic  27.8 us (8%)
  matrix products  26.3 us (7%)
  between operations  14.9 us (4%)
    psum x1, waiting for transfers between devices, shards(): summed_all = lax.psum(partial_sums.astype(jnp.bfloat16), 'req')  71.4 us
    pallas_call x2, Pallas kernels, gather_grid(): pl.pallas_call(functools.partial(gather_grid_kernel, axis, side), out_sha...  67.1 us
    pallas_call x4, Pallas kernels, exchange(): pl.pallas_call(functools.partial(exchange_kernel, axis, n, gather), out_s...  64 us
    reduce_scatter x1, waiting for transfers between devices, shards(): lax.psum_scatter(next_partial.astype(jnp.bfloat16), 'req', scatter_dimens...  31.9 us
    pallas_call x1, Pallas kernels, exchange_gelu(): pl.pallas_call(functools.partial(exchange_gelu_kernel, axis, n, start), o...  20.3 us
  transfers between devices with their start and end apart: 2, of which 2 were waited for; matrix products, arithmetic and copies ran while one was open for 1% of the time, Pallas kernels for 0%

profile of v14, /device:TPU:0, one launch (start us, length us, event | category | flops | bytes accessed | tf_op | source)
XLA Modules:
  0.0 357.6 jit_solution(7014228992294192728)
XLA Ops:
  7.2 30.9 %shard_map.131 = bf16[16,2,48,512]{3,2,1,0:T(8,128)(2,1)} custom-call(bf16[2,48,512]{2,1,0:T(8,128)(2,1)} %x_ref.1), custom_call_target="tpu_custom_call" | custom-call | bytes 3145728 | tf_op jit(solution)/shard_map/pallas_call | solution.py:193
  38.1 1.8 convert_reduce_fusion.1
  41.4 1.4 copy.208
  44.5 8.9 %shard_map.132 = f32[8,24,128]{2,1,0:T(8,128)} custom-call(f32[24,128]{1,0:T(8,128)} %reshape.467.x_ref), custom_call_target="tpu_custom_call" | custom-call | bytes 196608 | tf_op jit(solution)/shard_map/pallas_call | solution.py:214
  56.4 1.4 convolution_convert_fusion.2
  57.8 1.8 convolution_convert_fusion
  59.7 2.9 pad_maximum_fusion
  68.7 71.4 %all-reduce.6.cloned.1.call-done.hidden_ref = bf16[1536,1792]{1,0:T(8,128)(2,1)} async-done(((bf16[1536,1792]{1,0:T(8,128)(2,1)}), bf16[1536,1792]{1,0:T(8,128)(2,1)}) %all-reduce.6.cloned.1.call-update) | async-done | bytes 5505040 | tf_op jit(solution)/shard_map/psum | solution.py:313
  140.1 3.0 fusion.92
  144.2 1.4 fusion.93
  153.3 2.2 fusion.29
  155.6 2.2 fusion.26
  163.3 20.3 %shard_map.133 = (bf16[8,2,96,384]{3,2,1,0:T(8,128)(2,1)}, bf16[1536,1024]{1,0:T(8,128)(2,1)}) custom-call(bf16[8,2,96,384]{3,2,1,0:T(8,128)(2,1)} %copy_bitcast_fusion.x_ref, bf16[1536,1792]{1,0:T(8,128)(2,1)} %all-reduce.6.cloned.1.call-done.hidden_ref), custom_call_target="tpu_custom_call" | custom-call | flops 31457280 | bytes 25165824 | tf_op jit(solution)/shard_map/pallas_call | solution.py:124
  183.6 1.5 convert_element_type.157
  186.2 1.6 dynamic-slice_convert_fusion
  188.4 1.5 fusion.98
  191.4 1.4 stack_reshape.7
  192.8 1.5 pad_bitcast_fusion
  198.8 1.5 fusion.58
  202.5 1.4 fusion.94
  205.3 1.4 copy.234
  207.2 1.5 fusion.56
  210.4 15.0 %shard_map.134 = bf16[8,2,96,256]{3,2,1,0:T(8,128)(2,1)} custom-call(bf16[2,96,256]{2,1,0:T(8,128)(2,1)} %reshape.474.x_ref), custom_call_target="tpu_custom_call" | custom-call | bytes 1572864 | tf_op jit(solution)/shard_map/pallas_call | solution.py:214
  226.7 3.7 %fusion.100 = f32[1536,512]{1,0:T(8,128)S(1)} fusion(bf16[1536,1024]{1,0:T(8,128)(2,1)} %get-tuple-element.5, bf16[1024,512]{1,0:T(8,128)(2,1)S(1)} %copy-done.18), kind=kOutput, calls=%fused_computation.209 | convolution fusion | flops 1610612736 | bytes 7340032 | tf_op jit(solution)/shard_map/dot_general | solution.py:477
  230.4 1.7 fusion.5
  232.1 33.4 %shard_map.135 = bf16[16,96,512]{2,1,0:T(8,128)(2,1)} custom-call(bf16[16,96,512]{2,1,0:T(8,128)(2,1)} %bitcast.221), custom_call_target="tpu_custom_call" | custom-call | bytes 50331648 | tf_op jit(solution)/shard_map/pallas_call | solution.py:214
  265.6 1.7 convert_reduce_fusion
  268.3 6.7 %shard_map.136 = f32[8,2,128]{2,1,0:T(2,128)} custom-call(f32[2,128]{1,0:T(2,128)} %pad_bitcast_fusion.2.x_ref), custom_call_target="tpu_custom_call" | custom-call | bytes 16384 | tf_op jit(solution)/shard_map/pallas_call | solution.py:214
  276.6 36.2 %shard_map.137 = bf16[16,2,48,512]{3,2,1,0:T(8,128)(2,1)} custom-call(bf16[2,48,512]{2,1,0:T(8,128)(2,1)} %fusion.52.x_ref), custom_call_target="tpu_custom_call" | custom-call | bytes 3145728 | tf_op jit(solution)/shard_map/pallas_call | solution.py:193
  312.8 4.3 %convolution_convert_fusion.1 = bf16[1536,768]{1,0:T(8,128)(2,1)} fusion(bf16[1536,512]{1,0:T(8,128)(2,1)} %bitcast.226, bf16[512,768]{1,0:T(8,128)(2,1)S(1)} %copy-done.19), kind=kOutput, calls=%fused_computation.6 | convolution fusion | flops 1209139200 | bytes 4718592 | tf_op jit(solution)/shard_map/dot_general | solution.py:492
  317.1 31.9 %reduce-scatter.2.cloned.1.call-done = bf16[192,768]{1,0:T(8,128)(2,1)} async-done(((bf16[1536,768]{1,0:T(8,128)(2,1)}), bf16[192,768]{1,0:T(8,128)(2,1)}) %reduce-scatter.2.cloned.1.call-update) | async-done | bytes 294928 | tf_op jit(solution)/shard_map/reduce_scatter | solution.py:493
  349.0 1.7 copy.249
  (177 shorter events, 43.2 us)
Async XLA Ops:
  7.2 50.7 %copy-start = (bf16[512,1024]{1,0:T(8,128)(2,1)S(1)}, bf16[512,1024]{1,0:T(8,128)(2,1)}, u32[]{:S(2)}) copy-start(bf16[512,1024]{1,0:T(8,128)(2,1)} %param.15) | copy-start | bytes 3145732
  7.2 33.7 %copy-start.14 = (f32[3,512]{1,0:T(4,128)S(1)}, f32[3,512]{1,0:T(4,128)}, u32[]{:S(2)}) copy-start(f32[3,512]{1,0:T(4,128)} %param.13) | copy-start | bytes 18436
  7.2 132.9 %all-reduce.6.cloned.1.call-start = ((), (), s32[]{:S(2)}) async-start(), calls=%async_computation.1 | async-start | bytes 11010048 | tf_op jit(solution)/shard_map/psum | solution.py:313
  38.1 1.9 copy-start.3
  55.3 1.1 copy-start.6
  62.6 0.7 copy-start.17
  62.6 0.7 copy-start.2
  62.6 5.4 %copy-start.20 = (s32[1,96]{1,0:T(1,128)S(1)}, s32[1,96]{1,0:T(1,128)}, u32[]{:S(2)}) copy-start(s32[1,96]{1,0:T(1,128)} %param.23) | copy-start | bytes 1156
  62.6 286.4 %reduce-scatter.2.cloned.1.call-start = ((), (), s32[]{:S(2)}) async-start(), calls=%async_computation.2 | async-start | bytes 2654208 | tf_op jit(solution)/shard_map/reduce_scatter | solution.py:493
  146.8 2.2 copy-start.4
  185.6 5.0 %copy-start.15 = (s32[96]{0:T(128)S(1)}, s32[96]{0:T(128)}, u32[]{:S(2)}) copy-start(s32[96]{0:T(128)} %fusion.89) | copy-start | bytes 1156
  194.4 6.0 %copy-start.16 = (pred[2,2]{1,0:T(4,128)(4,1)S(1)}, pred[2,2]{1,0:T(4,128)(4,1)}, u32[]{:S(2)}) copy-start(pred[2,2]{1,0:T(4,128)(4,1)} %iota_compare_fusion.10) | copy-start | bytes 16
  202.5 4.3 %copy-start.11 = (bf16[1,96,2,128]{3,2,1,0:T(2,128)(2,1)S(1)}, bf16[1,96,2,128]{3,2,1,0:T(2,128)(2,1)}, u32[]{:S(2)}) copy-start(bf16[1,96,2,128]{3,2,1,0:T(2,128)(2,1)} %slice.218) | copy-start | bytes 147460
  202.5 4.3 %copy-start.12 = (bf16[1,96,2,128]{3,2,1,0:T(2,128)(2,1)S(1)}, bf16[1,96,2,128]{3,2,1,0:T(2,128)(2,1)}, u32[]{:S(2)}) copy-start(bf16[1,96,2,128]{3,2,1,0:T(2,128)(2,1)} %stack_reshape.7) | copy-start | bytes 147460
  202.5 4.5 %copy-start.8 = (bf16[1,2,96,2,128]{4,3,2,1,0:T(2,128)(2,1)S(1)}, bf16[1,2,96,2,128]{4,3,2,1,0:T(2,128)(2,1)}, u32[]{:S(2)}) copy-start(bf16[1,2,96,2,128]{4,3,2,1,0:T(2,128)(2,1)} %pad_bitcast_fusion) | copy-start | bytes 294916
  205.3 3.9 %copy-start.9 = (f32[2,96,2]{2,1,0:T(8,128)S(1)}, f32[2,96,2]{2,1,0:T(8,128)}, u32[]{:S(2)}) copy-start(f32[2,96,2]{2,1,0:T(8,128)} %copy.245) | copy-start | bytes 4612
  209.2 17.4 %copy-start.18 = (bf16[1024,512]{1,0:T(8,128)(2,1)S(1)}, bf16[1024,512]{1,0:T(8,128)(2,1)}, u32[]{:S(2)}) copy-start(bf16[1024,512]{1,0:T(8,128)(2,1)} %param.17) | copy-start | bytes 3145732
  226.6 3.8 %copy-start.10 = (bf16[256,512]{1,0:T(8,128)(2,1)S(1)}, bf16[256,512]{1,0:T(8,128)(2,1)}, u32[]{:S(2)}) copy-start(bf16[256,512]{1,0:T(8,128)(2,1)} %param.16) | copy-start | bytes 786436
  232.1 35.2 %copy-start.7 = (bf16[2,48,512]{2,1,0:T(8,128)(2,1)S(1)}, bf16[2,48,512]{2,1,0:T(8,128)(2,1)}, u32[]{:S(2)}) copy-start(bf16[2,48,512]{2,1,0:T(8,128)(2,1)} %x_ref.1) | copy-start | bytes 294916
  232.1 43.7 %copy-start.13 = (f32[1,512]{1,0:T(1,128)S(1)}, f32[1,512]{1,0:T(1,128)}, u32[]{:S(2)}) copy-start(f32[1,512]{1,0:T(1,128)} %get-tuple-element.56) | copy-start | bytes 6148
  265.6 47.2 %copy-start.19 = (bf16[512,768]{1,0:T(8,128)(2,1)S(1)}, bf16[512,768]{1,0:T(8,128)(2,1)}, u32[]{:S(2)}) copy-start(bf16[512,768]{1,0:T(8,128)(2,1)} %param.18) | copy-start | bytes 2359300
  267.4 49.7 %copy-start.5 = (bf16[2,48,512]{2,1,0:T(8,128)(2,1)}, bf16[2,48,512]{2,1,0:T(8,128)(2,1)S(1)}, u32[]{:S(2)}) copy-start(bf16[2,48,512]{2,1,0:T(8,128)(2,1)S(1)} %get-tuple-element.13) | copy-start | bytes 294916
  312.8 37.9 %copy-start.1 = (bf16[512,1024]{1,0:T(8,128)(2,1)S(1)}, bf16[512,1024]{1,0:T(8,128)(2,1)}, u32[]{:S(2)}) copy-start(bf16[512,1024]{1,0:T(8,128)(2,1)} %param.15) | copy-start | bytes 3145732
Sparse Core Ops, SparseCore 0:
  62.7 77.3 all-reduce.5
  317.3 31.7 reduce-scatter.1

commit v15 on v14

--- a/solution.py
+++ b/solution.py
@@ -82,7 +82,9 @@
     local.wait()
 
 
-def exchange_gelu_kernel(axis, n, start, x_ref, hidden_ref, out_ref, act_ref, send_sem, recv_sem, local_sem):
+def exchange_gelu_kernel(
+    axis, n, gather, start, first_row, x_ref, hidden_ref, out_ref, act_ref, send_sem, recv_sem, local_sem
+):
     me = lax.axis_index(axis)
     barrier = pltpu.get_barrier_semaphore()
     for k in range(1, n):
@@ -90,13 +92,13 @@
             barrier, inc=1, device_id={axis: lax.rem(me + k, n)}, device_id_type=MESH
         )
     pl.semaphore_wait(barrier, n - 1)
-    local = pltpu.make_async_copy(x_ref.at[me], out_ref.at[me], local_sem)
+    local = pltpu.make_async_copy(x_ref if gather else x_ref.at[me], out_ref.at[me], local_sem)
     local.start()
     copies = []
     for k in range(1, n):
         dest = lax.rem(me + k, n)
         copy = pltpu.make_async_remote_copy(
-            src_ref=x_ref.at[dest],
+            src_ref=x_ref if gather else x_ref.at[dest],
             dst_ref=out_ref.at[me],
             send_sem=send_sem.at[k],
             recv_sem=recv_sem.at[k],
@@ -107,10 +109,11 @@
         copies.append(copy)
     tile = 128
 
-    @pl.loop(0, hidden_ref.shape[0] // tile)
+    @pl.loop(0, act_ref.shape[0] // tile)
     def _(index):
         rows = pl.ds(pl.multiple_of(index * tile, tile), tile)
-        values = hidden_ref[rows, start : start + act_ref.shape[1]].astype(jnp.float32)
+        source = pl.ds(pl.multiple_of(first_row + index * tile, tile), tile)
+        values = hidden_ref[source, start : start + act_ref.shape[1]].astype(jnp.float32)
         gelu = 0.5 * values * (1.0 + lax.erf(values * (1.0 / math.sqrt(2.0))))
         act_ref[rows, :] = gelu.astype(act_ref.dtype)
 
@@ -119,12 +122,13 @@
     local.wait()
 
 
-def exchange_gelu(x, summed, start, axis, n, collective_id):
-    hidden = jax.ShapeDtypeStruct((summed.shape[0], summed.shape[1] - start), jnp.bfloat16)
+def exchange_gelu(x, summed, start, first_row, row_count, axis, n, gather, collective_id):
+    hidden = jax.ShapeDtypeStruct((row_count, summed.shape[1] - start), jnp.bfloat16)
+    shape = (n,) + (x.shape if gather else x.shape[1:])
     return pl.pallas_call(
-        functools.partial(exchange_gelu_kernel, axis, n, start),
+        functools.partial(exchange_gelu_kernel, axis, n, gather, start, first_row),
         out_shape=(
-            jax.ShapeDtypeStruct(x.shape, x.dtype),
+            jax.ShapeDtypeStruct(shape, x.dtype),
             hidden,
         ),
         in_specs=[pl.BlockSpec(memory_space=pltpu.VMEM)] * 2,
@@ -411,7 +415,10 @@
         axis=-1,
     )
     packed = packed.reshape(steps, req_size, own_count, -1).transpose(1, 0, 2, 3)
-    held, activated_all = exchange_gelu(packed, summed_all, triple_width, "req", req_size, 5)
+    split_row = steps * beam_total // 2
+    held, activated_first = exchange_gelu(
+        packed, summed_all, triple_width, 0, split_row, "req", req_size, False, 5
+    )
     held = held.astype(jnp.float32)
     base = head_count * HD
     held_top = held[..., base + head_count : base + 2 * head_count] + held[
@@ -466,7 +473,10 @@
     attended = (summed / total[..., None]).astype(jnp.bfloat16).reshape(
         steps, own_count, head_count * HD
     )
-    attended_all = exchange(attended, "req", req_size, True, 6)
+    attended_all, activated_second = exchange_gelu(
+        attended, summed_all, triple_width, split_row, split_row, "req", req_size, True, 6
+    )
+    activated_all = jnp.concatenate([activated_first, activated_second], axis=0)
     attended_msi = (
         attended_all.reshape(req_size, steps, per_own, local_rows, -1)
         .transpose(0, 2, 1, 3, 4)

time: 359 us -> 361 us (level)
    pallas_call x1 -> x2, Pallas kernels: 20.3 us -> 37.1 us  [exchange_gelu(): pl.pallas_call(functools.partial(exchange_gelu_kernel, axis, n, gather, s...]
    pallas_call x4 -> x3, Pallas kernels: 64 us -> 49.1 us  [exchange(): pl.pallas_call(functools.partial(exchange_kernel, axis, n, gather), out_s...]
where the time goes in v15:
time: 361 us; the launch traced here: 359 us
  Pallas kernels  153 us (42%)
  waiting for transfers between devices  103 us (29%)
  local copies, waits for them, and re-layouts  33.6 us (9%)
  other arithmetic  27.7 us (8%)
  matrix products  26.1 us (7%)
  between operations  14.9 us (4%)
    psum x1, waiting for transfers between devices, shards(): summed_all = lax.psum(partial_sums.astype(jnp.bfloat16), 'req')  71.3 us
    pallas_call x2, Pallas kernels, gather_grid(): pl.pallas_call(functools.partial(gather_grid_kernel, axis, side), out_sha...  67.2 us
    pallas_call x3, Pallas kernels, exchange(): pl.pallas_call(functools.partial(exchange_kernel, axis, n, gather), out_s...  49.1 us
    pallas_call x2, Pallas kernels, exchange_gelu(): pl.pallas_call(functools.partial(exchange_gelu_kernel, axis, n, gather, s...  37.1 us
    reduce_scatter x1, waiting for transfers between devices, shards(): lax.psum_scatter(next_partial.astype(jnp.bfloat16), 'req', scatter_dimens...  32 us
  transfers between devices with their start and end apart: 2, of which 2 were waited for; matrix products, arithmetic and copies ran while one was open for 1% of the time, Pallas kernels for 0%

profile of v15, /device:TPU:0, one launch (start us, length us, event | category | flops | bytes accessed | tf_op | source)
XLA Modules:
  0.0 359.4 jit_solution(17013543410842122733)
XLA Ops:
  7.2 30.9 %shard_map.131 = bf16[16,2,48,512]{3,2,1,0:T(8,128)(2,1)} custom-call(bf16[2,48,512]{2,1,0:T(8,128)(2,1)} %x_ref.1), custom_call_target="tpu_custom_call" | custom-call | bytes 3145728 | tf_op jit(solution)/shard_map/pallas_call | solution.py:197
  38.1 1.8 convert_reduce_fusion.1
  41.4 1.4 copy.208
  44.5 8.9 %shard_map.132 = f32[8,24,128]{2,1,0:T(8,128)} custom-call(f32[24,128]{1,0:T(8,128)} %reshape.467.x_ref), custom_call_target="tpu_custom_call" | custom-call | bytes 196608 | tf_op jit(solution)/shard_map/pallas_call | solution.py:218
  56.4 1.4 convolution_convert_fusion.2
  57.9 1.8 convolution_convert_fusion
  59.7 2.9 pad_maximum_fusion
  68.7 71.3 %all-reduce.6.cloned.1.call-done.hidden_ref = bf16[1536,1792]{1,0:T(8,128)(2,1)} async-done(((bf16[1536,1792]{1,0:T(8,128)(2,1)}), bf16[1536,1792]{1,0:T(8,128)(2,1)}) %all-reduce.6.cloned.1.call-update) | async-done | bytes 5505040 | tf_op jit(solution)/shard_map/psum | solution.py:317
  140.1 3.0 fusion.97
  144.2 1.4 fusion.98
  153.4 2.2 fusion.33
  155.6 2.2 fusion.30
  163.3 19.8 %shard_map.133 = (bf16[8,2,96,384]{3,2,1,0:T(8,128)(2,1)}, bf16[768,1024]{1,0:T(8,128)(2,1)}) custom-call(bf16[8,2,96,384]{3,2,1,0:T(8,128)(2,1)} %copy_bitcast_fusion.x_ref, bf16[1536,1792]{1,0:T(8,128)(2,1)} %all-reduce.6.cloned.1.call-done.hidden_ref), custom_call_target="tpu_custom_call" | custom-call | flops 15728640 | bytes 22020096 | tf_op jit(solution)/shard_map/pallas_call | solution.py:128
  183.1 1.5 convert_element_type.157
  185.6 1.6 dynamic-slice_convert_fusion
  187.9 1.5 fusion.103
  190.9 1.4 stack_reshape.7
  192.3 1.5 pad_bitcast_fusion
  198.3 1.5 fusion.62
  203.3 1.4 copy.236
  204.8 1.4 copy.234
  206.7 1.5 fusion.60
  209.8 17.4 %shard_map.134 = (bf16[8,2,96,256]{3,2,1,0:T(8,128)(2,1)}, bf16[768,1024]{1,0:T(8,128)(2,1)}) custom-call(bf16[2,96,256]{2,1,0:T(8,128)(2,1)} %reshape.474.x_ref, bf16[1536,1792]{1,0:T(8,128)(2,1)} %all-reduce.6.cloned.1.call-done.hidden_ref), custom_call_target="tpu_custom_call" | custom-call | flops 15728640 | bytes 4718592 | tf_op jit(solution)/shard_map/pallas_call | solution.py:128
  228.5 3.5 fusion.1
  232.0 1.7 fusion.9
  233.7 33.5 %shard_map.135 = bf16[16,96,512]{2,1,0:T(8,128)(2,1)} custom-call(bf16[16,96,512]{2,1,0:T(8,128)(2,1)} %bitcast.220), custom_call_target="tpu_custom_call" | custom-call | bytes 50331648 | tf_op jit(solution)/shard_map/pallas_call | solution.py:218
  267.2 1.7 convert_reduce_fusion
  269.9 6.6 %shard_map.136 = f32[8,2,128]{2,1,0:T(2,128)} custom-call(f32[2,128]{1,0:T(2,128)} %pad_bitcast_fusion.2.x_ref), custom_call_target="tpu_custom_call" | custom-call | bytes 16384 | tf_op jit(solution)/shard_map/pallas_call | solution.py:218
  278.2 36.3 %shard_map.137 = bf16[16,2,48,512]{3,2,1,0:T(8,128)(2,1)} custom-call(bf16[2,48,512]{2,1,0:T(8,128)(2,1)} %fusion.56.x_ref), custom_call_target="tpu_custom_call" | custom-call | bytes 3145728 | tf_op jit(solution)/shard_map/pallas_call | solution.py:197
  314.5 4.3 %convolution_convert_fusion.1 = bf16[1536,768]{1,0:T(8,128)(2,1)} fusion(bf16[1536,512]{1,0:T(8,128)(2,1)} %bitcast.224, bf16[512,768]{1,0:T(8,128)(2,1)S(1)} %copy-done.19), kind=kOutput, calls=%fused_computation.6 | convolution fusion | flops 1209139200 | bytes 4718592 | tf_op jit(solution)/shard_map/dot_general | solution.py:502
  318.8 32.0 %reduce-scatter.2.cloned.1.call-done = bf16[192,768]{1,0:T(8,128)(2,1)} async-done(((bf16[1536,768]{1,0:T(8,128)(2,1)}), bf16[192,768]{1,0:T(8,128)(2,1)}) %reduce-scatter.2.cloned.1.call-update) | async-done | bytes 294928 | tf_op jit(solution)/shard_map/reduce_scatter | solution.py:503
  350.9 1.7 copy.249
  (177 shorter events, 43.2 us)
Async XLA Ops:
  7.2 50.7 %copy-start = (bf16[512,1024]{1,0:T(8,128)(2,1)S(1)}, bf16[512,1024]{1,0:T(8,128)(2,1)}, u32[]{:S(2)}) copy-start(bf16[512,1024]{1,0:T(8,128)(2,1)} %param.15) | copy-start | bytes 3145732
  7.2 33.7 %copy-start.14 = (f32[3,512]{1,0:T(4,128)S(1)}, f32[3,512]{1,0:T(4,128)}, u32[]{:S(2)}) copy-start(f32[3,512]{1,0:T(4,128)} %param.13) | copy-start | bytes 18436
  7.2 132.9 %all-reduce.6.cloned.1.call-start = ((), (), s32[]{:S(2)}) async-start(), calls=%async_computation.1 | async-start | bytes 11010048 | tf_op jit(solution)/shard_map/psum | solution.py:317
  38.1 1.9 copy-start.3
  55.3 1.1 copy-start.6
  62.6 0.7 copy-start.17
  62.6 0.7 copy-start.2
  62.6 5.4 %copy-start.20 = (s32[1,96]{1,0:T(1,128)S(1)}, s32[1,96]{1,0:T(1,128)}, u32[]{:S(2)}) copy-start(s32[1,96]{1,0:T(1,128)} %param.23) | copy-start | bytes 1156
  62.6 288.3 %reduce-scatter.2.cloned.1.call-start = ((), (), s32[]{:S(2)}) async-start(), calls=%async_computation.2 | async-start | bytes 2654208 | tf_op jit(solution)/shard_map/reduce_scatter | solution.py:503
  146.8 2.2 copy-start.4
  185.0 5.0 %copy-start.15 = (s32[96]{0:T(128)S(1)}, s32[96]{0:T(128)}, u32[]{:S(2)}) copy-start(s32[96]{0:T(128)} %fusion.93) | copy-start | bytes 1156
  193.9 6.0 %copy-start.16 = (pred[2,2]{1,0:T(4,128)(4,1)S(1)}, pred[2,2]{1,0:T(4,128)(4,1)}, u32[]{:S(2)}) copy-start(pred[2,2]{1,0:T(4,128)(4,1)} %iota_compare_fusion.10) | copy-start | bytes 16
  202.0 4.3 %copy-start.11 = (bf16[1,96,2,128]{3,2,1,0:T(2,128)(2,1)S(1)}, bf16[1,96,2,128]{3,2,1,0:T(2,128)(2,1)}, u32[]{:S(2)}) copy-start(bf16[1,96,2,128]{3,2,1,0:T(2,128)(2,1)} %slice.218) | copy-start | bytes 147460
  202.0 4.3 %copy-start.12 = (bf16[1,96,2,128]{3,2,1,0:T(2,128)(2,1)S(1)}, bf16[1,96,2,128]{3,2,1,0:T(2,128)(2,1)}, u32[]{:S(2)}) copy-start(bf16[1,96,2,128]{3,2,1,0:T(2,128)(2,1)} %stack_reshape.7) | copy-start | bytes 147460
  202.0 4.4 %copy-start.8 = (bf16[1,2,96,2,128]{4,3,2,1,0:T(2,128)(2,1)S(1)}, bf16[1,2,96,2,128]{4,3,2,1,0:T(2,128)(2,1)}, u32[]{:S(2)}) copy-start(bf16[1,2,96,2,128]{4,3,2,1,0:T(2,128)(2,1)} %pad_bitcast_fusion) | copy-start | bytes 294916
  204.7 3.9 %copy-start.9 = (f32[2,96,2]{2,1,0:T(8,128)S(1)}, f32[2,96,2]{2,1,0:T(8,128)}, u32[]{:S(2)}) copy-start(f32[2,96,2]{2,1,0:T(8,128)} %copy.245) | copy-start | bytes 4612
  209.8 18.6 %copy-start.18 = (bf16[768,1024]{1,0:T(8,128)(2,1)S(1)}, bf16[768,1024]{1,0:T(8,128)(2,1)}, u32[]{:S(2)}) copy-start(bf16[768,1024]{1,0:T(8,128)(2,1)} %get-tuple-element.8) | copy-start | bytes 4718596
  228.4 3.6 copy-start.10
  233.7 35.2 %copy-start.7 = (bf16[2,48,512]{2,1,0:T(8,128)(2,1)S(1)}, bf16[2,48,512]{2,1,0:T(8,128)(2,1)}, u32[]{:S(2)}) copy-start(bf16[2,48,512]{2,1,0:T(8,128)(2,1)} %x_ref.1) | copy-start | bytes 294916
  233.7 43.7 %copy-start.13 = (f32[1,512]{1,0:T(1,128)S(1)}, f32[1,512]{1,0:T(1,128)}, u32[]{:S(2)}) copy-start(f32[1,512]{1,0:T(1,128)} %get-tuple-element.60) | copy-start | bytes 6148
  267.2 47.3 %copy-start.19 = (bf16[512,768]{1,0:T(8,128)(2,1)S(1)}, bf16[512,768]{1,0:T(8,128)(2,1)}, u32[]{:S(2)}) copy-start(bf16[512,768]{1,0:T(8,128)(2,1)} %param.18) | copy-start | bytes 2359300
  269.1 49.8 %copy-start.5 = (bf16[2,48,512]{2,1,0:T(8,128)(2,1)}, bf16[2,48,512]{2,1,0:T(8,128)(2,1)S(1)}, u32[]{:S(2)}) copy-start(bf16[2,48,512]{2,1,0:T(8,128)(2,1)S(1)} %get-tuple-element.17) | copy-start | bytes 294916
  314.5 38.1 %copy-start.1 = (bf16[512,1024]{1,0:T(8,128)(2,1)S(1)}, bf16[512,1024]{1,0:T(8,128)(2,1)}, u32[]{:S(2)}) copy-start(bf16[512,1024]{1,0:T(8,128)(2,1)} %param.15) | copy-start | bytes 3145732
Sparse Core Ops, SparseCore 0:
  62.7 77.2 all-reduce.5
  319.0 31.8 reduce-scatter.1

commit v16 on v14

--- a/solution.py
+++ b/solution.py
@@ -298,7 +298,7 @@
     gather_rows = valid_owner[:, None] * BEAM + jnp.arange(BEAM, dtype=jnp.int32)[None, :]
 
     block = inputs.astype(jnp.float32)
-    rows_all = gather_grid(inputs, "mlp", mlp_size, 0).reshape(steps * beam_total, -1)
+    rows_all = exchange(inputs, "mlp", mlp_size, True, 0).reshape(steps * beam_total, -1)
     normed = row_normalize(rows_all.astype(jnp.float32), 3)
     attn_in = (normed * norm_gains[0]).astype(jnp.bfloat16)
     mlp_in = (normed * norm_gains[1]).astype(jnp.bfloat16)
@@ -488,7 +488,7 @@
     )
     layer = (block + update.reshape(steps, local_rows, local_width)).astype(jnp.bfloat16)
     next_in = (row_normalize(layer.astype(jnp.float32), 4) * norm_gains[2]).astype(jnp.bfloat16)
-    gathered = gather_grid(next_in, "mlp", mlp_size, 2).reshape(steps * beam_total, -1)
+    gathered = exchange(next_in, "mlp", mlp_size, True, 2).reshape(steps * beam_total, -1)
     next_partial = jnp.dot(gathered, next_weight, preferred_element_type=jnp.float32)
     next_out = lax.psum_scatter(
         next_partial.astype(jnp.bfloat16), "req", scatter_dimension=0, tiled=True

time: 359 us -> 364 us (1.014)
  waiting for transfers between devices: 103 us -> 111 us
    pallas_call x2 -> x0, Pallas kernels: 67.1 us -> none  [gather_grid(): pl.pallas_call(functools.partial(gather_grid_kernel, axis, side), out_sha...]
    pallas_call x4 -> x6, Pallas kernels: 64 us -> 128 us  [exchange(): pl.pallas_call(functools.partial(exchange_kernel, axis, n, gather), out_s...]
    psum x1, waiting for transfers between devices: 71.4 us -> 75.8 us  [shards(): summed_all = lax.psum(partial_sums.astype(jnp.bfloat16), 'req')]
    reduce_scatter x1, waiting for transfers between devices: 31.9 us -> 35.6 us  [shards(): lax.psum_scatter(next_partial.astype(jnp.bfloat16), 'req', scatter_dimens...]
where the time goes in v16:
time: 364 us; the launch traced here: 362 us
  Pallas kernels  148 us (41%)
  waiting for transfers between devices  111 us (30%)
  local copies, waits for them, and re-layouts  33.6 us (9%)
  other arithmetic  27.8 us (8%)
  matrix products  26.3 us (7%)
  between operations  14.9 us (4%)
    pallas_call x6, Pallas kernels, exchange(): pl.pallas_call(functools.partial(exchange_kernel, axis, n, gather), out_s...  128 us
    psum x1, waiting for transfers between devices, shards(): summed_all = lax.psum(partial_sums.astype(jnp.bfloat16), 'req')  75.8 us
    reduce_scatter x1, waiting for transfers between devices, shards(): lax.psum_scatter(next_partial.astype(jnp.bfloat16), 'req', scatter_dimens...  35.6 us
    pallas_call x1, Pallas kernels, exchange_gelu(): pl.pallas_call(functools.partial(exchange_gelu_kernel, axis, n, start), o...  20.3 us
  transfers between devices with their start and end apart: 2, of which 2 were waited for; matrix products, arithmetic and copies ran while one was open for 1% of the time, Pallas kernels for 0%

profile of v16, /device:TPU:0, one launch (start us, length us, event | category | flops | bytes accessed | tf_op | source)
XLA Modules:
  0.0 362.5 jit_solution(17805124952501983723)
XLA Ops:
  7.2 29.2 %shard_map.131 = bf16[16,2,48,512]{3,2,1,0:T(8,128)(2,1)} custom-call(bf16[2,48,512]{2,1,0:T(8,128)(2,1)} %x_ref.1), custom_call_target="tpu_custom_call" | custom-call | bytes 3145728 | tf_op jit(solution)/shard_map/pallas_call | solution.py:214
  36.5 1.8 convert_reduce_fusion.1
  39.7 1.4 copy.208
  42.8 8.9 %shard_map.132 = f32[8,24,128]{2,1,0:T(8,128)} custom-call(f32[24,128]{1,0:T(8,128)} %reshape.467.x_ref), custom_call_target="tpu_custom_call" | custom-call | bytes 196608 | tf_op jit(solution)/shard_map/pallas_call | solution.py:214
  54.8 1.4 convolution_convert_fusion.2
  56.2 1.8 convolution_convert_fusion
  58.0 2.9 pad_maximum_fusion
  67.0 75.8 %all-reduce.6.cloned.1.call-done.hidden_ref = bf16[1536,1792]{1,0:T(8,128)(2,1)} async-done(((bf16[1536,1792]{1,0:T(8,128)(2,1)}), bf16[1536,1792]{1,0:T(8,128)(2,1)}) %all-reduce.6.cloned.1.call-update) | async-done | bytes 5505040 | tf_op jit(solution)/shard_map/psum | solution.py:313
  142.8 3.0 fusion.92
  146.9 1.4 fusion.93
  156.1 2.2 fusion.29
  158.3 2.2 fusion.26
  166.1 20.3 %shard_map.133 = (bf16[8,2,96,384]{3,2,1,0:T(8,128)(2,1)}, bf16[1536,1024]{1,0:T(8,128)(2,1)}) custom-call(bf16[8,2,96,384]{3,2,1,0:T(8,128)(2,1)} %copy_bitcast_fusion.x_ref, bf16[1536,1792]{1,0:T(8,128)(2,1)} %all-reduce.6.cloned.1.call-done.hidden_ref), custom_call_target="tpu_custom_call" | custom-call | flops 31457280 | bytes 25165824 | tf_op jit(solution)/shard_map/pallas_call | solution.py:124
  186.4 1.5 convert_element_type.157
  188.9 1.6 dynamic-slice_convert_fusion
  191.2 1.5 fusion.98
  194.2 1.4 stack_reshape.7
  195.6 1.5 pad_bitcast_fusion
  201.6 1.5 fusion.58
  205.3 1.4 fusion.94
  208.1 1.4 copy.234
  210.0 1.5 fusion.56
  213.2 15.0 %shard_map.134 = bf16[8,2,96,256]{3,2,1,0:T(8,128)(2,1)} custom-call(bf16[2,96,256]{2,1,0:T(8,128)(2,1)} %reshape.474.x_ref), custom_call_target="tpu_custom_call" | custom-call | bytes 1572864 | tf_op jit(solution)/shard_map/pallas_call | solution.py:214
  229.4 3.7 %fusion.100 = f32[1536,512]{1,0:T(8,128)S(1)} fusion(bf16[1536,1024]{1,0:T(8,128)(2,1)} %get-tuple-element.5, bf16[1024,512]{1,0:T(8,128)(2,1)S(1)} %copy-done.18), kind=kOutput, calls=%fused_computation.209 | convolution fusion | flops 1610612736 | bytes 7340032 | tf_op jit(solution)/shard_map/dot_general | solution.py:477
  233.2 1.7 fusion.5
  234.9 33.4 %shard_map.135 = bf16[16,96,512]{2,1,0:T(8,128)(2,1)} custom-call(bf16[16,96,512]{2,1,0:T(8,128)(2,1)} %bitcast.221), custom_call_target="tpu_custom_call" | custom-call | bytes 50331648 | tf_op jit(solution)/shard_map/pallas_call | solution.py:214
  268.3 1.7 convert_reduce_fusion
  271.0 6.7 %shard_map.136 = f32[8,2,128]{2,1,0:T(2,128)} custom-call(f32[2,128]{1,0:T(2,128)} %pad_bitcast_fusion.2.x_ref), custom_call_target="tpu_custom_call" | custom-call | bytes 16384 | tf_op jit(solution)/shard_map/pallas_call | solution.py:214
  279.3 34.7 %shard_map.137 = bf16[16,2,48,512]{3,2,1,0:T(8,128)(2,1)} custom-call(bf16[2,48,512]{2,1,0:T(8,128)(2,1)} %fusion.52.x_ref), custom_call_target="tpu_custom_call" | custom-call | bytes 3145728 | tf_op jit(solution)/shard_map/pallas_call | solution.py:214
  314.0 4.3 %convolution_convert_fusion.1 = bf16[1536,768]{1,0:T(8,128)(2,1)} fusion(bf16[1536,512]{1,0:T(8,128)(2,1)} %bitcast.226, bf16[512,768]{1,0:T(8,128)(2,1)S(1)} %copy-done.19), kind=kOutput, calls=%fused_computation.6 | convolution fusion | flops 1209139200 | bytes 4718592 | tf_op jit(solution)/shard_map/dot_general | solution.py:492
  318.3 35.6 %reduce-scatter.2.cloned.1.call-done = bf16[192,768]{1,0:T(8,128)(2,1)} async-done(((bf16[1536,768]{1,0:T(8,128)(2,1)}), bf16[192,768]{1,0:T(8,128)(2,1)}) %reduce-scatter.2.cloned.1.call-update) | async-done | bytes 294928 | tf_op jit(solution)/shard_map/reduce_scatter | solution.py:493
  353.9 1.7 copy.249
  (177 shorter events, 43.2 us)
Async XLA Ops:
  7.2 49.0 %copy-start = (bf16[512,1024]{1,0:T(8,128)(2,1)S(1)}, bf16[512,1024]{1,0:T(8,128)(2,1)}, u32[]{:S(2)}) copy-start(bf16[512,1024]{1,0:T(8,128)(2,1)} %param.15) | copy-start | bytes 3145732
  7.2 32.0 %copy-start.14 = (f32[3,512]{1,0:T(4,128)S(1)}, f32[3,512]{1,0:T(4,128)}, u32[]{:S(2)}) copy-start(f32[3,512]{1,0:T(4,128)} %param.13) | copy-start | bytes 18436
  7.2 135.6 %all-reduce.6.cloned.1.call-start = ((), (), s32[]{:S(2)}) async-start(), calls=%async_computation.1 | async-start | bytes 11010048 | tf_op jit(solution)/shard_map/psum | solution.py:313
  36.5 1.9 copy-start.3
  53.6 1.1 copy-start.6
  60.9 0.7 copy-start.17
  60.9 0.7 copy-start.2
  60.9 5.4 %copy-start.20 = (s32[1,96]{1,0:T(1,128)S(1)}, s32[1,96]{1,0:T(1,128)}, u32[]{:S(2)}) copy-start(s32[1,96]{1,0:T(1,128)} %param.23) | copy-start | bytes 1156
  60.9 293.0 %reduce-scatter.2.cloned.1.call-start = ((), (), s32[]{:S(2)}) async-start(), calls=%async_computation.2 | async-start | bytes 2654208 | tf_op jit(solution)/shard_map/reduce_scatter | solution.py:493
  149.5 2.2 copy-start.4
  188.3 5.0 %copy-start.15 = (s32[96]{0:T(128)S(1)}, s32[96]{0:T(128)}, u32[]{:S(2)}) copy-start(s32[96]{0:T(128)} %fusion.89) | copy-start | bytes 1156
  197.2 6.0 %copy-start.16 = (pred[2,2]{1,0:T(4,128)(4,1)S(1)}, pred[2,2]{1,0:T(4,128)(4,1)}, u32[]{:S(2)}) copy-start(pred[2,2]{1,0:T(4,128)(4,1)} %iota_compare_fusion.10) | copy-start | bytes 16
  205.3 4.3 %copy-start.11 = (bf16[1,96,2,128]{3,2,1,0:T(2,128)(2,1)S(1)}, bf16[1,96,2,128]{3,2,1,0:T(2,128)(2,1)}, u32[]{:S(2)}) copy-start(bf16[1,96,2,128]{3,2,1,0:T(2,128)(2,1)} %slice.218) | copy-start | bytes 147460
  205.3 4.3 %copy-start.12 = (bf16[1,96,2,128]{3,2,1,0:T(2,128)(2,1)S(1)}, bf16[1,96,2,128]{3,2,1,0:T(2,128)(2,1)}, u32[]{:S(2)}) copy-start(bf16[1,96,2,128]{3,2,1,0:T(2,128)(2,1)} %stack_reshape.7) | copy-start | bytes 147460
  205.3 4.5 %copy-start.8 = (bf16[1,2,96,2,128]{4,3,2,1,0:T(2,128)(2,1)S(1)}, bf16[1,2,96,2,128]{4,3,2,1,0:T(2,128)(2,1)}, u32[]{:S(2)}) copy-start(bf16[1,2,96,2,128]{4,3,2,1,0:T(2,128)(2,1)} %pad_bitcast_fusion) | copy-start | bytes 294916
  208.1 3.9 %copy-start.9 = (f32[2,96,2]{2,1,0:T(8,128)S(1)}, f32[2,96,2]{2,1,0:T(8,128)}, u32[]{:S(2)}) copy-start(f32[2,96,2]{2,1,0:T(8,128)} %copy.245) | copy-start | bytes 4612
  212.0 17.4 %copy-start.18 = (bf16[1024,512]{1,0:T(8,128)(2,1)S(1)}, bf16[1024,512]{1,0:T(8,128)(2,1)}, u32[]{:S(2)}) copy-start(bf16[1024,512]{1,0:T(8,128)(2,1)} %param.17) | copy-start | bytes 3145732
  229.4 3.8 %copy-start.10 = (bf16[256,512]{1,0:T(8,128)(2,1)S(1)}, bf16[256,512]{1,0:T(8,128)(2,1)}, u32[]{:S(2)}) copy-start(bf16[256,512]{1,0:T(8,128)(2,1)} %param.16) | copy-start | bytes 786436
  234.9 35.1 %copy-start.7 = (bf16[2,48,512]{2,1,0:T(8,128)(2,1)S(1)}, bf16[2,48,512]{2,1,0:T(8,128)(2,1)}, u32[]{:S(2)}) copy-start(bf16[2,48,512]{2,1,0:T(8,128)(2,1)} %x_ref.1) | copy-start | bytes 294916
  234.9 43.6 %copy-start.13 = (f32[1,512]{1,0:T(1,128)S(1)}, f32[1,512]{1,0:T(1,128)}, u32[]{:S(2)}) copy-start(f32[1,512]{1,0:T(1,128)} %get-tuple-element.56) | copy-start | bytes 6148
  268.3 45.7 %copy-start.19 = (bf16[512,768]{1,0:T(8,128)(2,1)S(1)}, bf16[512,768]{1,0:T(8,128)(2,1)}, u32[]{:S(2)}) copy-start(bf16[512,768]{1,0:T(8,128)(2,1)} %param.18) | copy-start | bytes 2359300
  270.1 48.2 %copy-start.5 = (bf16[2,48,512]{2,1,0:T(8,128)(2,1)}, bf16[2,48,512]{2,1,0:T(8,128)(2,1)S(1)}, u32[]{:S(2)}) copy-start(bf16[2,48,512]{2,1,0:T(8,128)(2,1)S(1)} %get-tuple-element.13) | copy-start | bytes 294916
  314.0 41.6 %copy-start.1 = (bf16[512,1024]{1,0:T(8,128)(2,1)S(1)}, bf16[512,1024]{1,0:T(8,128)(2,1)}, u32[]{:S(2)}) copy-start(bf16[512,1024]{1,0:T(8,128)(2,1)} %param.15) | copy-start | bytes 3145732
Sparse Core Ops, SparseCore 0:
  61.0 81.7 all-reduce.5
  318.5 35.4 reduce-scatter.1

commit v17 on v14

--- a/solution.py
+++ b/solution.py
@@ -490,9 +490,14 @@
     next_in = (row_normalize(layer.astype(jnp.float32), 4) * norm_gains[2]).astype(jnp.bfloat16)
     gathered = gather_grid(next_in, "mlp", mlp_size, 2).reshape(steps * beam_total, -1)
     next_partial = jnp.dot(gathered, next_weight, preferred_element_type=jnp.float32)
-    next_out = lax.psum_scatter(
-        next_partial.astype(jnp.bfloat16), "req", scatter_dimension=0, tiled=True
-    )
+    next_parts = exchange(
+        next_partial.astype(jnp.bfloat16).reshape(req_size, -1, next_partial.shape[1]),
+        "req",
+        req_size,
+        False,
+        7,
+    )
+    next_out = jnp.sum(next_parts.astype(jnp.float32), axis=0).astype(jnp.bfloat16)
     next_out = (
         next_out.reshape(per_own, steps, local_rows, -1)
         .transpose(1, 0, 2, 3)

time: 359 us -> 362 us (level)
  waiting for transfers between devices: 103 us -> 71.4 us
  Pallas kernels: 151 us -> 182 us
    reduce_scatter x1 -> x0, waiting for transfers between devices: 31.9 us -> none  [shards(): lax.psum_scatter(next_partial.astype(jnp.bfloat16), 'req', scatter_dimens...]
    pallas_call x4 -> x5, Pallas kernels: 64 us -> 94.8 us  [exchange(): pl.pallas_call(functools.partial(exchange_kernel, axis, n, gather), out_s...]
  transfers between devices with their start and end apart: 2 -> 1, of which waited for: 2 -> 1; matrix products, arithmetic and copies ran while one was open for 1% -> 1% of each run, Pallas kernels for 0% -> 0%
where the time goes in v17:
time: 362 us; the launch traced here: 358 us
  Pallas kernels  182 us (50%)
  waiting for transfers between devices  71.4 us (20%)
  local copies, waits for them, and re-layouts  32.9 us (9%)
  other arithmetic  29.9 us (8%)
  matrix products  26.2 us (7%)
  between operations  14.9 us (4%)
    pallas_call x5, Pallas kernels, exchange(): pl.pallas_call(functools.partial(exchange_kernel, axis, n, gather), out_s...  94.8 us
    psum x1, waiting for transfers between devices, shards(): summed_all = lax.psum(partial_sums.astype(jnp.bfloat16), 'req')  71.4 us
    pallas_call x2, Pallas kernels, gather_grid(): pl.pallas_call(functools.partial(gather_grid_kernel, axis, side), out_sha...  67.4 us
    pallas_call x1, Pallas kernels, exchange_gelu(): pl.pallas_call(functools.partial(exchange_gelu_kernel, axis, n, start), o...  20.3 us
  transfers between devices with their start and end apart: 1, of which 1 were waited for; matrix products, arithmetic and copies ran while one was open for 1% of the time, Pallas kernels for 0%

profile of v17, /device:TPU:0, one launch (start us, length us, event | category | flops | bytes accessed | tf_op | source)
XLA Modules:
  0.0 357.7 jit_solution(2668779463934360659)
XLA Ops:
  7.2 30.9 %shard_map.131 = bf16[16,2,48,512]{3,2,1,0:T(8,128)(2,1)} custom-call(bf16[2,48,512]{2,1,0:T(8,128)(2,1)} %x_ref.1), custom_call_target="tpu_custom_call" | custom-call | bytes 3145728 | tf_op jit(solution)/shard_map/pallas_call | solution.py:193
  38.1 1.8 convert_reduce_fusion.1
  41.4 1.4 copy.206
  44.5 8.9 %shard_map.132 = f32[8,24,128]{2,1,0:T(8,128)} custom-call(f32[24,128]{1,0:T(8,128)} %reshape.470.x_ref), custom_call_target="tpu_custom_call" | custom-call | bytes 196608 | tf_op jit(solution)/shard_map/pallas_call | solution.py:214
  56.4 1.4 convolution_convert_fusion.2
  57.8 1.8 convolution_convert_fusion
  59.7 2.9 pad_maximum_fusion
  68.7 71.4 %all-reduce.6.cloned.1.call-done.hidden_ref = bf16[1536,1792]{1,0:T(8,128)(2,1)} async-done(((bf16[1536,1792]{1,0:T(8,128)(2,1)}), bf16[1536,1792]{1,0:T(8,128)(2,1)}) %all-reduce.6.cloned.1.call-update) | async-done | bytes 5505040 | tf_op jit(solution)/shard_map/psum | solution.py:313
  140.1 3.0 fusion.92
  144.2 1.4 fusion.93
  153.3 2.2 fusion.29
  155.6 2.2 fusion.26
  163.3 20.3 %shard_map.133 = (bf16[8,2,96,384]{3,2,1,0:T(8,128)(2,1)}, bf16[1536,1024]{1,0:T(8,128)(2,1)}) custom-call(bf16[8,2,96,384]{3,2,1,0:T(8,128)(2,1)} %copy_bitcast_fusion.x_ref, bf16[1536,1792]{1,0:T(8,128)(2,1)} %all-reduce.6.cloned.1.call-done.hidden_ref), custom_call_target="tpu_custom_call" | custom-call | flops 31457280 | bytes 25165824 | tf_op jit(solution)/shard_map/pallas_call | solution.py:124
  183.6 1.5 convert_element_type.159
  186.2 1.6 dynamic-slice_convert_fusion
  188.4 1.5 fusion.98
  191.4 1.4 stack_reshape.7
  192.8 1.5 pad_bitcast_fusion
  198.8 1.5 fusion.58
  202.5 1.4 fusion.94
  205.3 1.4 copy.232
  207.2 1.5 fusion.56
  210.4 15.2 %shard_map.134 = bf16[8,2,96,256]{3,2,1,0:T(8,128)(2,1)} custom-call(bf16[2,96,256]{2,1,0:T(8,128)(2,1)} %reshape.477.x_ref), custom_call_target="tpu_custom_call" | custom-call | bytes 1572864 | tf_op jit(solution)/shard_map/pallas_call | solution.py:214
  226.9 3.7 %fusion.100 = f32[1536,512]{1,0:T(8,128)S(1)} fusion(bf16[1536,1024]{1,0:T(8,128)(2,1)} %get-tuple-element.5, bf16[1024,512]{1,0:T(8,128)(2,1)S(1)} %copy-done.18), kind=kOutput, calls=%fused_computation.209 | convolution fusion | flops 1610612736 | bytes 7340032 | tf_op jit(solution)/shard_map/dot_general | solution.py:477
  230.6 1.7 fusion.5
  232.4 33.5 %shard_map.135 = bf16[16,96,512]{2,1,0:T(8,128)(2,1)} custom-call(bf16[16,96,512]{2,1,0:T(8,128)(2,1)} %bitcast.222), custom_call_target="tpu_custom_call" | custom-call | bytes 50331648 | tf_op jit(solution)/shard_map/pallas_call | solution.py:214
  265.9 1.7 convert_reduce_fusion
  268.6 6.6 %shard_map.136 = f32[8,2,128]{2,1,0:T(2,128)} custom-call(f32[2,128]{1,0:T(2,128)} %pad_bitcast_fusion.2.x_ref), custom_call_target="tpu_custom_call" | custom-call | bytes 16384 | tf_op jit(solution)/shard_map/pallas_call | solution.py:214
  276.8 36.5 %shard_map.137 = bf16[16,2,48,512]{3,2,1,0:T(8,128)(2,1)} custom-call(bf16[2,48,512]{2,1,0:T(8,128)(2,1)} %fusion.52.x_ref), custom_call_target="tpu_custom_call" | custom-call | bytes 3145728 | tf_op jit(solution)/shard_map/pallas_call | solution.py:193
  313.4 4.2 %convolution_convert_fusion.1 = bf16[1536,768]{1,0:T(8,128)(2,1)} fusion(bf16[1536,512]{1,0:T(8,128)(2,1)} %bitcast.228, bf16[512,768]{1,0:T(8,128)(2,1)S(1)} %copy-done.19), kind=kOutput, calls=%fused_computation.6 | convolution fusion | flops 1209139200 | bytes 4718592 | tf_op jit(solution)/shard_map/dot_general | solution.py:492
  317.6 30.5 %shard_map.138 = bf16[8,192,768]{2,1,0:T(8,128)(2,1)} custom-call(bf16[8,192,768]{2,1,0:T(8,128)(2,1)} %bitcast.227), custom_call_target="tpu_custom_call" | custom-call | bytes 37748736 | tf_op jit(solution)/shard_map/pallas_call | solution.py:214
  348.1 2.1 reduce_sum.172
  (176 shorter events, 44.0 us)
Async XLA Ops:
  7.2 50.7 %copy-start = (bf16[512,1024]{1,0:T(8,128)(2,1)S(1)}, bf16[512,1024]{1,0:T(8,128)(2,1)}, u32[]{:S(2)}) copy-start(bf16[512,1024]{1,0:T(8,128)(2,1)} %param.15) | copy-start | bytes 3145732
  7.2 33.7 %copy-start.14 = (f32[3,512]{1,0:T(4,128)S(1)}, f32[3,512]{1,0:T(4,128)}, u32[]{:S(2)}) copy-start(f32[3,512]{1,0:T(4,128)} %param.13) | copy-start | bytes 18436
  7.2 132.9 %all-reduce.6.cloned.1.call-start = ((), (), s32[]{:S(2)}) async-start(), calls=%async_computation | async-start | bytes 11010048 | tf_op jit(solution)/shard_map/psum | solution.py:313
  38.1 1.9 copy-start.3
  55.3 1.1 copy-start.6
  62.6 0.7 copy-start.17
  62.6 0.7 copy-start.2
  63.2 4.8 %copy-start.20 = (s32[1,96]{1,0:T(1,128)S(1)}, s32[1,96]{1,0:T(1,128)}, u32[]{:S(2)}) copy-start(s32[1,96]{1,0:T(1,128)} %param.23) | copy-start | bytes 1156
  146.8 2.2 copy-start.4
  185.6 5.0 %copy-start.15 = (s32[96]{0:T(128)S(1)}, s32[96]{0:T(128)}, u32[]{:S(2)}) copy-start(s32[96]{0:T(128)} %fusion.89) | copy-start | bytes 1156
  194.4 6.0 %copy-start.16 = (pred[2,2]{1,0:T(4,128)(4,1)S(1)}, pred[2,2]{1,0:T(4,128)(4,1)}, u32[]{:S(2)}) copy-start(pred[2,2]{1,0:T(4,128)(4,1)} %iota_compare_fusion.10) | copy-start | bytes 16
  202.5 4.3 %copy-start.11 = (bf16[1,96,2,128]{3,2,1,0:T(2,128)(2,1)S(1)}, bf16[1,96,2,128]{3,2,1,0:T(2,128)(2,1)}, u32[]{:S(2)}) copy-start(bf16[1,96,2,128]{3,2,1,0:T(2,128)(2,1)} %slice.218) | copy-start | bytes 147460
  202.5 4.3 %copy-start.12 = (bf16[1,96,2,128]{3,2,1,0:T(2,128)(2,1)S(1)}, bf16[1,96,2,128]{3,2,1,0:T(2,128)(2,1)}, u32[]{:S(2)}) copy-start(bf16[1,96,2,128]{3,2,1,0:T(2,128)(2,1)} %stack_reshape.7) | copy-start | bytes 147460
  202.5 4.5 %copy-start.8 = (bf16[1,2,96,2,128]{4,3,2,1,0:T(2,128)(2,1)S(1)}, bf16[1,2,96,2,128]{4,3,2,1,0:T(2,128)(2,1)}, u32[]{:S(2)}) copy-start(bf16[1,2,96,2,128]{4,3,2,1,0:T(2,128)(2,1)} %pad_bitcast_fusion) | copy-start | bytes 294916
  205.3 3.9 %copy-start.9 = (f32[2,96,2]{2,1,0:T(8,128)S(1)}, f32[2,96,2]{2,1,0:T(8,128)}, u32[]{:S(2)}) copy-start(f32[2,96,2]{2,1,0:T(8,128)} %copy.243) | copy-start | bytes 4612
  209.2 17.7 %copy-start.18 = (bf16[1024,512]{1,0:T(8,128)(2,1)S(1)}, bf16[1024,512]{1,0:T(8,128)(2,1)}, u32[]{:S(2)}) copy-start(bf16[1024,512]{1,0:T(8,128)(2,1)} %param.17) | copy-start | bytes 3145732
  226.9 3.8 %copy-start.10 = (bf16[256,512]{1,0:T(8,128)(2,1)S(1)}, bf16[256,512]{1,0:T(8,128)(2,1)}, u32[]{:S(2)}) copy-start(bf16[256,512]{1,0:T(8,128)(2,1)} %param.16) | copy-start | bytes 786436
  232.4 35.2 %copy-start.7 = (bf16[2,48,512]{2,1,0:T(8,128)(2,1)S(1)}, bf16[2,48,512]{2,1,0:T(8,128)(2,1)}, u32[]{:S(2)}) copy-start(bf16[2,48,512]{2,1,0:T(8,128)(2,1)} %x_ref.1) | copy-start | bytes 294916
  232.4 43.7 %copy-start.13 = (f32[1,512]{1,0:T(1,128)S(1)}, f32[1,512]{1,0:T(1,128)}, u32[]{:S(2)}) copy-start(f32[1,512]{1,0:T(1,128)} %get-tuple-element.56) | copy-start | bytes 6148
  265.8 47.5 %copy-start.19 = (bf16[512,768]{1,0:T(8,128)(2,1)S(1)}, bf16[512,768]{1,0:T(8,128)(2,1)}, u32[]{:S(2)}) copy-start(bf16[512,768]{1,0:T(8,128)(2,1)} %param.18) | copy-start | bytes 2359300
  267.7 49.9 %copy-start.5 = (bf16[2,48,512]{2,1,0:T(8,128)(2,1)}, bf16[2,48,512]{2,1,0:T(8,128)(2,1)S(1)}, u32[]{:S(2)}) copy-start(bf16[2,48,512]{2,1,0:T(8,128)(2,1)S(1)} %get-tuple-element.13) | copy-start | bytes 294916
  317.6 33.3 %copy-start.1 = (bf16[512,1024]{1,0:T(8,128)(2,1)S(1)}, bf16[512,1024]{1,0:T(8,128)(2,1)}, u32[]{:S(2)}) copy-start(bf16[512,1024]{1,0:T(8,128)(2,1)} %param.15) | copy-start | bytes 3145732
Sparse Core Ops, SparseCore 0:
  62.7 77.3 all-reduce.5
